TPU v7x, 512 devices: a whole 4x8x8 slice. The times are simulated.
512 devices in a mesh: blocks: 128 (over x, y, z_hi, core), phi: 4 (over z_lo).
Axes of the slice: x: 4, y: 8, z: 8 (z_hi: 2, z_lo: 4; z = z_hi * 4 + z_lo), core: 2. Of those that a mesh axis runs over, the one named last changes fastest.
Arguments:
- field: float32 [3, 2048, 64, 512], P(None, 'blocks', 'phi'), may hold values from -6 to 6
- velocity: float32 [3, 2048, 64, 512], P(None, 'blocks', 'phi'), may hold values from -6 to 6
- strip_shift: int32 [2048], P('blocks'), may hold values from 0 to 6, as said below
- strip_frac: float32 [2048], P('blocks'), may hold values from 0 to 1
- edge_shift: int32 [2], replicated, may hold values from 0 to 6, as said below
- edge_frac: float32 [2], replicated, may hold values from 0 to 1
Outputs:
- advected: float32 [3, 2048, 64, 512], P(None, 'blocks', 'phi')
Inputs may be any that keep to these rules, and one draw needn't show every extreme that they name: `strip_shift`: some strip has a shift of exactly 6 and some strip a shift of 0. `edge_shift`: exactly one of the two boundary offsets equals 6; the other is smaller.
All inputs are finite; a program needn't handle non-finite values.
Results may differ from a plain program's by a relative error of at most 0.00002.
Values sent between devices are 32-bit elements; how exact they have to be, the bound alone decides.
No kernel may reach another device: no remote copies, remote signals or barrier semaphores. Data moves between devices by JAX's collectives and lax.ppermute only.
A program may use at most 128 MiB of HBM per device.

v0:
```python
import jax
import jax.numpy as jnp
from jax import lax
from jax.sharding import PartitionSpec as P

KMAX = 6


COURANT = 0.4


def with_halo(shard, sides, width):
    for axis, dim in sides:
        peers, length = (lax.axis_size(axis), shard.shape[dim])
        up = [(i, (i + 1) % peers) for i in range(peers)]
        down = [(j, i) for i, j in up]
        last = lax.slice_in_dim(shard, length - width, length, axis=dim)
        first = lax.slice_in_dim(shard, 0, width, axis=dim)
        before = lax.ppermute(last, axis, up)
        after = lax.ppermute(first, axis, down)
        shard = jnp.concatenate([before, shard, after], axis=dim)
    return shard


def from_behind(shard, axis, by):
    peers = lax.axis_size(axis)
    return lax.ppermute(shard, axis, [(i, (i + by) % peers) for i in range(peers)])


def below(values):
    return jnp.roll(values, 1, axis=-1)


def above(values):
    return jnp.roll(values, -1, axis=-1)


def ct_update(padded):
    field_x, field_y, field_z = (padded[0], padded[1], padded[2])
    flow_x, flow_y, flow_z = (padded[3], padded[4], padded[5])
    zedge_fx = 0.5 * (field_x[1:, 1:] + field_x[1:, :-1])
    zedge_fy = 0.5 * (field_y[1:, 1:] + field_y[:-1, 1:])
    zedge_vx = 0.25 * (flow_x[1:, 1:] + flow_x[:-1, 1:] + flow_x[1:, :-1] + flow_x[:-1, :-1])
    zedge_vy = 0.25 * (flow_y[1:, 1:] + flow_y[:-1, 1:] + flow_y[1:, :-1] + flow_y[:-1, :-1])
    emf_z = zedge_vy * zedge_fx - zedge_vx * zedge_fy
    middle_fx = field_x[:, 1:-1]
    middle_fz = field_z[:, 1:-1]
    middle_vx = flow_x[:, 1:-1]
    middle_vz = flow_z[:, 1:-1]
    yedge_fx = 0.5 * (middle_fx[1:] + below(middle_fx[1:]))
    yedge_fz = 0.5 * (middle_fz[1:] + middle_fz[:-1])
    paired_vx = middle_vx[1:] + middle_vx[:-1]
    paired_vz = middle_vz[1:] + middle_vz[:-1]
    yedge_vx = 0.25 * (paired_vx + below(paired_vx))
    yedge_vz = 0.25 * (paired_vz + below(paired_vz))
    emf_y = yedge_vx * yedge_fz - yedge_vz * yedge_fx
    radial_fy = field_y[1:-1]
    radial_fz = field_z[1:-1]
    radial_vy = flow_y[1:-1]
    radial_vz = flow_z[1:-1]
    xedge_fy = 0.5 * (radial_fy[:, 1:] + below(radial_fy[:, 1:]))
    xedge_fz = 0.5 * (radial_fz[:, 1:] + radial_fz[:, :-1])
    couple_vy = radial_vy[:, 1:] + radial_vy[:, :-1]
    couple_vz = radial_vz[:, 1:] + radial_vz[:, :-1]
    xedge_vy = 0.25 * (couple_vy + below(couple_vy))
    xedge_vz = 0.25 * (couple_vz + below(couple_vz))
    emf_x = xedge_vz * xedge_fy - xedge_vy * xedge_fz
    radial_count = emf_x.shape[0]
    azimuth_count = emf_y.shape[1]
    new_x = field_x[1:-1, 1:-1] - COURANT * (
        emf_z[:radial_count, 1:]
        - emf_z[:radial_count, :azimuth_count]
        - (above(emf_y[:radial_count]) - emf_y[:radial_count])
    )
    new_y = field_y[1:-1, 1:-1] - COURANT * (
        above(emf_x[:, :azimuth_count])
        - emf_x[:, :azimuth_count]
        - (emf_z[1:, :azimuth_count] - emf_z[:radial_count, :azimuth_count])
    )
    new_z = field_z[1:-1, 1:-1] - COURANT * (
        emf_y[1:] - emf_y[:radial_count] - (emf_x[:, 1:] - emf_x[:, :azimuth_count])
    )
    return jnp.stack([new_x, new_y, new_z])


def blend_rows(extended, near_start, far_start, weight, length):
    leading = lax.dynamic_slice_in_dim(extended, near_start, length, axis=1)
    trailing = lax.dynamic_slice_in_dim(extended, far_start, length, axis=1)
    return (1.0 - weight) * leading + weight * trailing


def body(field, velocity, strip_shift, strip_frac, edge_shift, edge_frac):
    azimuth = field.shape[2]
    stacked = jnp.concatenate([field, velocity], axis=0)
    first_block = lax.axis_index("blocks") == 0
    last_block = lax.axis_index("blocks") == lax.axis_size("blocks") - 1
    inner_shift = edge_shift[0]
    outer_shift = edge_shift[1]
    padded = with_halo(stacked, (("blocks", 1), ("phi", 2)), 1)
    low_rows = padded[:, 0]
    high_rows = padded[:, -1]
    taken_low = from_behind(low_rows[:, azimuth - KMAX - 1 : azimuth + 1], "phi", 1)
    taken_high = from_behind(high_rows[:, 1 : KMAX + 3], "phi", -1)
    extended_low = jnp.concatenate([taken_low, low_rows[:, 1:]], axis=1)
    extended_high = jnp.concatenate([high_rows[:, : azimuth + 1], taken_high], axis=1)
    span = azimuth + 2
    remapped_low = blend_rows(
        extended_low, KMAX + 1 - inner_shift, KMAX - inner_shift, edge_frac[0], span
    )
    remapped_high = blend_rows(extended_high, outer_shift, outer_shift + 1, edge_frac[1], span)
    padded = padded.at[:, 0].set(jnp.where(first_block, remapped_low, low_rows))
    padded = padded.at[:, -1].set(jnp.where(last_block, remapped_high, high_rows))
    updated = ct_update(padded)
    received = from_behind(updated[:, :, azimuth - KMAX - 1 :], "phi", 1)
    extended = jnp.concatenate([received, updated], axis=2)

    def one_strip(rows, shift, weight):
        return blend_rows(rows, KMAX + 1 - shift, KMAX - shift, weight, azimuth)

    return jax.vmap(one_strip, in_axes=(1, 0, 0), out_axes=1)(extended, strip_shift, strip_frac)


def solution(mesh):
    placed = (
        P(None, "blocks", "phi", None),
        P(None, "blocks", "phi", None),
        P("blocks"),
        P("blocks"),
        P(),
        P(),
    )
    return jax.shard_map(
        body, mesh=mesh, in_specs=placed, out_specs=P(None, "blocks", "phi", None), check_vma=False
    )
```

profile of v0, /device:TPU:1, one launch (start us, length us, event | category | flops | bytes accessed | tf_op | source)
XLA Modules:
  0.0 130.4 jit_solution(6518724160644557688)
XLA Ops:
  0.0 2.3 %pad_maximum_fusion.1 = f32[6,16,16,512]{3,2,1,0:T(8,128)S(1)} fusion(f32[3,16,16,512]{3,2,1,0:T(8,128)} %param.11, f32[3,16,16,512]{3,2,1,0:T(8,128)} %param.10), kind=kLoop, calls=%fused_computation.3 | loop fusion | flops 786432 | bytes 6291456 | tf_op jit(solution)/shard_map/concatenate | solution.py:94
  2.4 12.0 %collective-permute-start = (f32[6,1,16,512]{3,2,0,1:T(8,128)S(1)}, f32[6,1,16,512]{3,2,0,1:T(8,128)S(1)}, u32[]{:S(2)}, u32[]{:S(2)}) collective-permute-start(f32[6,1,16,512]{3,2,0,1:T(8,128)S(1)} %copy.23), channel_id=1, source_target_pairs={{0,4},{4,8},{8,12},{12,16},{16,20},{20,24},{24,28},{28,32},{32,36}... | collective-permute-start | bytes 589832 | tf_op jit(solution)/shard_map/ppermute | solution.py:19
  14.5 1.9 %collective-permute-start.1 = (f32[6,1,16,512]{3,2,0,1:T(8,128)S(1)}, f32[6,1,16,512]{3,2,0,1:T(8,128)S(1)}, u32[]{:S(2)}, u32[]{:S(2)}) collective-permute-start(f32[6,1,16,512]{3,2,0,1:T(8,128)S(1)} %copy.24), channel_id=1, source_target_pairs={{4,0},{8,4},{12,8},{16,12},{20,16},{24,20},{28,24},{32,28},{36,32}... | collective-permute-start | bytes 589832 | tf_op jit(solution)/shard_map/ppermute | solution.py:20
  16.4 0.6 collective-permute-done
  17.5 10.2 %collective-permute-done.1 = f32[6,1,16,512]{3,2,0,1:T(8,128)S(1)} collective-permute-done((f32[6,1,16,512]{3,2,0,1:T(8,128)S(1)}, f32[6,1,16,512]{3,2,0,1:T(8,128)S(1)}, u32[]{:S(2)}, u32[]{:S(2)}) %collective-permute-start.1) | collective-permute-done | bytes 196640 | tf_op jit(solution)/shard_map/ppermute | solution.py:20
  27.7 1.2 fusion.50
  28.9 2.0 %collective-permute-start.2 = (f32[6,18,1,512]{3,2,0,1:T(1,128)}, f32[6,18,1,512]{3,2,0,1:T(1,128)}, u32[]{:S(2)}, u32[]{:S(2)}) collective-permute-start(f32[6,18,1,512]{3,2,0,1:T(1,128)} %get-tuple-element.41), channel_id=1, source_target_pairs={{0,1},{1,2},{2,3},{3,0},{4,5},{5,6},{6,7},{7,4},{8,9},{9,10},{10,1... | collective-permute-start | bytes 663560 | tf_op jit(solution)/shard_map/ppermute | solution.py:19
  30.8 5.1 %collective-permute-start.3 = (f32[6,18,1,512]{3,2,0,1:T(1,128)}, f32[6,18,1,512]{3,2,0,1:T(1,128)}, u32[]{:S(2)}, u32[]{:S(2)}) collective-permute-start(f32[6,18,1,512]{3,2,0,1:T(1,128)} %get-tuple-element.42), channel_id=1, source_target_pairs={{1,0},{2,1},{3,2},{0,3},{5,4},{6,5},{7,6},{4,7},{9,8},{10,9},{11,1... | collective-permute-start | bytes 663560 | tf_op jit(solution)/shard_map/ppermute | solution.py:20
  39.1 0.9 collective-permute-done.2
  40.1 3.9 %collective-permute-done.3 = f32[6,18,1,512]{3,2,0,1:T(1,128)} collective-permute-done((f32[6,18,1,512]{3,2,0,1:T(1,128)}, f32[6,18,1,512]{3,2,0,1:T(1,128)}, u32[]{:S(2)}, u32[]{:S(2)}) %collective-permute-start.3) | collective-permute-done | bytes 221216 | tf_op jit(solution)/shard_map/ppermute | solution.py:20
  43.9 2.1 %pad_maximum_fusion = f32[6,18,18,512]{3,2,0,1:T(8,128)S(1)} fusion(f32[6,18,1,512]{3,2,0,1:T(1,128)} %collective-permute-done.3, f32[6,18,16,512]{3,2,0,1:T(8,128)S(1)} %constant_dynamic-update-slice_fusion, f32[6,18,1,512]{3,2,0,1:T(1,128)} %collective-permute-done.2), kind=kLoop, calls=%fused_computation.2 | loop fusion | flops 1990656 | bytes 7962624 | tf_op jit(solution)/shard_map/concatenate | solution.py:21
  46.0 2.3 %copy-done = f32[6,18,18,512]{3,2,0,1:T(8,128)} copy-done((f32[6,18,18,512]{3,2,0,1:T(8,128)}, f32[6,18,18,512]{3,2,0,1:T(8,128)S(1)}, u32[]{:S(2)}) %copy-start) | copy-done | bytes 3981336
  48.4 2.2 %collective-permute-start.4 = (f32[6,8,512]{2,1,0:T(8,128)S(1)}, f32[6,8,512]{2,1,0:T(8,128)S(1)}, u32[]{:S(2)}, u32[]{:S(2)}) collective-permute-start(f32[6,8,512]{2,1,0:T(8,128)S(1)} %slice.423), channel_id=1, source_target_pairs={{0,1},{1,2},{2,3},{3,0},{4,5},{5,6},{6,7},{7,4},{8,9},{9,10},{10,1... | collective-permute-start | bytes 294920 | tf_op jit(solution)/shard_map/ppermute | solution.py:27
  51.9 5.7 %copy.27 = f32[6,18,18,512]{3,2,0,1:T(8,128)} copy(f32[6,18,18,512]{3,2,0,1:T(8,128)} %copy-done) | data formatting | bytes 7962624
  57.5 2.5 %slice_bitcast_fusion.10 = (f32[6,18,512]{2,1,0:T(8,128)S(1)}, f32[6,18,18,512]{3,2,0,1:T(8,128)}) fusion(f32[6,18,18,512]{3,2,0,1:T(8,128)} %copy.27, f32[6,18,512]{2,1,0:T(8,128)S(1)} %slice_bitcast_fusion.11, s32[]{:T(128)S(6)} %select_n.34, f32[]{:T(128)} %bitcast, s32[]{:T(128)S(6)} %select_n.33, f32[6,17,512]{2,1,0:T(8,128)S(1)} %slice.424, ...), kind=kLoop, calls=%fused_computation.98 | loop fusion | flops 331776 | bytes 1339917 | tf_op jit(solution)/shard_map/squeeze | solution.py:101
  60.0 5.1 %collective-permute-start.5 = (f32[6,8,512]{2,1,0:T(8,128)S(1)}, f32[6,8,512]{2,1,0:T(8,128)S(1)}, u32[]{:S(2)}, u32[]{:S(2)}) collective-permute-start(f32[6,8,512]{2,1,0:T(8,128)S(1)} %slice.427), channel_id=1, source_target_pairs={{0,3},{1,0},{2,1},{3,2},{4,7},{5,4},{6,5},{7,6},{8,11},{9,8},{10,9... | collective-permute-start | bytes 294920 | tf_op jit(solution)/shard_map/ppermute | solution.py:27
  68.6 7.2 %copy.15 = f32[6,18,18,512]{3,1,2,0:T(8,128)} copy(f32[6,18,18,512]{3,2,0,1:T(8,128)} %get-tuple-element.40) | data formatting | bytes 7962624 | tf_op jit(solution)/shard_map/scatter | solution.py:111
  75.8 1.8 %fusion.35 = f32[6,18,512]{2,1,0:T(8,128)S(1)} fusion(s32[]{:T(128)S(6)} %select_n.38, f32[6,17,512]{2,1,0:T(8,128)S(1)} %bitcast.70, s32[]{:T(128)S(6)} %select_n.37, f32[6,8,512]{2,1,0:T(8,128)S(1)} %collective-permute-done.5, f32[]{:T(128)} %bitcast.7, f32[]{:T(128)S(6)} %sub.78, pred[]{:T(512)S(6)} %eq.7, f32[6,18,18,512]{3,2,0,1:T(8,128)} %copy-done), kind=kLoop, calls=%fused_computation.87 | loop fusion | flops 331776 | bytes 749585 | tf_op jit(solution)/shard_map/jit(_where)/select_n | solution.py:112
  77.8 8.6 %scatter.9 = f32[6,18,18,512]{3,1,2,0:T(8,128)} dynamic-update-slice(f32[6,18,18,512]{3,1,2,0:T(8,128)} %copy.15, f32[6,1,18,512]{3,1,2,0:T(1,128)S(1)} %reshape.87, s32[]{:T(128)} %constant.89.clone.1, s32[]{:T(128)} %constant.98.clone.1, s32[]{:T(128)} %constant.89.clone.1, s32[]{:T(128)} %constant.89.clone.1) | dynamic-update-slice | bytes 442372 | tf_op jit(solution)/shard_map/scatter | solution.py:112
  86.4 2.6 %slice_bitcast_fusion.7 = (f32[16,18,512]{2,0,1:T(8,128)S(1)}, f32[16,18,512]{2,0,1:T(8,128)S(1)}, f32[16,18,512]{2,0,1:T(8,128)S(1)}, f32[16,18,512]{2,0,1:T(8,128)S(1)}) fusion(f32[6,18,18,512]{3,1,2,0:T(8,128)} %scatter.9), kind=kLoop, calls=%fused_computation.43 | loop fusion | bytes 4718592 | tf_op jit(solution)/shard_map/slice | solution.py:59
  90.5 1.1 slice_bitcast_fusion.4
  92.3 1.0 fusion.9
  93.5 0.9 fusion.2
  94.5 1.0 fusion.31
  97.0 0.6 pad_maximum_fusion.2
  97.8 2.1 %collective-permute-start.6 = (f32[3,16,7,512]{3,1,2,0:T(8,128)S(1)}, f32[3,16,7,512]{3,1,2,0:T(8,128)S(1)}, u32[]{:S(2)}, u32[]{:S(2)}) collective-permute-start(f32[3,16,7,512]{3,1,2,0:T(8,128)S(1)} %copy.18), channel_id=1, source_target_pairs={{0,1},{1,2},{2,3},{3,0},{4,5},{5,6},{6,7},{7,4},{8,9},{9,10},{10,1... | collective-permute-start | bytes 2064392 | tf_op jit(solution)/shard_map/ppermute | solution.py:27
  100.0 17.5 %collective-permute-done.6 = f32[3,16,7,512]{3,1,2,0:T(8,128)S(1)} collective-permute-done((f32[3,16,7,512]{3,1,2,0:T(8,128)S(1)}, f32[3,16,7,512]{3,1,2,0:T(8,128)S(1)}, u32[]{:S(2)}, u32[]{:S(2)}) %collective-permute-start.6) | collective-permute-done | bytes 688160 | tf_op jit(solution)/shard_map/ppermute | solution.py:27
  118.0 1.8 %maximum_bitcast_fusion = f32[16,3,23,512]{3,1,0,2:T(4,128)S(1)} fusion(f32[1,16,16,512]{3,0,1,2:T(1,128)S(1)} %stack.14, f32[1,16,16,512]{3,0,1,2:T(1,128)S(1)} %copy.17, f32[1,16,16,512]{3,0,1,2:T(1,128)S(1)} %copy.16, f32[3,16,7,512]{3,0,1,2:T(4,128)S(1)} %copy.19), kind=kLoop, calls=%fused_computation.4 | loop fusion | flops 1695744 | bytes 4521984 | tf_op jit(solution)/shard_map/vmap()/transpose | solution.py:87
  119.9 3.0 %gather_fusion = f32[16,3,16,512]{3,1,2,0:T(4,128)} fusion(f32[16,3,23,512]{3,1,0,2:T(4,128)S(1)} %maximum_bitcast_fusion, s32[16]{0:T(128)S(1)} %get-tuple-element.48), kind=kCustom, calls=%fused_computation | custom fusion | bytes 3145984 | tf_op jit(solution)/shard_map/vmap()/gather | solution.py:87
  122.8 3.0 %gather_fusion.1 = f32[16,3,16,512]{3,1,2,0:T(4,128)} fusion(f32[16,3,23,512]{3,1,0,2:T(4,128)S(1)} %maximum_bitcast_fusion, s32[16]{0:T(128)S(1)} %get-tuple-element.49), kind=kCustom, calls=%fused_computation.1 | custom fusion | bytes 3145984 | tf_op jit(solution)/shard_map/vmap()/gather | solution.py:88
  125.9 3.0 %add_bitcast_fusion = f32[3,16,16,512]{3,0,2,1:T(4,128)S(1)} fusion(f32[16,3,16,512]{3,1,2,0:T(4,128)} %gather_fusion.1, f32[16,3,16,512]{3,1,2,0:T(4,128)} %gather_fusion, f32[16]{0:T(128)S(1)} %copy-done.5, f32[16]{0:T(128)S(1)} %broadcast_subtract_fusion), kind=kLoop, calls=%fused_computation.5 | loop fusion | flops 1179648 | bytes 4718720 | tf_op jit(solution)/shard_map/vmap()/add | solution.py:89
  128.8 1.6 %copy.20 = f32[3,16,16,512]{3,2,1,0:T(8,128)} copy(f32[3,16,16,512]{3,0,2,1:T(4,128)S(1)} %add_bitcast_fusion) | data formatting | bytes 3145728 | tf_op jit(solution)/shard_map/vmap()/add | solution.py:89
  (55 shorter events, 6.5 us)
Async XLA Ops:
  0.0 17.1 %copy-start.2 = (f32[3,16,16,512]{3,2,1,0:T(8,128)S(1)}, f32[3,16,16,512]{3,2,1,0:T(8,128)}, u32[]{:S(2)}) copy-start(f32[3,16,16,512]{3,2,1,0:T(8,128)} %param.10) | copy-start | bytes 4718596
  0.0 17.1 %copy-start.1 = (f32[3,16,16,512]{3,2,1,0:T(8,128)S(1)}, f32[3,16,16,512]{3,2,1,0:T(8,128)}, u32[]{:S(2)}) copy-start(f32[3,16,16,512]{3,2,1,0:T(8,128)} %param.11) | copy-start | bytes 4718596
  2.4 14.6 %collective-permute-start = (f32[6,1,16,512]{3,2,0,1:T(8,128)S(1)}, f32[6,1,16,512]{3,2,0,1:T(8,128)S(1)}, u32[]{:S(2)}, u32[]{:S(2)}) collective-permute-start(f32[6,1,16,512]{3,2,0,1:T(8,128)S(1)} %copy.23), channel_id=1, source_target_pairs={{0,4},{4,8},{8,12},{12,16},{16,20},{20,24},{24,28},{28,32},{32,36}... | collective-permute-start | bytes 589832 | tf_op jit(solution)/shard_map/ppermute | solution.py:19
  14.5 13.2 %collective-permute-start.1 = (f32[6,1,16,512]{3,2,0,1:T(8,128)S(1)}, f32[6,1,16,512]{3,2,0,1:T(8,128)S(1)}, u32[]{:S(2)}, u32[]{:S(2)}) collective-permute-start(f32[6,1,16,512]{3,2,0,1:T(8,128)S(1)} %copy.24), channel_id=1, source_target_pairs={{4,0},{8,4},{12,8},{16,12},{20,16},{24,20},{28,24},{32,28},{36,32}... | collective-permute-start | bytes 589832 | tf_op jit(solution)/shard_map/ppermute | solution.py:20
  17.1 18.9 %copy-start.3 = (s32[2]{0:T(128)S(1)}, s32[2]{0:T(128)}, u32[]{:S(2)}) copy-start(s32[2]{0:T(128)} %param.14) | copy-start | bytes 28
  28.9 11.2 %collective-permute-start.2 = (f32[6,18,1,512]{3,2,0,1:T(1,128)}, f32[6,18,1,512]{3,2,0,1:T(1,128)}, u32[]{:S(2)}, u32[]{:S(2)}) collective-permute-start(f32[6,18,1,512]{3,2,0,1:T(1,128)} %get-tuple-element.41), channel_id=1, source_target_pairs={{0,1},{1,2},{2,3},{3,0},{4,5},{5,6},{6,7},{7,4},{8,9},{9,10},{10,1... | collective-permute-start | bytes 663560 | tf_op jit(solution)/shard_map/ppermute | solution.py:19
  30.8 13.1 %collective-permute-start.3 = (f32[6,18,1,512]{3,2,0,1:T(1,128)}, f32[6,18,1,512]{3,2,0,1:T(1,128)}, u32[]{:S(2)}, u32[]{:S(2)}) collective-permute-start(f32[6,18,1,512]{3,2,0,1:T(1,128)} %get-tuple-element.42), channel_id=1, source_target_pairs={{1,0},{2,1},{3,2},{0,3},{5,4},{6,5},{7,6},{4,7},{9,8},{10,9},{11,1... | collective-permute-start | bytes 663560 | tf_op jit(solution)/shard_map/ppermute | solution.py:20
  39.1 11.5 %copy-start.4 = (f32[2]{0:T(128)S(1)}, f32[2]{0:T(128)}, u32[]{:S(2)}) copy-start(f32[2]{0:T(128)} %param.15) | copy-start | bytes 28
  46.0 2.4 %copy-start = (f32[6,18,18,512]{3,2,0,1:T(8,128)}, f32[6,18,18,512]{3,2,0,1:T(8,128)S(1)}, u32[]{:S(2)}) copy-start(f32[6,18,18,512]{3,2,0,1:T(8,128)S(1)} %pad_maximum_fusion) | copy-start | bytes 11943940
  48.4 9.1 %collective-permute-start.4 = (f32[6,8,512]{2,1,0:T(8,128)S(1)}, f32[6,8,512]{2,1,0:T(8,128)S(1)}, u32[]{:S(2)}, u32[]{:S(2)}) collective-permute-start(f32[6,8,512]{2,1,0:T(8,128)S(1)} %slice.423), channel_id=1, source_target_pairs={{0,1},{1,2},{2,3},{3,0},{4,5},{5,6},{6,7},{7,4},{8,9},{9,10},{10,1... | collective-permute-start | bytes 294920 | tf_op jit(solution)/shard_map/ppermute | solution.py:27
  60.0 15.8 %collective-permute-start.5 = (f32[6,8,512]{2,1,0:T(8,128)S(1)}, f32[6,8,512]{2,1,0:T(8,128)S(1)}, u32[]{:S(2)}, u32[]{:S(2)}) collective-permute-start(f32[6,8,512]{2,1,0:T(8,128)S(1)} %slice.427), channel_id=1, source_target_pairs={{0,3},{1,0},{2,1},{3,2},{4,7},{5,4},{6,5},{7,6},{8,11},{9,8},{10,9... | collective-permute-start | bytes 294920 | tf_op jit(solution)/shard_map/ppermute | solution.py:27
  86.4 3.9 %slice-start = ((s8[5308416]{0:T(1024)(128)(4,1)}), s8[4194304]{0:T(1024)(128)(4,1)S(1)}, s32[]{:S(2)}) async-start(s8[5308416]{0:T(1024)(128)(4,1)} %bitcast.64), calls=%async_computation | async-start | bytes 8388608
  89.1 1.4 %slice-start.1 = ((s8[5308416]{0:T(1024)(128)(4,1)}), s8[1114112]{0:T(1024)(128)(4,1)S(1)}, s32[]{:S(2)}) async-start(s8[5308416]{0:T(1024)(128)(4,1)} %bitcast.64), calls=%async_computation.1 | async-start | bytes 2228224
  96.0 4.0 %copy-start.5 = (f32[16]{0:T(128)S(1)}, f32[16]{0:T(128)}, u32[]{:S(2)}) copy-start(f32[16]{0:T(128)} %param.13) | copy-start | bytes 196
  96.0 4.0 %copy-start.6 = (s32[16]{0:T(128)S(1)}, s32[16]{0:T(128)}, u32[]{:S(2)}) copy-start(s32[16]{0:T(128)} %param.12) | copy-start | bytes 196
  97.8 19.7 %collective-permute-start.6 = (f32[3,16,7,512]{3,1,2,0:T(8,128)S(1)}, f32[3,16,7,512]{3,1,2,0:T(8,128)S(1)}, u32[]{:S(2)}, u32[]{:S(2)}) collective-permute-start(f32[3,16,7,512]{3,1,2,0:T(8,128)S(1)} %copy.18), channel_id=1, source_target_pairs={{0,1},{1,2},{2,3},{3,0},{4,5},{5,6},{6,7},{7,4},{8,9},{9,10},{10,1... | collective-permute-start | bytes 2064392 | tf_op jit(solution)/shard_map/ppermute | solution.py:27
where the time goes:
time: 131 us; the launch traced here: 130 us
  local copies, waits for them, and re-layouts  41.4 us (32%)
  waiting for transfers between devices  33.1 us (25%)
  starting transfers between devices  30.4 us (23%)
  other arithmetic  18.4 us (14%)
  between operations  7.11 us (5%)
    ppermute x3, waiting for transfers between devices, from_behind(): lax.ppermute(shard, axis, [(i, (i + by) % peers) for i in range(peers)])  17.5 us
    ppermute x2, waiting for transfers between devices, with_halo(): after = lax.ppermute(first, axis, down)  14 us
    ppermute x2, starting transfers between devices, with_halo(): before = lax.ppermute(last, axis, up)  14 us
    ppermute x3, starting transfers between devices, from_behind(): lax.ppermute(shard, axis, [(i, (i + by) % peers) for i in range(peers)])  9.4 us
    scatter x1, local copies, waits for them, and re-layouts, body(): padded.at[:, -1].set(jnp.where(last_block, remapped_high, high_rows))  8.59 us
    unnamed x22, local copies, waits for them, and re-layouts  8.29 us
    scatter x1, local copies, waits for them, and re-layouts, body(): padded = padded.at[:, 0].set(jnp.where(first_block, remapped_low, low_rows))  7.23 us
    ppermute x2, starting transfers between devices, with_halo(): after = lax.ppermute(first, axis, down)  7.03 us
  transfers between devices with their start and end apart: 7, of which 5 were waited for; matrix products, arithmetic and copies ran while one was open for 11% of the time, Pallas kernels for 0%

commit v1 on v0

v1 whole, which is shorter than its diff:
```python
import jax
import jax.numpy as jnp
from jax import lax
from jax.experimental import pallas as pl
from jax.experimental.pallas import tpu as pltpu
from jax.sharding import PartitionSpec as P

KMAX = 6
COURANT = 0.4
WIDE = KMAX + 2


def shifted(x, db, dp):
    nb, nq = lax.axis_size("blocks"), lax.axis_size("phi")
    if dp == 0:
        return lax.ppermute(x, "blocks", [(b, (b + db) % nb) for b in range(nb)])
    if db == 0:
        return lax.ppermute(x, "phi", [(q, (q + dp) % nq) for q in range(nq)])
    pairs = [
        (b * nq + q, ((b + db) % nb) * nq + (q + dp) % nq)
        for b in range(nb)
        for q in range(nq)
    ]
    return lax.ppermute(x, ("blocks", "phi"), pairs)


def below(v):
    return pltpu.roll(v, 1, 1)


def above(v):
    return pltpu.roll(v, v.shape[1] - 1, 1)


def ct_kernel(p_ref, u_ref, ez_s, ey_s, ex_s):
    rows = u_ref.shape[1]
    ny = u_ref.shape[2]

    def emf_row(a, carry):
        fx_a = p_ref[0, a, pl.ds(1, ny + 1), :]
        fx_ab = p_ref[0, a, pl.ds(0, ny + 1), :]
        fy_a = p_ref[1, a, pl.ds(1, ny + 1), :]
        fy_m = p_ref[1, a - 1, pl.ds(1, ny + 1), :]
        vx = (
            p_ref[3, a, pl.ds(1, ny + 1), :]
            + p_ref[3, a - 1, pl.ds(1, ny + 1), :]
            + p_ref[3, a, pl.ds(0, ny + 1), :]
            + p_ref[3, a - 1, pl.ds(0, ny + 1), :]
        )
        vy = (
            p_ref[4, a, pl.ds(1, ny + 1), :]
            + p_ref[4, a - 1, pl.ds(1, ny + 1), :]
            + p_ref[4, a, pl.ds(0, ny + 1), :]
            + p_ref[4, a - 1, pl.ds(0, ny + 1), :]
        )
        ez = (0.25 * vy) * (0.5 * (fx_a + fx_ab)) - (0.25 * vx) * (0.5 * (fy_a + fy_m))
        ez_s[a - 1, pl.ds(0, ny + 1), :] = ez

        mfx = p_ref[0, a, pl.ds(1, ny), :]
        mfz = p_ref[2, a, pl.ds(1, ny), :]
        mfz_m = p_ref[2, a - 1, pl.ds(1, ny), :]
        pvx = p_ref[3, a, pl.ds(1, ny), :] + p_ref[3, a - 1, pl.ds(1, ny), :]
        pvz = p_ref[5, a, pl.ds(1, ny), :] + p_ref[5, a - 1, pl.ds(1, ny), :]
        yfx = 0.5 * (mfx + below(mfx))
        yfz = 0.5 * (mfz + mfz_m)
        yvx = 0.25 * (pvx + below(pvx))
        yvz = 0.25 * (pvz + below(pvz))
        ey_s[a - 1] = yvx * yfz - yvz * yfx

        rfy = p_ref[1, a, pl.ds(1, ny + 1), :]
        rfz = p_ref[2, a, pl.ds(1, ny + 1), :]
        rfz_b = p_ref[2, a, pl.ds(0, ny + 1), :]
        cvy = p_ref[4, a, pl.ds(1, ny + 1), :] + p_ref[4, a, pl.ds(0, ny + 1), :]
        cvz = p_ref[5, a, pl.ds(1, ny + 1), :] + p_ref[5, a, pl.ds(0, ny + 1), :]
        xfy = 0.5 * (rfy + below(rfy))
        xfz = 0.5 * (rfz + rfz_b)
        xvy = 0.25 * (cvy + below(cvy))
        xvz = 0.25 * (cvz + below(cvz))
        ex_s[a - 1, pl.ds(0, ny + 1), :] = xvz * xfy - xvy * xfz
        return carry

    lax.fori_loop(1, rows + 2, emf_row, 0)

    def update_row(r, carry):
        a = r + 1
        ez_r = ez_s[r, pl.ds(0, ny), :]
        ez_r1 = ez_s[r, pl.ds(1, ny), :]
        ez_n = ez_s[r + 1, pl.ds(0, ny), :]
        ey_r = ey_s[r]
        ey_n = ey_s[r + 1]
        ex_r = ex_s[r, pl.ds(0, ny), :]
        ex_r1 = ex_s[r, pl.ds(1, ny), :]
        fx = p_ref[0, a, pl.ds(1, ny), :]
        fy = p_ref[1, a, pl.ds(1, ny), :]
        fz = p_ref[2, a, pl.ds(1, ny), :]
        u_ref[0, r] = fx - COURANT * ((ez_r1 - ez_r) - (above(ey_r) - ey_r))
        u_ref[1, r] = fy - COURANT * ((above(ex_r) - ex_r) - (ez_n - ez_r))
        u_ref[2, r] = fz - COURANT * ((ey_n - ey_r) - (ex_r1 - ex_r))
        return carry

    lax.fori_loop(0, rows, update_row, 0)


def ct_update(padded):
    _, px, py, nz = padded.shape
    rows, ny = px - 2, py - 2
    vmem = pl.BlockSpec(memory_space=pltpu.VMEM)
    return pl.pallas_call(
        ct_kernel,
        out_shape=jax.ShapeDtypeStruct((3, rows, ny, nz), padded.dtype),
        in_specs=[vmem],
        out_specs=vmem,
        scratch_shapes=[
            pltpu.VMEM((rows + 1, ny + 8, nz), jnp.float32),
            pltpu.VMEM((rows + 1, ny, nz), jnp.float32),
            pltpu.VMEM((rows + 1, ny + 8, nz), jnp.float32),
        ],
        cost_estimate=pl.CostEstimate(
            flops=120 * rows * ny * nz, transcendentals=0,
            bytes_accessed=4 * (6 * px * py + 3 * rows * ny) * nz,
        ),
    )(padded)


def advect_kernel(shift_ref, frac_ref, u_ref, rec_ref, o_ref, ext):
    rows, ny = u_ref.shape[1], u_ref.shape[2]
    lead = 8
    ext[:, :, pl.ds(lead - KMAX - 1, KMAX + 1), :] = rec_ref[...]
    ext[:, :, pl.ds(lead, ny), :] = u_ref[...]

    def strip(x, carry):
        s = shift_ref[x]
        w = frac_ref[x]
        for k in range(KMAX + 1):
            @pl.when(s == k)
            def _():
                near = ext[:, x, pl.ds(lead - k, ny), :]
                far = ext[:, x, pl.ds(lead - k - 1, ny), :]
                o_ref[:, x] = (1.0 - w) * near + w * far
        return carry

    lax.fori_loop(0, rows, strip, 0)


def advect(updated, received, strip_shift, strip_frac):
    _, rows, ny, nz = updated.shape
    vmem = pl.BlockSpec(memory_space=pltpu.VMEM)
    smem = pl.BlockSpec(memory_space=pltpu.SMEM)
    return pl.pallas_call(
        advect_kernel,
        out_shape=jax.ShapeDtypeStruct(updated.shape, updated.dtype),
        in_specs=[smem, smem, vmem, vmem],
        out_specs=vmem,
        scratch_shapes=[pltpu.VMEM((3, rows, ny + 8, nz), jnp.float32)],
        cost_estimate=pl.CostEstimate(
            flops=3 * 3 * rows * ny * nz, transcendentals=0,
            bytes_accessed=4 * 3 * rows * (2 * ny + KMAX + 1) * nz,
        ),
    )(strip_shift, strip_frac, updated, received)


def body(field, velocity, strip_shift, strip_frac, edge_shift, edge_frac):
    stacked = jnp.concatenate([field, velocity], axis=0)
    _, nx, ny, nz = stacked.shape
    nb = lax.axis_size("blocks")
    b = lax.axis_index("blocks")

    xm = shifted(stacked[:, nx - 1], 1, 0)
    xp = shifted(stacked[:, 0], -1, 0)
    ym = shifted(stacked[:, :, ny - 1], 0, 1)
    yp = shifted(stacked[:, :, 0], 0, -1)
    mm = shifted(stacked[:, nx - 1, ny - WIDE :], 1, 1)
    pm = shifted(stacked[:, 0, ny - 1 : ny], -1, 1)
    mp = shifted(stacked[:, nx - 1, 0:1], 1, -1)
    pp = shifted(stacked[:, 0, :WIDE], -1, -1)

    span = ny + 2
    low_line = jnp.concatenate([mm, xm, mp], axis=1)
    inner = edge_shift[0]
    low_ghost = (1.0 - edge_frac[0]) * lax.dynamic_slice_in_dim(
        low_line, WIDE - 1 - inner, span, axis=1
    ) + edge_frac[0] * lax.dynamic_slice_in_dim(low_line, WIDE - 2 - inner, span, axis=1)
    low_row = jnp.where(b == 0, low_ghost, low_line[:, WIDE - 1 : WIDE - 1 + span])

    high_line = jnp.concatenate([pm, xp, pp], axis=1)
    outer = edge_shift[1]
    high_ghost = (1.0 - edge_frac[1]) * lax.dynamic_slice_in_dim(
        high_line, outer, span, axis=1
    ) + edge_frac[1] * lax.dynamic_slice_in_dim(high_line, outer + 1, span, axis=1)
    high_row = jnp.where(b == nb - 1, high_ghost, high_line[:, :span])

    middle = jnp.concatenate([ym[:, :, None], stacked, yp[:, :, None]], axis=2)
    padded = jnp.concatenate([low_row[:, None], middle, high_row[:, None]], axis=1)

    updated = ct_update(padded)
    received = shifted(updated[:, :, ny - KMAX - 1 :], 0, 1)
    return advect(updated, received, strip_shift, strip_frac)


def solution(mesh):
    placed = (
        P(None, "blocks", "phi", None),
        P(None, "blocks", "phi", None),
        P("blocks"),
        P("blocks"),
        P(),
        P(),
    )
    return jax.shard_map(
        body, mesh=mesh, in_specs=placed, out_specs=P(None, "blocks", "phi", None), check_vma=False
    )
```

time: 131 us -> 109 us (0.83)
  the two profiles are of different devices: /device:TPU:1 before, /device:TPU:56 now
where the time goes in v1:
time: 109 us; the launch traced here: 108 us
  starting transfers between devices  40.1 us (37%)
  waiting for transfers between devices  26.7 us (24%)
  Pallas kernels  12.5 us (11%)
  other arithmetic  10.8 us (10%)
  local copies, waits for them, and re-layouts  10.6 us (10%)
  between operations  7.37 us (7%)
    ppermute x3, waiting for transfers between devices, shifted(): return lax.ppermute(x, 'phi', [(q, (q + dp) % nq) for q in range(nq)])  26.7 us
    ppermute x4, starting transfers between devices, shifted(): return lax.ppermute(x, ('blocks', 'phi'), pairs)  20.7 us
    ppermute x2, starting transfers between devices, shifted(): return lax.ppermute(x, 'blocks', [(b, (b + db) % nb) for b in range(nb)])  10.4 us
    ppermute x3, starting transfers between devices, shifted(): return lax.ppermute(x, 'phi', [(q, (q + dp) % nq) for q in range(nq)])  9.02 us
    pallas_call x1, Pallas kernels, ct_update(): pl.pallas_call(ct_kernel, out_shape=jax.ShapeDtypeStruct((3, rows, ny, nz...  8.39 us
    pallas_call x1, Pallas kernels, advect(): pl.pallas_call(advect_kernel, out_shape=jax.ShapeDtypeStruct(updated.shap...  4.15 us
    concatenate x1, other arithmetic, body(): jnp.concatenate([low_row[:, None], middle, high_row[:, None]], axis=1)  2.86 us
    broadcast_in_dim x2, local copies, waits for them, and re-layouts, body(): middle = jnp.concatenate([ym[:, :, None], stacked, yp[:, :, None]], axis=2)  2.26 us
  transfers between devices with their start and end apart: 9, of which 3 were waited for; matrix products, arithmetic and copies ran while one was open for 11% of the time, Pallas kernels for 0%

profile of v1, /device:TPU:56, one launch (start us, length us, event | category | flops | bytes accessed | tf_op | source)
XLA Modules:
  0.0 108.1 jit_solution(2751172218319970829)
XLA Ops:
  0.0 1.6 %slice_bitcast_fusion.5 = (f32[6,1,512]{2,1,0:T(1,128)}, f32[6,1,512]{2,1,0:T(1,128)S(1)}) fusion(f32[3,16,16,512]{3,2,1,0:T(8,128)} %param.7, f32[3,16,16,512]{3,2,1,0:T(8,128)} %param.6), kind=kLoop, calls=%fused_computation.15 | loop fusion | flops 786432 | bytes 3170304 | tf_op jit(solution)/shard_map/squeeze | solution.py:174
  1.6 7.3 %collective-permute-start.2 = (f32[6,1,512]{2,1,0:T(1,128)}, f32[6,1,512]{2,1,0:T(1,128)}, u32[]{:S(2)}, u32[]{:S(2)}) collective-permute-start(f32[6,1,512]{2,1,0:T(1,128)} %get-tuple-element.5), channel_id=1, source_target_pairs={{0,7},{1,4},{2,5},{3,6},{4,11},{5,8},{6,9},{7,10},{8,15},{9,12},{1... | collective-permute-start | bytes 36872 | tf_op jit(solution)/shard_map/ppermute | solution.py:24
  9.0 5.7 %collective-permute-start.5 = (f32[6,1,512]{2,1,0:T(1,128)S(1)}, f32[6,1,512]{2,1,0:T(1,128)}, u32[]{:S(2)}, u32[]{:S(2)}) collective-permute-start(f32[6,1,512]{2,1,0:T(1,128)S(1)} %get-tuple-element.6), channel_id=1, source_target_pairs={{0,509},{1,510},{2,511},{3,508},{4,1},{5,2},{6,3},{7,0},{8,5},{9,6... | collective-permute-start | bytes 36872 | tf_op jit(solution)/shard_map/ppermute | solution.py:24
  14.7 0.7 slice_bitcast_fusion.3
  15.4 1.9 %collective-permute-start = (f32[6,8,512]{2,1,0:T(8,128)S(1)}, f32[6,8,512]{2,1,0:T(8,128)}, u32[]{:S(2)}, u32[]{:S(2)}) collective-permute-start(f32[6,8,512]{2,1,0:T(8,128)S(1)} %get-tuple-element.9), channel_id=1, source_target_pairs={{0,5},{1,6},{2,7},{3,4},{4,9},{5,10},{6,11},{7,8},{8,13},{9,14},{1... | collective-permute-start | bytes 294920 | tf_op jit(solution)/shard_map/ppermute | solution.py:24
  17.3 5.7 %collective-permute-start.7 = (f32[6,8,512]{2,1,0:T(8,128)}, f32[6,8,512]{2,1,0:T(8,128)}, u32[]{:S(2)}, u32[]{:S(2)}) collective-permute-start(f32[6,8,512]{2,1,0:T(8,128)} %get-tuple-element.10), channel_id=1, source_target_pairs={{0,511},{1,508},{2,509},{3,510},{4,3},{5,0},{6,1},{7,2},{8,7},{9,4... | collective-permute-start | bytes 294920 | tf_op jit(solution)/shard_map/ppermute | solution.py:24
  23.1 0.8 slice_bitcast_fusion.1
  23.8 2.7 %collective-permute-start.1 = (f32[6,16,512]{2,1,0:T(8,128)}, f32[6,16,512]{2,1,0:T(8,128)}, u32[]{:S(2)}, u32[]{:S(2)}) collective-permute-start(f32[6,16,512]{2,1,0:T(8,128)} %get-tuple-element.7), channel_id=1, source_target_pairs={{0,4},{4,8},{8,12},{12,16},{16,20},{20,24},{24,28},{28,32},{32,36}... | collective-permute-start | bytes 589832 | tf_op jit(solution)/shard_map/ppermute | solution.py:16
  26.6 2.0 %pad_maximum_fusion.2 = f32[6,16,16,512]{3,2,1,0:T(8,128)} fusion(f32[3,16,16,512]{3,2,1,0:T(8,128)S(1)} %copy-done, f32[3,16,16,512]{3,2,1,0:T(8,128)S(1)} %copy-done.1), kind=kLoop, calls=%fused_computation.2 | loop fusion | flops 786432 | bytes 6291456 | tf_op jit(solution)/shard_map/concatenate | solution.py:163
  28.5 0.6 fusion.4
  36.7 0.7 copy.57
  37.4 0.7 copy.56
  38.8 7.7 %collective-permute-start.6 = (f32[6,16,512]{2,1,0:T(8,128)}, f32[6,16,512]{2,1,0:T(8,128)}, u32[]{:S(2)}, u32[]{:S(2)}) collective-permute-start(f32[6,16,512]{2,1,0:T(8,128)} %get-tuple-element.8), channel_id=1, source_target_pairs={{0,508},{4,0},{8,4},{12,8},{16,12},{20,16},{24,20},{28,24},{32,28}... | collective-permute-start | bytes 589832 | tf_op jit(solution)/shard_map/ppermute | solution.py:16
  46.5 0.9 constant_dynamic-update-slice_fusion.1
  47.4 4.3 %collective-permute-start.4 = (f32[6,16,512]{2,1,0:T(8,128)}, f32[6,16,512]{2,1,0:T(8,128)}, u32[]{:S(2)}, u32[]{:S(2)}) collective-permute-start(f32[6,16,512]{2,1,0:T(8,128)} %bitcast.34), channel_id=1, source_target_pairs={{0,3},{1,0},{2,1},{3,2},{4,7},{5,4},{6,5},{7,6},{8,11},{9,8},{10,9... | collective-permute-start | bytes 589832 | tf_op jit(solution)/shard_map/ppermute | solution.py:18
  51.7 0.9 constant_dynamic-update-slice_fusion
  52.6 2.8 %collective-permute-start.3 = (f32[6,16,512]{2,1,0:T(8,128)}, f32[6,16,512]{2,1,0:T(8,128)}, u32[]{:S(2)}, u32[]{:S(2)}) collective-permute-start(f32[6,16,512]{2,1,0:T(8,128)} %bitcast.33), channel_id=1, source_target_pairs={{0,1},{1,2},{2,3},{3,0},{4,5},{5,6},{6,7},{7,4},{8,9},{9,10},{10,1... | collective-permute-start | bytes 589832 | tf_op jit(solution)/shard_map/ppermute | solution.py:18
  55.4 0.8 dynamic-update-slice.2
  56.3 0.7 fusion.1
  56.9 1.6 %collective-permute-done.4 = f32[6,16,512]{2,1,0:T(8,128)} collective-permute-done((f32[6,16,512]{2,1,0:T(8,128)}, f32[6,16,512]{2,1,0:T(8,128)}, u32[]{:S(2)}, u32[]{:S(2)}) %collective-permute-start.4) | collective-permute-done | bytes 196640 | tf_op jit(solution)/shard_map/ppermute | solution.py:18
  58.6 1.1 %copy.34 = f32[6,16,1,512]{3,2,0,1:T(1,128)S(1)} copy(f32[6,16,1,512]{3,1,0,2:T(8,128)} %bitcast.13) | data formatting | bytes 393216 | tf_op jit(solution)/shard_map/broadcast_in_dim | solution.py:192
  59.7 8.2 %collective-permute-done.3 = f32[6,16,512]{2,1,0:T(8,128)} collective-permute-done((f32[6,16,512]{2,1,0:T(8,128)}, f32[6,16,512]{2,1,0:T(8,128)}, u32[]{:S(2)}, u32[]{:S(2)}) %collective-permute-start.3) | collective-permute-done | bytes 196640 | tf_op jit(solution)/shard_map/ppermute | solution.py:18
  67.9 1.1 %copy.33 = f32[6,16,1,512]{3,2,0,1:T(1,128)S(1)} copy(f32[6,16,1,512]{3,1,0,2:T(8,128)} %bitcast.11) | data formatting | bytes 393216 | tf_op jit(solution)/shard_map/broadcast_in_dim | solution.py:192
  69.1 1.0 pad_maximum_fusion.3
  70.1 0.8 fusion
  70.9 2.9 %pad_maximum_fusion.p_ref = f32[6,18,18,512]{3,2,1,0:T(8,128)} fusion(f32[6,1,18,512]{3,2,1,0:T(8,128)S(1)} %fusion, f32[6,1,18,512]{3,2,1,0:T(8,128)S(1)} %fusion.1, f32[6,16,1,512]{3,2,0,1:T(1,128)S(1)} %copy.34, f32[6,16,1,512]{3,2,0,1:T(1,128)S(1)} %copy.33, f32[6,16,16,512]{3,2,1,0:T(8,128)S(1)} %copy-done.2), kind=kLoop, calls=%fused_computation | loop fusion | flops 3760128 | bytes 7962624 | tf_op jit(solution)/shard_map/concatenate | solution.py:193
  73.8 8.4 %shard_map.64.u_ref = f32[3,16,16,512]{3,2,1,0:T(8,128)} custom-call(f32[6,18,18,512]{3,2,1,0:T(8,128)} %pad_maximum_fusion.p_ref), custom_call_target="tpu_custom_call" | custom-call | flops 15728640 | bytes 5554176 | tf_op jit(solution)/shard_map/pallas_call | solution.py:108
  82.2 1.2 %slice.72 = f32[3,16,7,512]{3,2,1,0:T(8,128)S(1)} slice(f32[3,16,16,512]{3,2,1,0:T(8,128)} %shard_map.64.u_ref), slice={[0:3], [0:16], [9:16], [0:512]} | slice | bytes 1376256 | tf_op jit(solution)/shard_map/slice | solution.py:196
  83.8 1.9 %collective-permute-start.8 = (f32[3,16,7,512]{3,1,2,0:T(8,128)S(1)}, f32[3,16,7,512]{3,1,2,0:T(8,128)S(1)}, u32[]{:S(2)}, u32[]{:S(2)}) collective-permute-start(f32[3,16,7,512]{3,1,2,0:T(8,128)S(1)} %copy.37), channel_id=1, source_target_pairs={{0,1},{1,2},{2,3},{3,0},{4,5},{5,6},{6,7},{7,4},{8,9},{9,10},{10,1... | collective-permute-start | bytes 2064392 | tf_op jit(solution)/shard_map/ppermute | solution.py:18
  85.7 16.9 %collective-permute-done.8 = f32[3,16,7,512]{3,1,2,0:T(8,128)S(1)} collective-permute-done((f32[3,16,7,512]{3,1,2,0:T(8,128)S(1)}, f32[3,16,7,512]{3,1,2,0:T(8,128)S(1)}, u32[]{:S(2)}, u32[]{:S(2)}) %collective-permute-start.8) | collective-permute-done | bytes 688160 | tf_op jit(solution)/shard_map/ppermute | solution.py:18
  102.6 1.3 %copy.38.rec_ref = f32[3,16,7,512]{3,2,1,0:T(8,128)} copy(f32[3,16,7,512]{3,1,2,0:T(8,128)S(1)} %collective-permute-done.8) | data formatting | bytes 1376256 | tf_op jit(solution)/shard_map/ppermute | solution.py:18
  103.9 4.2 %shard_map.65 = f32[3,16,16,512]{3,2,1,0:T(8,128)} custom-call(s32[16]{0:T(128)} %shift_ref.1, f32[16]{0:T(128)} %frac_ref.1, f32[3,16,16,512]{3,2,1,0:T(8,128)} %shard_map.64.u_ref, f32[3,16,7,512]{3,2,1,0:T(8,128)} %copy.38.rec_ref), custom_call_target="tpu_custom_call" | custom-call | flops 1179648 | bytes 3833856 | tf_op jit(solution)/shard_map/pallas_call | solution.py:149
  (19 shorter events, 1.5 us)
Async XLA Ops:
  0.0 14.7 %copy-start = (f32[3,16,16,512]{3,2,1,0:T(8,128)S(1)}, f32[3,16,16,512]{3,2,1,0:T(8,128)}, u32[]{:S(2)}) copy-start(f32[3,16,16,512]{3,2,1,0:T(8,128)} %param.7) | copy-start | bytes 4718596
  0.0 14.7 %copy-start.1 = (f32[3,16,16,512]{3,2,1,0:T(8,128)S(1)}, f32[3,16,16,512]{3,2,1,0:T(8,128)}, u32[]{:S(2)}) copy-start(f32[3,16,16,512]{3,2,1,0:T(8,128)} %param.6) | copy-start | bytes 4718596
  1.6 51.0 %collective-permute-start.2 = (f32[6,1,512]{2,1,0:T(1,128)}, f32[6,1,512]{2,1,0:T(1,128)}, u32[]{:S(2)}, u32[]{:S(2)}) collective-permute-start(f32[6,1,512]{2,1,0:T(1,128)} %get-tuple-element.5), channel_id=1, source_target_pairs={{0,7},{1,4},{2,5},{3,6},{4,11},{5,8},{6,9},{7,10},{8,15},{9,12},{1... | collective-permute-start | bytes 36872 | tf_op jit(solution)/shard_map/ppermute | solution.py:24
  9.0 60.1 %collective-permute-start.5 = (f32[6,1,512]{2,1,0:T(1,128)S(1)}, f32[6,1,512]{2,1,0:T(1,128)}, u32[]{:S(2)}, u32[]{:S(2)}) collective-permute-start(f32[6,1,512]{2,1,0:T(1,128)S(1)} %get-tuple-element.6), channel_id=1, source_target_pairs={{0,509},{1,510},{2,511},{3,508},{4,1},{5,2},{6,3},{7,0},{8,5},{9,6... | collective-permute-start | bytes 36872 | tf_op jit(solution)/shard_map/ppermute | solution.py:24
  15.4 23.4 %collective-permute-start = (f32[6,8,512]{2,1,0:T(8,128)S(1)}, f32[6,8,512]{2,1,0:T(8,128)}, u32[]{:S(2)}, u32[]{:S(2)}) collective-permute-start(f32[6,8,512]{2,1,0:T(8,128)S(1)} %get-tuple-element.9), channel_id=1, source_target_pairs={{0,5},{1,6},{2,7},{3,4},{4,9},{5,10},{6,11},{7,8},{8,13},{9,14},{1... | collective-permute-start | bytes 294920 | tf_op jit(solution)/shard_map/ppermute | solution.py:24
  17.3 51.7 %collective-permute-start.7 = (f32[6,8,512]{2,1,0:T(8,128)}, f32[6,8,512]{2,1,0:T(8,128)}, u32[]{:S(2)}, u32[]{:S(2)}) collective-permute-start(f32[6,8,512]{2,1,0:T(8,128)} %get-tuple-element.10), channel_id=1, source_target_pairs={{0,511},{1,508},{2,509},{3,510},{4,3},{5,0},{6,1},{7,2},{8,7},{9,4... | collective-permute-start | bytes 294920 | tf_op jit(solution)/shard_map/ppermute | solution.py:24
  23.8 23.5 %collective-permute-start.1 = (f32[6,16,512]{2,1,0:T(8,128)}, f32[6,16,512]{2,1,0:T(8,128)}, u32[]{:S(2)}, u32[]{:S(2)}) collective-permute-start(f32[6,16,512]{2,1,0:T(8,128)} %get-tuple-element.7), channel_id=1, source_target_pairs={{0,4},{4,8},{8,12},{12,16},{16,20},{20,24},{24,28},{28,32},{32,36}... | collective-permute-start | bytes 589832 | tf_op jit(solution)/shard_map/ppermute | solution.py:16
  26.5 2.0 %copy-start.3 = (s32[2]{0:T(128)S(1)}, s32[2]{0:T(128)}, u32[]{:S(2)}) copy-start(s32[2]{0:T(128)} %param.10) | copy-start | bytes 28
  26.5 7.8 %copy-start.4 = (f32[2]{0:T(128)S(1)}, f32[2]{0:T(128)}, u32[]{:S(2)}) copy-start(f32[2]{0:T(128)} %param.11) | copy-start | bytes 28
  36.7 34.3 %copy-start.2 = (f32[6,16,16,512]{3,2,1,0:T(8,128)S(1)}, f32[6,16,16,512]{3,2,1,0:T(8,128)}, u32[]{:S(2)}) copy-start(f32[6,16,16,512]{3,2,1,0:T(8,128)} %pad_maximum_fusion.2) | copy-start | bytes 9437188
  38.8 30.3 %collective-permute-start.6 = (f32[6,16,512]{2,1,0:T(8,128)}, f32[6,16,512]{2,1,0:T(8,128)}, u32[]{:S(2)}, u32[]{:S(2)}) collective-permute-start(f32[6,16,512]{2,1,0:T(8,128)} %get-tuple-element.8), channel_id=1, source_target_pairs={{0,508},{4,0},{8,4},{12,8},{16,12},{20,16},{24,20},{28,24},{32,28}... | collective-permute-start | bytes 589832 | tf_op jit(solution)/shard_map/ppermute | solution.py:16
  47.4 11.2 %collective-permute-start.4 = (f32[6,16,512]{2,1,0:T(8,128)}, f32[6,16,512]{2,1,0:T(8,128)}, u32[]{:S(2)}, u32[]{:S(2)}) collective-permute-start(f32[6,16,512]{2,1,0:T(8,128)} %bitcast.34), channel_id=1, source_target_pairs={{0,3},{1,0},{2,1},{3,2},{4,7},{5,4},{6,5},{7,6},{8,11},{9,8},{10,9... | collective-permute-start | bytes 589832 | tf_op jit(solution)/shard_map/ppermute | solution.py:18
  52.6 15.3 %collective-permute-start.3 = (f32[6,16,512]{2,1,0:T(8,128)}, f32[6,16,512]{2,1,0:T(8,128)}, u32[]{:S(2)}, u32[]{:S(2)}) collective-permute-start(f32[6,16,512]{2,1,0:T(8,128)} %bitcast.33), channel_id=1, source_target_pairs={{0,1},{1,2},{2,3},{3,0},{4,5},{5,6},{6,7},{7,4},{8,9},{9,10},{10,1... | collective-permute-start | bytes 589832 | tf_op jit(solution)/shard_map/ppermute | solution.py:18
  83.8 18.8 %collective-permute-start.8 = (f32[3,16,7,512]{3,1,2,0:T(8,128)S(1)}, f32[3,16,7,512]{3,1,2,0:T(8,128)S(1)}, u32[]{:S(2)}, u32[]{:S(2)}) collective-permute-start(f32[3,16,7,512]{3,1,2,0:T(8,128)S(1)} %copy.37), channel_id=1, source_target_pairs={{0,1},{1,2},{2,3},{3,0},{4,5},{5,6},{6,7},{7,4},{8,9},{9,10},{10,1... | collective-permute-start | bytes 2064392 | tf_op jit(solution)/shard_map/ppermute | solution.py:18

commit v2 on v1

--- a/solution.py
+++ b/solution.py
@@ -167,28 +167,36 @@
 
     xm = shifted(stacked[:, nx - 1], 1, 0)
     xp = shifted(stacked[:, 0], -1, 0)
-    ym = shifted(stacked[:, :, ny - 1], 0, 1)
-    yp = shifted(stacked[:, :, 0], 0, -1)
-    mm = shifted(stacked[:, nx - 1, ny - WIDE :], 1, 1)
-    pm = shifted(stacked[:, 0, ny - 1 : ny], -1, 1)
-    mp = shifted(stacked[:, nx - 1, 0:1], 1, -1)
-    pp = shifted(stacked[:, 0, :WIDE], -1, -1)
+    low_col = jnp.concatenate(
+        [xm[:, ny - WIDE :], xm[:, ny - 1 : ny], stacked[:, :, ny - 1], xp[:, ny - 1 : ny]], axis=1
+    )
+    high_col = jnp.concatenate(
+        [xp[:, :WIDE], xm[:, 0:1], stacked[:, :, 0], xp[:, 0:1]], axis=1
+    )
+    from_low = shifted(low_col, 0, 1)
+    from_high = shifted(high_col, 0, -1)
+    ym = from_low[:, WIDE:]
+    yp = from_high[:, WIDE:]
 
     span = ny + 2
-    low_line = jnp.concatenate([mm, xm, mp], axis=1)
+    low_line = jnp.concatenate([from_low[:, :WIDE], xm, yp[:, 0:1]], axis=1)
     inner = edge_shift[0]
     low_ghost = (1.0 - edge_frac[0]) * lax.dynamic_slice_in_dim(
         low_line, WIDE - 1 - inner, span, axis=1
     ) + edge_frac[0] * lax.dynamic_slice_in_dim(low_line, WIDE - 2 - inner, span, axis=1)
-    low_row = jnp.where(b == 0, low_ghost, low_line[:, WIDE - 1 : WIDE - 1 + span])
-
-    high_line = jnp.concatenate([pm, xp, pp], axis=1)
+    low_plain = jnp.concatenate([ym[:, 0:1], xm, yp[:, 0:1]], axis=1)
+    low_row = jnp.where(b == 0, low_ghost, low_plain)
+
+    high_line = jnp.concatenate([ym[:, nx + 1 :], xp, from_high[:, :WIDE]], axis=1)
     outer = edge_shift[1]
     high_ghost = (1.0 - edge_frac[1]) * lax.dynamic_slice_in_dim(
         high_line, outer, span, axis=1
     ) + edge_frac[1] * lax.dynamic_slice_in_dim(high_line, outer + 1, span, axis=1)
-    high_row = jnp.where(b == nb - 1, high_ghost, high_line[:, :span])
-
+    high_plain = jnp.concatenate([ym[:, nx + 1 :], xp, yp[:, nx + 1 :]], axis=1)
+    high_row = jnp.where(b == nb - 1, high_ghost, high_plain)
+
+    ym = ym[:, 1 : nx + 1]
+    yp = yp[:, 1 : nx + 1]
     middle = jnp.concatenate([ym[:, :, None], stacked, yp[:, :, None]], axis=2)
     padded = jnp.concatenate([low_row[:, None], middle, high_row[:, None]], axis=1)
 

time: 109 us -> 101 us (0.927)
  the two profiles are of different devices: /device:TPU:56 before, /device:TPU:6 now
where the time goes in v2:
time: 101 us; the launch traced here: 99.9 us
  waiting for transfers between devices  27.2 us (27%)
  starting transfers between devices  26.1 us (26%)
  local copies, waits for them, and re-layouts  19.2 us (19%)
  Pallas kernels  12.6 us (12%)
  other arithmetic  7.77 us (8%)
  between operations  7.18 us (7%)
    ppermute x2, starting transfers between devices, shifted(): return lax.ppermute(x, 'blocks', [(b, (b + db) % nb) for b in range(nb)])  15.4 us
    ppermute x2, waiting for transfers between devices, shifted(): return lax.ppermute(x, 'blocks', [(b, (b + db) % nb) for b in range(nb)])  13.7 us
    ppermute x3, waiting for transfers between devices, shifted(): return lax.ppermute(x, 'phi', [(q, (q + dp) % nq) for q in range(nq)])  13.5 us
    ppermute x3, starting transfers between devices, shifted(): return lax.ppermute(x, 'phi', [(q, (q + dp) % nq) for q in range(nq)])  10.6 us
    pallas_call x1, Pallas kernels, ct_update(): pl.pallas_call(ct_kernel, out_shape=jax.ShapeDtypeStruct((3, rows, ny, nz...  8.4 us
    pallas_call x1, Pallas kernels, advect(): pl.pallas_call(advect_kernel, out_shape=jax.ShapeDtypeStruct(updated.shap...  4.16 us
    concatenate x1, other arithmetic, body(): jnp.concatenate([low_row[:, None], middle, high_row[:, None]], axis=1)  3.01 us
    unnamed x5, local copies, waits for them, and re-layouts  2.45 us
  transfers between devices with their start and end apart: 5, of which 3 were waited for; matrix products, arithmetic and copies ran while one was open for 6% of the time, Pallas kernels for 0%

profile of v2, /device:TPU:6, one launch (start us, length us, event | category | flops | bytes accessed | tf_op | source)
XLA Modules:
  0.0 99.9 jit_solution(12145289330699889113)
XLA Ops:
  0.0 2.4 %copy_dynamic-update-slice_fusion.1 = f32[6,16,16,512]{3,1,0,2:T(8,128)S(1)} fusion(f32[3,16,16,512]{3,2,1,0:T(8,128)} %param.6), kind=kLoop, calls=%fused_computation.3 | loop fusion | bytes 3145728
  2.5 0.9 copy_dynamic-update-slice_fusion
  3.8 0.7 copy.37
  4.5 13.5 %collective-permute-start.1 = (f32[6,16,512]{2,1,0:T(8,128)}, f32[6,16,512]{2,1,0:T(8,128)S(1)}, u32[]{:S(2)}, u32[]{:S(2)}) collective-permute-start(f32[6,16,512]{2,1,0:T(8,128)} %bitcast.25), channel_id=1, source_target_pairs={{0,508},{4,0},{8,4},{12,8},{16,12},{20,16},{24,20},{28,24},{32,28}... | collective-permute-start | bytes 589832 | tf_op jit(solution)/shard_map/ppermute | solution.py:16
  18.0 0.7 copy.38
  18.7 1.9 %collective-permute-start = (f32[6,16,512]{2,1,0:T(8,128)}, f32[6,16,512]{2,1,0:T(8,128)S(1)}, u32[]{:S(2)}, u32[]{:S(2)}) collective-permute-start(f32[6,16,512]{2,1,0:T(8,128)} %bitcast.26), channel_id=1, source_target_pairs={{0,4},{4,8},{8,12},{12,16},{16,20},{20,24},{24,28},{28,32},{32,36}... | collective-permute-start | bytes 589832 | tf_op jit(solution)/shard_map/ppermute | solution.py:16
  20.7 0.7 slice_bitcast_fusion.3
  21.4 13.7 %collective-permute-done = f32[6,16,512]{2,1,0:T(8,128)S(1)} collective-permute-done((f32[6,16,512]{2,1,0:T(8,128)}, f32[6,16,512]{2,1,0:T(8,128)S(1)}, u32[]{:S(2)}, u32[]{:S(2)}) %collective-permute-start) | collective-permute-done | bytes 196640 | tf_op jit(solution)/shard_map/ppermute | solution.py:16
  35.1 0.6 fusion.6
  35.7 0.8 pad_maximum_fusion.2
  36.5 1.9 %collective-permute-start.2 = (f32[6,26,512]{2,1,0:T(8,128)}, f32[6,26,512]{2,1,0:T(8,128)}, u32[]{:S(2)}, u32[]{:S(2)}) collective-permute-start(f32[6,26,512]{2,1,0:T(8,128)} %pad_maximum_fusion.2), channel_id=1, source_target_pairs={{0,1},{1,2},{2,3},{3,0},{4,5},{5,6},{6,7},{7,4},{8,9},{9,10},{10,1... | collective-permute-start | bytes 958472 | tf_op jit(solution)/shard_map/ppermute | solution.py:18
  38.5 0.6 fusion.8
  44.2 1.7 %pad_maximum_fusion.3 = f32[6,26,512]{2,1,0:T(8,128)} fusion(f32[6,1,512]{2,1,0:T(1,128)} %get-tuple-element.16, f32[6,16,512]{2,1,0:T(8,128)} %get-tuple-element.6, f32[6,1,512]{2,1,0:T(1,128)S(1)} %get-tuple-element.14, f32[6,8,512]{2,1,0:T(8,128)S(1)} %slice.111), kind=kLoop, calls=%fused_computation.5 | loop fusion | flops 239616 | bytes 638976 | tf_op jit(solution)/shard_map/concatenate | solution.py:173
  45.9 5.7 %collective-permute-start.3 = (f32[6,26,512]{2,1,0:T(8,128)}, f32[6,26,512]{2,1,0:T(8,128)}, u32[]{:S(2)}, u32[]{:S(2)}) collective-permute-start(f32[6,26,512]{2,1,0:T(8,128)} %pad_maximum_fusion.3), channel_id=1, source_target_pairs={{0,3},{1,0},{2,1},{3,2},{4,7},{5,4},{6,5},{7,6},{8,11},{9,8},{10,9... | collective-permute-start | bytes 958472 | tf_op jit(solution)/shard_map/ppermute | solution.py:18
  51.7 1.3 %fusion.7 = (f32[1]{0:T(128)}, f32[1]{0:T(128)}) fusion(f32[2]{0:T(128)} %param.11), kind=kLoop, calls=%fused_computation.23 | loop fusion | bytes 16 | tf_op jit(solution)/shard_map/slice | solution.py:184
  54.8 1.0 slice_bitcast_fusion.1
  55.8 1.4 %collective-permute-done.3 = f32[6,26,512]{2,1,0:T(8,128)} collective-permute-done((f32[6,26,512]{2,1,0:T(8,128)}, f32[6,26,512]{2,1,0:T(8,128)}, u32[]{:S(2)}, u32[]{:S(2)}) %collective-permute-start.3) | collective-permute-done | bytes 319520 | tf_op jit(solution)/shard_map/ppermute | solution.py:18
  57.3 1.0 slice_bitcast_fusion
  58.2 0.6 pad_maximum_fusion.1
  58.9 2.1 %copy.30 = f32[6,16,18,512]{3,2,1,0:T(8,128)S(1)} copy(f32[6,16,18,512]{3,1,0,2:T(8,128)S(1)} %pad_maximum_fusion.1) | data formatting | bytes 7077888 | tf_op jit(solution)/shard_map/concatenate | solution.py:200
  61.0 1.0 fusion.3
  61.9 0.9 slice.110
  62.8 1.0 fusion.4
  63.8 0.9 slice.120
  64.8 1.5 %fusion = (f32[6,1,18,512]{3,2,1,0:T(8,128)S(1)}, f32[6,1,18,512]{3,2,1,0:T(8,128)S(1)}) fusion(f32[6,1,512]{2,1,0:T(1,128)S(1)} %get-tuple-element.11, f32[6,16,512]{2,1,0:T(8,128)S(1)} %collective-permute-done, f32[6,1,512]{2,1,0:T(1,128)S(1)} %get-tuple-element.9, f32[6,25,512]{2,1,0:T(8,128)S(1)} %pad_maximum_fusion.4, s32[]{:T(128)S(6)} %select_n.28, ...), kind=kLoop, calls=%fused_computation.9 | loop fusion | flops 663552 | bytes 1769506 | tf_op jit(solution)/shard_map/broadcast_in_dim | solution.py:201
  66.3 3.0 %pad_maximum_fusion.p_ref = f32[6,18,18,512]{3,2,1,0:T(8,128)} fusion(f32[6,1,18,512]{3,2,1,0:T(8,128)S(1)} %get-tuple-element.22, f32[6,16,18,512]{3,2,1,0:T(8,128)S(1)} %copy.30, f32[6,1,18,512]{3,2,1,0:T(8,128)S(1)} %get-tuple-element.21), kind=kLoop, calls=%fused_computation | loop fusion | flops 1990656 | bytes 7962624 | tf_op jit(solution)/shard_map/concatenate | solution.py:201
  69.3 8.4 %shard_map.64.u_ref = f32[3,16,16,512]{3,2,1,0:T(8,128)} custom-call(f32[6,18,18,512]{3,2,1,0:T(8,128)} %pad_maximum_fusion.p_ref), custom_call_target="tpu_custom_call" | custom-call | flops 15728640 | bytes 5554176 | tf_op jit(solution)/shard_map/pallas_call | solution.py:108
  77.7 1.2 %slice.122 = f32[3,16,7,512]{3,2,1,0:T(8,128)S(1)} slice(f32[3,16,16,512]{3,2,1,0:T(8,128)} %shard_map.64.u_ref), slice={[0:3], [0:16], [9:16], [0:512]} | slice | bytes 1376256 | tf_op jit(solution)/shard_map/slice | solution.py:204
  79.3 3.0 %collective-permute-start.4 = (f32[3,16,7,512]{3,1,2,0:T(8,128)S(1)}, f32[3,16,7,512]{3,1,2,0:T(8,128)S(1)}, u32[]{:S(2)}, u32[]{:S(2)}) collective-permute-start(f32[3,16,7,512]{3,1,2,0:T(8,128)S(1)} %copy.31), channel_id=1, source_target_pairs={{0,1},{1,2},{2,3},{3,0},{4,5},{5,6},{6,7},{7,4},{8,9},{9,10},{10,1... | collective-permute-start | bytes 2064392 | tf_op jit(solution)/shard_map/ppermute | solution.py:18
  82.4 12.1 %collective-permute-done.4 = f32[3,16,7,512]{3,1,2,0:T(8,128)S(1)} collective-permute-done((f32[3,16,7,512]{3,1,2,0:T(8,128)S(1)}, f32[3,16,7,512]{3,1,2,0:T(8,128)S(1)}, u32[]{:S(2)}, u32[]{:S(2)}) %collective-permute-start.4) | collective-permute-done | bytes 688160 | tf_op jit(solution)/shard_map/ppermute | solution.py:18
  94.4 1.3 %copy.32.rec_ref = f32[3,16,7,512]{3,2,1,0:T(8,128)} copy(f32[3,16,7,512]{3,1,2,0:T(8,128)S(1)} %collective-permute-done.4) | data formatting | bytes 1376256 | tf_op jit(solution)/shard_map/ppermute | solution.py:18
  95.7 4.2 %shard_map.65 = f32[3,16,16,512]{3,2,1,0:T(8,128)} custom-call(s32[16]{0:T(128)} %shift_ref.1, f32[16]{0:T(128)} %frac_ref.1, f32[3,16,16,512]{3,2,1,0:T(8,128)} %shard_map.64.u_ref, f32[3,16,7,512]{3,2,1,0:T(8,128)} %copy.32.rec_ref), custom_call_target="tpu_custom_call" | custom-call | flops 1179648 | bytes 3833856 | tf_op jit(solution)/shard_map/pallas_call | solution.py:149
  (13 shorter events, 0.9 us)
Async XLA Ops:
  0.0 2.4 %copy-start = (f32[3,16,16,512]{3,2,1,0:T(8,128)S(1)}, f32[3,16,16,512]{3,2,1,0:T(8,128)}, u32[]{:S(2)}) copy-start(f32[3,16,16,512]{3,2,1,0:T(8,128)} %param.7) | copy-start | bytes 4718596
  2.5 36.0 %copy-start.1 = (s32[2]{0:T(128)S(1)}, s32[2]{0:T(128)}, u32[]{:S(2)}) copy-start(s32[2]{0:T(128)} %param.10) | copy-start | bytes 28
  4.5 30.6 %collective-permute-start.1 = (f32[6,16,512]{2,1,0:T(8,128)}, f32[6,16,512]{2,1,0:T(8,128)S(1)}, u32[]{:S(2)}, u32[]{:S(2)}) collective-permute-start(f32[6,16,512]{2,1,0:T(8,128)} %bitcast.25), channel_id=1, source_target_pairs={{0,508},{4,0},{8,4},{12,8},{16,12},{20,16},{24,20},{28,24},{32,28}... | collective-permute-start | bytes 589832 | tf_op jit(solution)/shard_map/ppermute | solution.py:16
  18.7 16.3 %collective-permute-start = (f32[6,16,512]{2,1,0:T(8,128)}, f32[6,16,512]{2,1,0:T(8,128)S(1)}, u32[]{:S(2)}, u32[]{:S(2)}) collective-permute-start(f32[6,16,512]{2,1,0:T(8,128)} %bitcast.26), channel_id=1, source_target_pairs={{0,4},{4,8},{8,12},{12,16},{16,20},{20,24},{24,28},{28,32},{32,36}... | collective-permute-start | bytes 589832 | tf_op jit(solution)/shard_map/ppermute | solution.py:16
  36.5 18.3 %collective-permute-start.2 = (f32[6,26,512]{2,1,0:T(8,128)}, f32[6,26,512]{2,1,0:T(8,128)}, u32[]{:S(2)}, u32[]{:S(2)}) collective-permute-start(f32[6,26,512]{2,1,0:T(8,128)} %pad_maximum_fusion.2), channel_id=1, source_target_pairs={{0,1},{1,2},{2,3},{3,0},{4,5},{5,6},{6,7},{7,4},{8,9},{9,10},{10,1... | collective-permute-start | bytes 958472 | tf_op jit(solution)/shard_map/ppermute | solution.py:18
  45.9 11.3 %collective-permute-start.3 = (f32[6,26,512]{2,1,0:T(8,128)}, f32[6,26,512]{2,1,0:T(8,128)}, u32[]{:S(2)}, u32[]{:S(2)}) collective-permute-start(f32[6,26,512]{2,1,0:T(8,128)} %pad_maximum_fusion.3), channel_id=1, source_target_pairs={{0,3},{1,0},{2,1},{3,2},{4,7},{5,4},{6,5},{7,6},{8,11},{9,8},{10,9... | collective-permute-start | bytes 958472 | tf_op jit(solution)/shard_map/ppermute | solution.py:18
  79.3 15.1 %collective-permute-start.4 = (f32[3,16,7,512]{3,1,2,0:T(8,128)S(1)}, f32[3,16,7,512]{3,1,2,0:T(8,128)S(1)}, u32[]{:S(2)}, u32[]{:S(2)}) collective-permute-start(f32[3,16,7,512]{3,1,2,0:T(8,128)S(1)} %copy.31), channel_id=1, source_target_pairs={{0,1},{1,2},{2,3},{3,0},{4,5},{5,6},{6,7},{7,4},{8,9},{9,10},{10,1... | collective-permute-start | bytes 2064392 | tf_op jit(solution)/shard_map/ppermute | solution.py:18

commit v3 on v2

--- a/solution.py
+++ b/solution.py
@@ -32,46 +32,63 @@
     return pltpu.roll(v, v.shape[1] - 1, 1)
 
 
-def ct_kernel(p_ref, u_ref, ez_s, ey_s, ex_s):
+OFF = 7
+
+
+def ct_kernel(f_hbm, v_hbm, low_ref, high_ref, lcol_ref, hcol_ref, u_ref, top_ref,
+              p_ref, ez_s, ey_s, ex_s, sem):
     rows = u_ref.shape[1]
     ny = u_ref.shape[2]
+    copies = [
+        pltpu.make_async_copy(f_hbm, p_ref.at[0:3, 1 : rows + 1, pl.ds(OFF + 1, ny)], sem.at[0]),
+        pltpu.make_async_copy(v_hbm, p_ref.at[3:6, 1 : rows + 1, pl.ds(OFF + 1, ny)], sem.at[1]),
+    ]
+    for c in copies:
+        c.start()
+    p_ref[:, 0, pl.ds(OFF, ny + 2), :] = low_ref[...]
+    p_ref[:, rows + 1, pl.ds(OFF, ny + 2), :] = high_ref[...]
+    for a in range(rows):
+        p_ref[:, a + 1, OFF, :] = lcol_ref[:, WIDE + 1 + a, :]
+        p_ref[:, a + 1, OFF + ny + 1, :] = hcol_ref[:, WIDE + 1 + a, :]
+    for c in copies:
+        c.wait()
 
     def emf_row(a, carry):
-        fx_a = p_ref[0, a, pl.ds(1, ny + 1), :]
-        fx_ab = p_ref[0, a, pl.ds(0, ny + 1), :]
-        fy_a = p_ref[1, a, pl.ds(1, ny + 1), :]
-        fy_m = p_ref[1, a - 1, pl.ds(1, ny + 1), :]
+        fx_a = p_ref[0, a, pl.ds(OFF + 1, ny + 1), :]
+        fx_ab = p_ref[0, a, pl.ds(OFF, ny + 1), :]
+        fy_a = p_ref[1, a, pl.ds(OFF + 1, ny + 1), :]
+        fy_m = p_ref[1, a - 1, pl.ds(OFF + 1, ny + 1), :]
         vx = (
-            p_ref[3, a, pl.ds(1, ny + 1), :]
-            + p_ref[3, a - 1, pl.ds(1, ny + 1), :]
-            + p_ref[3, a, pl.ds(0, ny + 1), :]
-            + p_ref[3, a - 1, pl.ds(0, ny + 1), :]
+            p_ref[3, a, pl.ds(OFF + 1, ny + 1), :]
+            + p_ref[3, a - 1, pl.ds(OFF + 1, ny + 1), :]
+            + p_ref[3, a, pl.ds(OFF, ny + 1), :]
+            + p_ref[3, a - 1, pl.ds(OFF, ny + 1), :]
         )
         vy = (
-            p_ref[4, a, pl.ds(1, ny + 1), :]
-            + p_ref[4, a - 1, pl.ds(1, ny + 1), :]
-            + p_ref[4, a, pl.ds(0, ny + 1), :]
-            + p_ref[4, a - 1, pl.ds(0, ny + 1), :]
+            p_ref[4, a, pl.ds(OFF + 1, ny + 1), :]
+            + p_ref[4, a - 1, pl.ds(OFF + 1, ny + 1), :]
+            + p_ref[4, a, pl.ds(OFF, ny + 1), :]
+            + p_ref[4, a - 1, pl.ds(OFF, ny + 1), :]
         )
         ez = (0.25 * vy) * (0.5 * (fx_a + fx_ab)) - (0.25 * vx) * (0.5 * (fy_a + fy_m))
         ez_s[a - 1, pl.ds(0, ny + 1), :] = ez
 
-        mfx = p_ref[0, a, pl.ds(1, ny), :]
-        mfz = p_ref[2, a, pl.ds(1, ny), :]
-        mfz_m = p_ref[2, a - 1, pl.ds(1, ny), :]
-        pvx = p_ref[3, a, pl.ds(1, ny), :] + p_ref[3, a - 1, pl.ds(1, ny), :]
-        pvz = p_ref[5, a, pl.ds(1, ny), :] + p_ref[5, a - 1, pl.ds(1, ny), :]
+        mfx = p_ref[0, a, pl.ds(OFF + 1, ny), :]
+        mfz = p_ref[2, a, pl.ds(OFF + 1, ny), :]
+        mfz_m = p_ref[2, a - 1, pl.ds(OFF + 1, ny), :]
+        pvx = p_ref[3, a, pl.ds(OFF + 1, ny), :] + p_ref[3, a - 1, pl.ds(OFF + 1, ny), :]
+        pvz = p_ref[5, a, pl.ds(OFF + 1, ny), :] + p_ref[5, a - 1, pl.ds(OFF + 1, ny), :]
         yfx = 0.5 * (mfx + below(mfx))
         yfz = 0.5 * (mfz + mfz_m)
         yvx = 0.25 * (pvx + below(pvx))
         yvz = 0.25 * (pvz + below(pvz))
         ey_s[a - 1] = yvx * yfz - yvz * yfx
 
-        rfy = p_ref[1, a, pl.ds(1, ny + 1), :]
-        rfz = p_ref[2, a, pl.ds(1, ny + 1), :]
-        rfz_b = p_ref[2, a, pl.ds(0, ny + 1), :]
-        cvy = p_ref[4, a, pl.ds(1, ny + 1), :] + p_ref[4, a, pl.ds(0, ny + 1), :]
-        cvz = p_ref[5, a, pl.ds(1, ny + 1), :] + p_ref[5, a, pl.ds(0, ny + 1), :]
+        rfy = p_ref[1, a, pl.ds(OFF + 1, ny + 1), :]
+        rfz = p_ref[2, a, pl.ds(OFF + 1, ny + 1), :]
+        rfz_b = p_ref[2, a, pl.ds(OFF, ny + 1), :]
+        cvy = p_ref[4, a, pl.ds(OFF + 1, ny + 1), :] + p_ref[4, a, pl.ds(OFF, ny + 1), :]
+        cvz = p_ref[5, a, pl.ds(OFF + 1, ny + 1), :] + p_ref[5, a, pl.ds(OFF, ny + 1), :]
         xfy = 0.5 * (rfy + below(rfy))
         xfz = 0.5 * (rfz + rfz_b)
         xvy = 0.25 * (cvy + below(cvy))
@@ -80,6 +97,8 @@
         return carry
 
     lax.fori_loop(1, rows + 2, emf_row, 0)
+
+    keep = KMAX + 1
 
     def update_row(r, carry):
         a = r + 1
@@ -90,42 +109,58 @@
         ey_n = ey_s[r + 1]
         ex_r = ex_s[r, pl.ds(0, ny), :]
         ex_r1 = ex_s[r, pl.ds(1, ny), :]
-        fx = p_ref[0, a, pl.ds(1, ny), :]
-        fy = p_ref[1, a, pl.ds(1, ny), :]
-        fz = p_ref[2, a, pl.ds(1, ny), :]
-        u_ref[0, r] = fx - COURANT * ((ez_r1 - ez_r) - (above(ey_r) - ey_r))
-        u_ref[1, r] = fy - COURANT * ((above(ex_r) - ex_r) - (ez_n - ez_r))
-        u_ref[2, r] = fz - COURANT * ((ey_n - ey_r) - (ex_r1 - ex_r))
+        fx = p_ref[0, a, pl.ds(OFF + 1, ny), :]
+        fy = p_ref[1, a, pl.ds(OFF + 1, ny), :]
+        fz = p_ref[2, a, pl.ds(OFF + 1, ny), :]
+        new = (
+            fx - COURANT * ((ez_r1 - ez_r) - (above(ey_r) - ey_r)),
+            fy - COURANT * ((above(ex_r) - ex_r) - (ez_n - ez_r)),
+            fz - COURANT * ((ey_n - ey_r) - (ex_r1 - ex_r)),
+        )
+        for c in range(3):
+            u_ref[c, r] = new[c]
         return carry
 
     lax.fori_loop(0, rows, update_row, 0)
-
-
-def ct_update(padded):
-    _, px, py, nz = padded.shape
-    rows, ny = px - 2, py - 2
+    for c in range(3):
+        for r in range(rows):
+            top_ref[pl.ds((c * rows + r) * keep, keep), :] = u_ref[c, r, pl.ds(ny - keep, keep), :]
+
+
+def ct_update(field, velocity, low_row, high_row, low_col, high_col):
+    _, rows, ny, nz = field.shape
+    keep = KMAX + 1
     vmem = pl.BlockSpec(memory_space=pltpu.VMEM)
+    hbm = pl.BlockSpec(memory_space=pl.ANY)
     return pl.pallas_call(
         ct_kernel,
-        out_shape=jax.ShapeDtypeStruct((3, rows, ny, nz), padded.dtype),
-        in_specs=[vmem],
-        out_specs=vmem,
+        out_shape=(
+            jax.ShapeDtypeStruct((3, rows, ny, nz), field.dtype),
+            jax.ShapeDtypeStruct((3 * rows * keep, nz), field.dtype),
+        ),
+        in_specs=[hbm, hbm, vmem, vmem, vmem, vmem],
+        out_specs=(vmem, vmem),
         scratch_shapes=[
+            pltpu.VMEM((6, rows + 2, OFF + ny + 2, nz), jnp.float32),
             pltpu.VMEM((rows + 1, ny + 8, nz), jnp.float32),
             pltpu.VMEM((rows + 1, ny, nz), jnp.float32),
             pltpu.VMEM((rows + 1, ny + 8, nz), jnp.float32),
+            pltpu.SemaphoreType.DMA((2,)),
         ],
         cost_estimate=pl.CostEstimate(
             flops=120 * rows * ny * nz, transcendentals=0,
-            bytes_accessed=4 * (6 * px * py + 3 * rows * ny) * nz,
+            bytes_accessed=4 * (6 * rows * ny + 3 * rows * ny) * nz,
         ),
-    )(padded)
+    )(field, velocity, low_row, high_row, low_col, high_col)
 
 
 def advect_kernel(shift_ref, frac_ref, u_ref, rec_ref, o_ref, ext):
     rows, ny = u_ref.shape[1], u_ref.shape[2]
     lead = 8
-    ext[:, :, pl.ds(lead - KMAX - 1, KMAX + 1), :] = rec_ref[...]
+    keep = KMAX + 1
+    for c in range(3):
+        for x in range(rows):
+            ext[c, x, pl.ds(lead - keep, keep), :] = rec_ref[pl.ds((c * rows + x) * keep, keep), :]
     ext[:, :, pl.ds(lead, ny), :] = u_ref[...]
 
     def strip(x, carry):
@@ -160,18 +195,29 @@
 
 
 def body(field, velocity, strip_shift, strip_frac, edge_shift, edge_frac):
-    stacked = jnp.concatenate([field, velocity], axis=0)
-    _, nx, ny, nz = stacked.shape
+    _, nx, ny, nz = field.shape
     nb = lax.axis_size("blocks")
     b = lax.axis_index("blocks")
 
-    xm = shifted(stacked[:, nx - 1], 1, 0)
-    xp = shifted(stacked[:, 0], -1, 0)
+    xm = shifted(jnp.concatenate([field[:, nx - 1], velocity[:, nx - 1]], axis=0), 1, 0)
+    xp = shifted(jnp.concatenate([field[:, 0], velocity[:, 0]], axis=0), -1, 0)
     low_col = jnp.concatenate(
-        [xm[:, ny - WIDE :], xm[:, ny - 1 : ny], stacked[:, :, ny - 1], xp[:, ny - 1 : ny]], axis=1
+        [
+            xm[:, ny - WIDE :],
+            xm[:, ny - 1 : ny],
+            jnp.concatenate([field[:, :, ny - 1], velocity[:, :, ny - 1]], axis=0),
+            xp[:, ny - 1 : ny],
+        ],
+        axis=1,
     )
     high_col = jnp.concatenate(
-        [xp[:, :WIDE], xm[:, 0:1], stacked[:, :, 0], xp[:, 0:1]], axis=1
+        [
+            xp[:, :WIDE],
+            xm[:, 0:1],
+            jnp.concatenate([field[:, :, 0], velocity[:, :, 0]], axis=0),
+            xp[:, 0:1],
+        ],
+        axis=1,
     )
     from_low = shifted(low_col, 0, 1)
     from_high = shifted(high_col, 0, -1)
@@ -195,13 +241,8 @@
     high_plain = jnp.concatenate([ym[:, nx + 1 :], xp, yp[:, nx + 1 :]], axis=1)
     high_row = jnp.where(b == nb - 1, high_ghost, high_plain)
 
-    ym = ym[:, 1 : nx + 1]
-    yp = yp[:, 1 : nx + 1]
-    middle = jnp.concatenate([ym[:, :, None], stacked, yp[:, :, None]], axis=2)
-    padded = jnp.concatenate([low_row[:, None], middle, high_row[:, None]], axis=1)
-
-    updated = ct_update(padded)
-    received = shifted(updated[:, :, ny - KMAX - 1 :], 0, 1)
+    updated, top = ct_update(field, velocity, low_row, high_row, from_low, from_high)
+    received = shifted(top, 0, 1)
     return advect(updated, received, strip_shift, strip_frac)
 
 

time: 101 us -> 86.4 us (0.86)
  the two profiles are of different devices: /device:TPU:6 before, /device:TPU:56 now
where the time goes in v3:
time: 86.4 us; the launch traced here: 85.9 us
  waiting for transfers between devices  33.4 us (39%)
  starting transfers between devices  23.1 us (27%)
  Pallas kernels  12.5 us (14%)
  between operations  7.27 us (8%)
  local copies, waits for them, and re-layouts  6.39 us (7%)
  other arithmetic  3.21 us (4%)
    ppermute x3, waiting for transfers between devices, shifted(): return lax.ppermute(x, 'phi', [(q, (q + dp) % nq) for q in range(nq)])  24.2 us
    ppermute x2, starting transfers between devices, shifted(): return lax.ppermute(x, 'blocks', [(b, (b + db) % nb) for b in range(nb)])  13.1 us
    ppermute x3, starting transfers between devices, shifted(): return lax.ppermute(x, 'phi', [(q, (q + dp) % nq) for q in range(nq)])  10 us
    ppermute x2, waiting for transfers between devices, shifted(): return lax.ppermute(x, 'blocks', [(b, (b + db) % nb) for b in range(nb)])  9.21 us
    pallas_call x1, Pallas kernels, ct_update(): pl.pallas_call(ct_kernel, out_shape=(jax.ShapeDtypeStruct((3, rows, ny, n...  8.42 us
    pallas_call x1, Pallas kernels, advect(): pl.pallas_call(advect_kernel, out_shape=jax.ShapeDtypeStruct(updated.shap...  4.13 us
  transfers between devices with their start and end apart: 5, of which 3 were waited for; matrix products, arithmetic and copies ran while one was open for 5% of the time, Pallas kernels for 0%

profile of v3, /device:TPU:56, one launch (start us, length us, event | category | flops | bytes accessed | tf_op | source)
XLA Modules:
  0.0 85.9 jit_solution(6460656206541586281)
XLA Ops:
  0.0 1.1 %slice_bitcast_fusion.2 = (f32[3,16,512]{2,1,0:T(8,128)S(1)}, f32[3,16,512]{2,1,0:T(8,128)S(1)}, f32[3,16,512]{2,1,0:T(8,128)S(1)}, f32[3,16,512]{2,1,0:T(8,128)S(1)}) fusion(f32[3,16,16,512]{3,2,1,0:T(8,128)} %v_hbm.1, f32[3,16,16,512]{3,2,1,0:T(8,128)} %f_hbm.1), kind=kLoop, calls=%fused_computation.14 | loop fusion | bytes 786432 | tf_op jit(solution)/shard_map/squeeze | solution.py:202
  1.1 0.0 copy-start.3
  1.1 11.1 %collective-permute-start.1 = (f32[6,16,512]{2,1,0:T(8,128)S(1)}, f32[6,16,512]{2,1,0:T(8,128)S(1)}, u32[]{:S(2)}, u32[]{:S(2)}) collective-permute-start(f32[6,16,512]{2,1,0:T(8,128)S(1)} %pad_maximum_fusion.5), channel_id=1, source_target_pairs={{0,508},{4,0},{8,4},{12,8},{16,12},{20,16},{24,20},{28,24},{32,28}... | collective-permute-start | bytes 589832 | tf_op jit(solution)/shard_map/ppermute | solution.py:16
  12.3 1.9 %collective-permute-start = (f32[6,16,512]{2,1,0:T(8,128)S(1)}, f32[6,16,512]{2,1,0:T(8,128)S(1)}, u32[]{:S(2)}, u32[]{:S(2)}) collective-permute-start(f32[6,16,512]{2,1,0:T(8,128)S(1)} %pad_maximum_fusion.4), channel_id=1, source_target_pairs={{0,4},{4,8},{8,12},{12,16},{16,20},{20,24},{24,28},{28,32},{32,36}... | collective-permute-start | bytes 589832 | tf_op jit(solution)/shard_map/ppermute | solution.py:16
  14.2 1.6 %fusion = (f32[3,16,1,512]{3,2,1,0:T(1,128)S(1)}, f32[3,16,1,512]{3,2,1,0:T(1,128)S(1)}) fusion(f32[3,16,16,512]{3,2,1,0:T(8,128)} %f_hbm.1), kind=kLoop, calls=%fused_computation.16 | loop fusion | bytes 393216 | tf_op jit(solution)/shard_map/slice | solution.py:208
  15.8 0.0 copy-start.4
  15.8 1.6 %fusion.1 = (f32[3,16,1,512]{3,2,1,0:T(1,128)S(1)}, f32[3,16,1,512]{3,2,1,0:T(1,128)S(1)}) fusion(f32[3,16,16,512]{3,2,1,0:T(8,128)} %v_hbm.1), kind=kLoop, calls=%fused_computation.17 | loop fusion | bytes 393216 | tf_op jit(solution)/shard_map/slice | solution.py:208
  17.4 9.2 %collective-permute-done = f32[6,16,512]{2,1,0:T(8,128)S(1)} collective-permute-done((f32[6,16,512]{2,1,0:T(8,128)S(1)}, f32[6,16,512]{2,1,0:T(8,128)S(1)}, u32[]{:S(2)}, u32[]{:S(2)}) %collective-permute-start) | collective-permute-done | bytes 196640 | tf_op jit(solution)/shard_map/ppermute | solution.py:16
  26.6 0.0 collective-permute-done.1
  26.7 0.1 pad_maximum_fusion
  26.7 2.3 %collective-permute-start.2 = (f32[6,26,512]{2,1,0:T(8,128)S(1)}, f32[6,26,512]{2,1,0:T(8,128)S(1)}, u32[]{:S(2)}, u32[]{:S(2)}) collective-permute-start(f32[6,26,512]{2,1,0:T(8,128)S(1)} %pad_maximum_fusion), channel_id=1, source_target_pairs={{0,1},{1,2},{2,3},{3,0},{4,5},{5,6},{6,7},{7,4},{8,9},{9,10},{10,1... | collective-permute-start | bytes 958472 | tf_op jit(solution)/shard_map/ppermute | solution.py:18
  29.0 0.0 copy-done.3
  29.0 0.6 fusion.7
  34.7 0.1 pad_maximum_fusion.1
  34.8 5.4 %collective-permute-start.3 = (f32[6,26,512]{2,1,0:T(8,128)S(1)}, f32[6,26,512]{2,1,0:T(8,128)S(1)}, u32[]{:S(2)}, u32[]{:S(2)}) collective-permute-start(f32[6,26,512]{2,1,0:T(8,128)S(1)} %pad_maximum_fusion.1), channel_id=1, source_target_pairs={{0,3},{1,0},{2,1},{3,2},{4,7},{5,4},{6,5},{7,6},{8,11},{9,8},{10,9... | collective-permute-start | bytes 958472 | tf_op jit(solution)/shard_map/ppermute | solution.py:18
  40.2 0.0 copy-done.4
  40.2 0.6 fusion.6
  42.7 0.0 collective-permute-done.2.lcol_ref
  42.7 0.0 copy-start.1
  42.8 5.7 %collective-permute-done.3.hcol_ref = f32[6,26,512]{2,1,0:T(8,128)S(1)} collective-permute-done((f32[6,26,512]{2,1,0:T(8,128)S(1)}, f32[6,26,512]{2,1,0:T(8,128)S(1)}, u32[]{:S(2)}, u32[]{:S(2)}) %collective-permute-start.3) | collective-permute-done | bytes 319520 | tf_op jit(solution)/shard_map/ppermute | solution.py:18
  48.5 0.0 copy-start.2
  48.5 0.1 pad_maximum_fusion.3
  48.6 1.5 %maximum_select_fusion.1.high_ref = f32[6,18,512]{2,1,0:T(8,128)} fusion(f32[6,1,512]{2,1,0:T(1,128)S(1)} %get-tuple-element.19, f32[6,16,512]{2,1,0:T(8,128)S(1)} %collective-permute-done.1, f32[6,1,512]{2,1,0:T(1,128)S(1)} %get-tuple-element.17, f32[6,25,512]{2,1,0:T(8,128)S(1)} %pad_maximum_fusion.3, s32[]{:T(128)S(6)} %select_n.32, s32[]{:T(128)S(6)} %select_n.31, ...), kind=kLoop, calls=%fused_computation.5 | loop fusion | flops 331776 | bytes 884753 | tf_op jit(solution)/shard_map/jit(_where)/select_n | solution.py:242
  50.1 1.5 %maximum_select_fusion.low_ref = f32[6,18,512]{2,1,0:T(8,128)} fusion(f32[6,1,512]{2,1,0:T(1,128)S(1)} %get-tuple-element.20, f32[6,16,512]{2,1,0:T(8,128)S(1)} %collective-permute-done, f32[6,1,512]{2,1,0:T(1,128)S(1)} %get-tuple-element.18, f32[6,25,512]{2,1,0:T(8,128)S(1)} %pad_maximum_fusion.2, s32[]{:T(128)S(6)} %select_n.28, s32[]{:T(128)S(6)} %select_n.27, ...), kind=kLoop, calls=%fused_computation.4 | loop fusion | flops 331776 | bytes 884753 | tf_op jit(solution)/shard_map/jit(_where)/select_n | solution.py:234
  51.6 0.0 copy-done.1
  51.6 0.0 copy-done.2
  51.6 8.4 %shard_map.64 = (f32[3,16,16,512]{3,2,1,0:T(8,128)}, f32[336,512]{1,0:T(8,128)}) custom-call(f32[3,16,16,512]{3,2,1,0:T(8,128)} %f_hbm.1, f32[3,16,16,512]{3,2,1,0:T(8,128)} %v_hbm.1, f32[6,18,512]{2,1,0:T(8,128)} %maximum_select_fusion.low_ref, f32[6,18,512]{2,1,0:T(8,128)} %maximum_select_fusion.1.high_ref, f32[6,26,512]{2,1,0:T(8,128)} %copy-done.1, ...), custom_call_target="tpu_custom_call" | custom-call | flops 15728640 | bytes 4718592 | tf_op jit(solution)/shard_map/pallas_call | solution.py:135
  60.0 2.4 %collective-permute-start.4 = (f32[336,512]{1,0:T(8,128)}, f32[336,512]{1,0:T(8,128)S(1)}, u32[]{:S(2)}, u32[]{:S(2)}) collective-permute-start(f32[336,512]{1,0:T(8,128)} %get-tuple-element.8), channel_id=1, source_target_pairs={{0,1},{1,2},{2,3},{3,0},{4,5},{5,6},{6,7},{7,4},{8,9},{9,10},{10,1... | collective-permute-start | bytes 2064392 | tf_op jit(solution)/shard_map/ppermute | solution.py:18
  62.4 18.5 %collective-permute-done.4.rec_ref = f32[336,512]{1,0:T(8,128)S(1)} collective-permute-done((f32[336,512]{1,0:T(8,128)}, f32[336,512]{1,0:T(8,128)S(1)}, u32[]{:S(2)}, u32[]{:S(2)}) %collective-permute-start.4) | collective-permute-done | bytes 688160 | tf_op jit(solution)/shard_map/ppermute | solution.py:18
  80.9 0.0 copy-start
  80.9 0.9 copy-done
  81.8 4.1 %shard_map.65 = f32[3,16,16,512]{3,2,1,0:T(8,128)} custom-call(s32[16]{0:T(128)} %shift_ref.1, f32[16]{0:T(128)} %frac_ref.1, f32[3,16,16,512]{3,2,1,0:T(8,128)} %get-tuple-element.7.u_ref, f32[336,512]{1,0:T(8,128)} %copy-done), custom_call_target="tpu_custom_call" | custom-call | flops 1179648 | bytes 3833856 | tf_op jit(solution)/shard_map/pallas_call | solution.py:184
  (13 shorter events, 0.2 us)
Async XLA Ops:
  1.1 27.9 %copy-start.3 = (s32[2]{0:T(128)S(1)}, s32[2]{0:T(128)}, u32[]{:S(2)}) copy-start(s32[2]{0:T(128)} %param.10) | copy-start | bytes 28
  1.1 25.5 %collective-permute-start.1 = (f32[6,16,512]{2,1,0:T(8,128)S(1)}, f32[6,16,512]{2,1,0:T(8,128)S(1)}, u32[]{:S(2)}, u32[]{:S(2)}) collective-permute-start(f32[6,16,512]{2,1,0:T(8,128)S(1)} %pad_maximum_fusion.5), channel_id=1, source_target_pairs={{0,508},{4,0},{8,4},{12,8},{16,12},{20,16},{24,20},{28,24},{32,28}... | collective-permute-start | bytes 589832 | tf_op jit(solution)/shard_map/ppermute | solution.py:16
  12.3 14.3 %collective-permute-start = (f32[6,16,512]{2,1,0:T(8,128)S(1)}, f32[6,16,512]{2,1,0:T(8,128)S(1)}, u32[]{:S(2)}, u32[]{:S(2)}) collective-permute-start(f32[6,16,512]{2,1,0:T(8,128)S(1)} %pad_maximum_fusion.4), channel_id=1, source_target_pairs={{0,4},{4,8},{8,12},{12,16},{16,20},{20,24},{24,28},{28,32},{32,36}... | collective-permute-start | bytes 589832 | tf_op jit(solution)/shard_map/ppermute | solution.py:16
  15.8 24.4 %copy-start.4 = (f32[2]{0:T(128)S(1)}, f32[2]{0:T(128)}, u32[]{:S(2)}) copy-start(f32[2]{0:T(128)} %param.11) | copy-start | bytes 28
  26.7 16.0 %collective-permute-start.2 = (f32[6,26,512]{2,1,0:T(8,128)S(1)}, f32[6,26,512]{2,1,0:T(8,128)S(1)}, u32[]{:S(2)}, u32[]{:S(2)}) collective-permute-start(f32[6,26,512]{2,1,0:T(8,128)S(1)} %pad_maximum_fusion), channel_id=1, source_target_pairs={{0,1},{1,2},{2,3},{3,0},{4,5},{5,6},{6,7},{7,4},{8,9},{9,10},{10,1... | collective-permute-start | bytes 958472 | tf_op jit(solution)/shard_map/ppermute | solution.py:18
  34.8 13.7 %collective-permute-start.3 = (f32[6,26,512]{2,1,0:T(8,128)S(1)}, f32[6,26,512]{2,1,0:T(8,128)S(1)}, u32[]{:S(2)}, u32[]{:S(2)}) collective-permute-start(f32[6,26,512]{2,1,0:T(8,128)S(1)} %pad_maximum_fusion.1), channel_id=1, source_target_pairs={{0,3},{1,0},{2,1},{3,2},{4,7},{5,4},{6,5},{7,6},{8,11},{9,8},{10,9... | collective-permute-start | bytes 958472 | tf_op jit(solution)/shard_map/ppermute | solution.py:18
  42.7 8.9 %copy-start.1 = (f32[6,26,512]{2,1,0:T(8,128)}, f32[6,26,512]{2,1,0:T(8,128)S(1)}, u32[]{:S(2)}) copy-start(f32[6,26,512]{2,1,0:T(8,128)S(1)} %collective-permute-done.2.lcol_ref) | copy-start | bytes 958468
  48.5 3.1 %copy-start.2 = (f32[6,26,512]{2,1,0:T(8,128)}, f32[6,26,512]{2,1,0:T(8,128)S(1)}, u32[]{:S(2)}) copy-start(f32[6,26,512]{2,1,0:T(8,128)S(1)} %collective-permute-done.3.hcol_ref) | copy-start | bytes 958468
  60.0 20.9 %collective-permute-start.4 = (f32[336,512]{1,0:T(8,128)}, f32[336,512]{1,0:T(8,128)S(1)}, u32[]{:S(2)}, u32[]{:S(2)}) collective-permute-start(f32[336,512]{1,0:T(8,128)} %get-tuple-element.8), channel_id=1, source_target_pairs={{0,1},{1,2},{2,3},{3,0},{4,5},{5,6},{6,7},{7,4},{8,9},{9,10},{10,1... | collective-permute-start | bytes 2064392 | tf_op jit(solution)/shard_map/ppermute | solution.py:18
  80.9 0.9 copy-start

commit v4 on v3

v4 whole, which is shorter than its diff:
```python
import jax
import jax.numpy as jnp
from jax import lax
from jax.experimental import pallas as pl
from jax.experimental.pallas import tpu as pltpu
from jax.sharding import PartitionSpec as P

KMAX = 6
COURANT = 0.4
WIDE = KMAX + 2


def shifted(x, db, dp):
    nb, nq = lax.axis_size("blocks"), lax.axis_size("phi")
    if dp == 0:
        return lax.ppermute(x, "blocks", [(b, (b + db) % nb) for b in range(nb)])
    if db == 0:
        return lax.ppermute(x, "phi", [(q, (q + dp) % nq) for q in range(nq)])
    pairs = [
        (b * nq + q, ((b + db) % nb) * nq + (q + dp) % nq)
        for b in range(nb)
        for q in range(nq)
    ]
    return lax.ppermute(x, ("blocks", "phi"), pairs)


def below(v):
    return pltpu.roll(v, 1, 1)


def above(v):
    return pltpu.roll(v, v.shape[1] - 1, 1)


OFF = 7
LEAD = 8


def assemble(f_hbm, v_hbm, low_ref, high_ref, lcol_ref, hcol_ref, p_ref, sem, y0):
    rows = p_ref.shape[1] - 2
    ny = p_ref.shape[2] - OFF - 2
    cells = ny - y0
    copies = [
        pltpu.make_async_copy(
            f_hbm.at[:, :, pl.ds(y0, cells)], p_ref.at[0:3, 1 : rows + 1, pl.ds(OFF + 1 + y0, cells)], sem.at[0]
        ),
        pltpu.make_async_copy(
            v_hbm.at[:, :, pl.ds(y0, cells)], p_ref.at[3:6, 1 : rows + 1, pl.ds(OFF + 1 + y0, cells)], sem.at[1]
        ),
    ]
    for c in copies:
        c.start()
    p_ref[:, 0, pl.ds(OFF, ny + 2), :] = low_ref[...]
    p_ref[:, rows + 1, pl.ds(OFF, ny + 2), :] = high_ref[...]
    for a in range(rows):
        if lcol_ref is not None:
            p_ref[:, a + 1, OFF, :] = lcol_ref[:, WIDE + 1 + a, :]
        if hcol_ref is not None:
            p_ref[:, a + 1, OFF + ny + 1, :] = hcol_ref[:, WIDE + 1 + a, :]
    for c in copies:
        c.wait()


def ct_window(p_ref, ez_s, ey_s, ex_s, ylo, n, emit):
    rows = p_ref.shape[1] - 2
    hi = OFF + ylo + 1
    lo = OFF + ylo

    def emf_row(a, carry):
        fx_a = p_ref[0, a, pl.ds(hi, n + 1), :]
        fx_ab = p_ref[0, a, pl.ds(lo, n + 1), :]
        fy_a = p_ref[1, a, pl.ds(hi, n + 1), :]
        fy_m = p_ref[1, a - 1, pl.ds(hi, n + 1), :]
        vx = (
            p_ref[3, a, pl.ds(hi, n + 1), :]
            + p_ref[3, a - 1, pl.ds(hi, n + 1), :]
            + p_ref[3, a, pl.ds(lo, n + 1), :]
            + p_ref[3, a - 1, pl.ds(lo, n + 1), :]
        )
        vy = (
            p_ref[4, a, pl.ds(hi, n + 1), :]
            + p_ref[4, a - 1, pl.ds(hi, n + 1), :]
            + p_ref[4, a, pl.ds(lo, n + 1), :]
            + p_ref[4, a - 1, pl.ds(lo, n + 1), :]
        )
        ez = (0.25 * vy) * (0.5 * (fx_a + fx_ab)) - (0.25 * vx) * (0.5 * (fy_a + fy_m))
        ez_s[a - 1, pl.ds(0, n + 1), :] = ez

        mfx = p_ref[0, a, pl.ds(hi, n), :]
        mfz = p_ref[2, a, pl.ds(hi, n), :]
        mfz_m = p_ref[2, a - 1, pl.ds(hi, n), :]
        pvx = p_ref[3, a, pl.ds(hi, n), :] + p_ref[3, a - 1, pl.ds(hi, n), :]
        pvz = p_ref[5, a, pl.ds(hi, n), :] + p_ref[5, a - 1, pl.ds(hi, n), :]
        yfx = 0.5 * (mfx + below(mfx))
        yfz = 0.5 * (mfz + mfz_m)
        yvx = 0.25 * (pvx + below(pvx))
        yvz = 0.25 * (pvz + below(pvz))
        ey_s[a - 1, pl.ds(0, n), :] = yvx * yfz - yvz * yfx

        rfy = p_ref[1, a, pl.ds(hi, n + 1), :]
        rfz = p_ref[2, a, pl.ds(hi, n + 1), :]
        rfz_b = p_ref[2, a, pl.ds(lo, n + 1), :]
        cvy = p_ref[4, a, pl.ds(hi, n + 1), :] + p_ref[4, a, pl.ds(lo, n + 1), :]
        cvz = p_ref[5, a, pl.ds(hi, n + 1), :] + p_ref[5, a, pl.ds(lo, n + 1), :]
        xfy = 0.5 * (rfy + below(rfy))
        xfz = 0.5 * (rfz + rfz_b)
        xvy = 0.25 * (cvy + below(cvy))
        xvz = 0.25 * (cvz + below(cvz))
        ex_s[a - 1, pl.ds(0, n + 1), :] = xvz * xfy - xvy * xfz
        return carry

    lax.fori_loop(1, rows + 2, emf_row, 0)

    def update_row(r, carry):
        a = r + 1
        ez_r = ez_s[r, pl.ds(0, n), :]
        ez_r1 = ez_s[r, pl.ds(1, n), :]
        ez_n = ez_s[r + 1, pl.ds(0, n), :]
        ey_r = ey_s[r, pl.ds(0, n), :]
        ey_n = ey_s[r + 1, pl.ds(0, n), :]
        ex_r = ex_s[r, pl.ds(0, n), :]
        ex_r1 = ex_s[r, pl.ds(1, n), :]
        fx = p_ref[0, a, pl.ds(hi, n), :]
        fy = p_ref[1, a, pl.ds(hi, n), :]
        fz = p_ref[2, a, pl.ds(hi, n), :]
        emit(0, r, fx - COURANT * ((ez_r1 - ez_r) - (above(ey_r) - ey_r)))
        emit(1, r, fy - COURANT * ((above(ex_r) - ex_r) - (ez_n - ez_r)))
        emit(2, r, fz - COURANT * ((ey_n - ey_r) - (ex_r1 - ex_r)))
        return carry

    lax.fori_loop(0, rows, update_row, 0)


def scratch_for(rows, ny, nz):
    return [
        pltpu.VMEM((6, rows + 2, OFF + ny + 2, nz), jnp.float32),
        pltpu.VMEM((rows + 1, ny + 8, nz), jnp.float32),
        pltpu.VMEM((rows + 1, ny + 8, nz), jnp.float32),
        pltpu.VMEM((rows + 1, ny + 8, nz), jnp.float32),
        pltpu.SemaphoreType.DMA((2,)),
    ]


def top_kernel(f_hbm, v_hbm, low_ref, high_ref, hcol_ref, top_ref, p_ref, ez_s, ey_s, ex_s, sem):
    rows, ny = p_ref.shape[1] - 2, p_ref.shape[2] - OFF - 2
    keep = KMAX + 1
    assemble(f_hbm, v_hbm, low_ref, high_ref, None, hcol_ref, p_ref, sem, ny - keep - 1)

    def emit(c, r, value):
        top_ref[c, r] = value

    ct_window(p_ref, ez_s, ey_s, ex_s, ny - keep, keep, emit)


def ct_top(field, velocity, low_row, high_row, high_col):
    _, rows, ny, nz = field.shape
    keep = KMAX + 1
    vmem = pl.BlockSpec(memory_space=pltpu.VMEM)
    hbm = pl.BlockSpec(memory_space=pl.ANY)
    return pl.pallas_call(
        top_kernel,
        out_shape=jax.ShapeDtypeStruct((3, rows, keep, nz), field.dtype),
        in_specs=[hbm, hbm, vmem, vmem, vmem],
        out_specs=vmem,
        scratch_shapes=scratch_for(rows, ny, nz),
        cost_estimate=pl.CostEstimate(
            flops=120 * rows * keep * nz, transcendentals=0,
            bytes_accessed=4 * 9 * rows * keep * nz,
        ),
    )(field, velocity, low_row, high_row, high_col)


def blend(ext, o_ref, x, s, w, start, count):
    for k in range(KMAX + 1):
        @pl.when(s == k)
        def _():
            near = ext[:, x, pl.ds(LEAD + start - k, count), :]
            far = ext[:, x, pl.ds(LEAD + start - k - 1, count), :]
            o_ref[:, x, pl.ds(start, count), :] = (1.0 - w) * near + w * far


def bottom_kernel(shift_ref, frac_ref, f_hbm, v_hbm, low_ref, high_ref, lcol_ref, top_ref,
                  o_ref, low_u_ref, p_ref, ez_s, ey_s, ex_s, sem, ext):
    rows, ny = p_ref.shape[1] - 2, p_ref.shape[2] - OFF - 2
    keep = KMAX + 1
    n = ny - keep
    assemble(f_hbm, v_hbm, low_ref, high_ref, lcol_ref, None, p_ref, sem, 0)

    def emit(c, r, value):
        ext[c, r, pl.ds(LEAD, n), :] = value

    ct_window(p_ref, ez_s, ey_s, ex_s, 0, n, emit)
    ext[:, :, pl.ds(LEAD + n, keep), :] = top_ref[...]
    low_u_ref[...] = ext[:, :, pl.ds(LEAD, LEAD), :]

    def strip(x, carry):
        blend(ext, o_ref, x, shift_ref[x], frac_ref[x], keep, ny - keep)
        return carry

    lax.fori_loop(0, rows, strip, 0)


def ct_bottom(strip_shift, strip_frac, field, velocity, low_row, high_row, low_col, top):
    _, rows, ny, nz = field.shape
    vmem = pl.BlockSpec(memory_space=pltpu.VMEM)
    smem = pl.BlockSpec(memory_space=pltpu.SMEM)
    hbm = pl.BlockSpec(memory_space=pl.ANY)
    keep = KMAX + 1
    return pl.pallas_call(
        bottom_kernel,
        out_shape=(
            jax.ShapeDtypeStruct(field.shape, field.dtype),
            jax.ShapeDtypeStruct((3, rows, LEAD, nz), field.dtype),
        ),
        in_specs=[smem, smem, hbm, hbm, vmem, vmem, vmem, vmem],
        out_specs=(vmem, vmem),
        scratch_shapes=scratch_for(rows, ny, nz) + [pltpu.VMEM((3, rows, LEAD + ny, nz), jnp.float32)],
        cost_estimate=pl.CostEstimate(
            flops=130 * rows * (ny - keep) * nz, transcendentals=0,
            bytes_accessed=4 * 12 * rows * ny * nz,
        ),
    )(strip_shift, strip_frac, field, velocity, low_row, high_row, low_col, top)


def edge_kernel(shift_ref, frac_ref, rec_ref, low_u_ref, part_ref, o_ref, ext):
    rows = low_u_ref.shape[1]
    keep = KMAX + 1
    ext[:, :, pl.ds(LEAD - keep, keep), :] = rec_ref[...]
    ext[:, :, pl.ds(LEAD, LEAD), :] = low_u_ref[...]
    ny = part_ref.shape[2]
    o_ref[:, :, pl.ds(keep, ny - keep), :] = part_ref[:, :, pl.ds(keep, ny - keep), :]

    def strip(x, carry):
        blend(ext, o_ref, x, shift_ref[x], frac_ref[x], 0, keep)
        return carry

    lax.fori_loop(0, rows, strip, 0)


def advect_edge(strip_shift, strip_frac, received, low_u, partial):
    _, rows, ny, nz = partial.shape
    vmem = pl.BlockSpec(memory_space=pltpu.VMEM)
    smem = pl.BlockSpec(memory_space=pltpu.SMEM)
    keep = KMAX + 1
    return pl.pallas_call(
        edge_kernel,
        out_shape=jax.ShapeDtypeStruct(partial.shape, partial.dtype),
        in_specs=[smem, smem, vmem, vmem, vmem],
        out_specs=vmem,
        scratch_shapes=[pltpu.VMEM((3, rows, 2 * LEAD, nz), jnp.float32)],
        cost_estimate=pl.CostEstimate(
            flops=9 * rows * keep * nz, transcendentals=0,
            bytes_accessed=4 * 3 * rows * 3 * keep * nz,
        ),
    )(strip_shift, strip_frac, received, low_u, partial)


def body(field, velocity, strip_shift, strip_frac, edge_shift, edge_frac):
    _, nx, ny, nz = field.shape
    nb = lax.axis_size("blocks")
    b = lax.axis_index("blocks")

    xm = shifted(jnp.concatenate([field[:, nx - 1], velocity[:, nx - 1]], axis=0), 1, 0)
    xp = shifted(jnp.concatenate([field[:, 0], velocity[:, 0]], axis=0), -1, 0)
    low_col = jnp.concatenate(
        [
            xm[:, ny - WIDE :],
            xm[:, ny - 1 : ny],
            jnp.concatenate([field[:, :, ny - 1], velocity[:, :, ny - 1]], axis=0),
            xp[:, ny - 1 : ny],
        ],
        axis=1,
    )
    high_col = jnp.concatenate(
        [
            xp[:, :WIDE],
            xm[:, 0:1],
            jnp.concatenate([field[:, :, 0], velocity[:, :, 0]], axis=0),
            xp[:, 0:1],
        ],
        axis=1,
    )
    from_low = shifted(low_col, 0, 1)
    from_high = shifted(high_col, 0, -1)
    ym = from_low[:, WIDE:]
    yp = from_high[:, WIDE:]

    span = ny + 2
    low_line = jnp.concatenate([from_low[:, :WIDE], xm, yp[:, 0:1]], axis=1)
    inner = edge_shift[0]
    low_ghost = (1.0 - edge_frac[0]) * lax.dynamic_slice_in_dim(
        low_line, WIDE - 1 - inner, span, axis=1
    ) + edge_frac[0] * lax.dynamic_slice_in_dim(low_line, WIDE - 2 - inner, span, axis=1)
    low_plain = jnp.concatenate([ym[:, 0:1], xm, yp[:, 0:1]], axis=1)
    low_row = jnp.where(b == 0, low_ghost, low_plain)

    high_line = jnp.concatenate([ym[:, nx + 1 :], xp, from_high[:, :WIDE]], axis=1)
    outer = edge_shift[1]
    high_ghost = (1.0 - edge_frac[1]) * lax.dynamic_slice_in_dim(
        high_line, outer, span, axis=1
    ) + edge_frac[1] * lax.dynamic_slice_in_dim(high_line, outer + 1, span, axis=1)
    high_plain = jnp.concatenate([ym[:, nx + 1 :], xp, yp[:, nx + 1 :]], axis=1)
    high_row = jnp.where(b == nb - 1, high_ghost, high_plain)

    top = ct_top(field, velocity, low_row, high_row, from_high)
    received = shifted(top, 0, 1)
    partial, low_u = ct_bottom(strip_shift, strip_frac, field, velocity, low_row, high_row, from_low, top)
    return advect_edge(strip_shift, strip_frac, received, low_u, partial)


def solution(mesh):
    placed = (
        P(None, "blocks", "phi", None),
        P(None, "blocks", "phi", None),
        P("blocks"),
        P("blocks"),
        P(),
        P(),
    )
    return jax.shard_map(
        body, mesh=mesh, in_specs=placed, out_specs=P(None, "blocks", "phi", None), check_vma=False
    )
```

time: 86.4 us -> 87.6 us (1.014)
  the two profiles are of different devices: /device:TPU:56 before, /device:TPU:1 now
where the time goes in v4:
time: 87.6 us; the launch traced here: 87.1 us
  waiting for transfers between devices  26.6 us (30%)
  starting transfers between devices  21.2 us (24%)
  Pallas kernels  20.3 us (23%)
  local copies, waits for them, and re-layouts  8.4 us (10%)
  between operations  7.31 us (8%)
  other arithmetic  3.25 us (4%)
    ppermute x3, waiting for transfers between devices, shifted(): return lax.ppermute(x, 'phi', [(q, (q + dp) % nq) for q in range(nq)])  18.5 us
    ppermute x2, starting transfers between devices, shifted(): return lax.ppermute(x, 'blocks', [(b, (b + db) % nb) for b in range(nb)])  13.9 us
    pallas_call x1, Pallas kernels, ct_bottom(): pl.pallas_call(bottom_kernel, out_shape=(jax.ShapeDtypeStruct(field.shape...  9.46 us
    ppermute x2, waiting for transfers between devices, shifted(): return lax.ppermute(x, 'blocks', [(b, (b + db) % nb) for b in range(nb)])  8.08 us
    ppermute x3, starting transfers between devices, shifted(): return lax.ppermute(x, 'phi', [(q, (q + dp) % nq) for q in range(nq)])  7.28 us
    pallas_call x1, Pallas kernels, ct_top(): pl.pallas_call(top_kernel, out_shape=jax.ShapeDtypeStruct((3, rows, keep,...  6.53 us
    pallas_call x1, Pallas kernels, advect_edge(): pl.pallas_call(edge_kernel, out_shape=jax.ShapeDtypeStruct(partial.shape,...  4.28 us
  transfers between devices with their start and end apart: 5, of which 3 were waited for; matrix products, arithmetic and copies ran while one was open for 5% of the time, Pallas kernels for 11%

profile of v4, /device:TPU:1, one launch (start us, length us, event | category | flops | bytes accessed | tf_op | source)
XLA Modules:
  0.0 87.1 jit_solution(10038254654363940298)
XLA Ops:
  0.0 1.1 %slice_bitcast_fusion.2 = (f32[3,16,512]{2,1,0:T(8,128)S(1)}, f32[3,16,512]{2,1,0:T(8,128)S(1)}, f32[3,16,512]{2,1,0:T(8,128)S(1)}, f32[3,16,512]{2,1,0:T(8,128)S(1)}) fusion(f32[3,16,16,512]{3,2,1,0:T(8,128)} %v_hbm.3, f32[3,16,16,512]{3,2,1,0:T(8,128)} %f_hbm.3), kind=kLoop, calls=%fused_computation.14 | loop fusion | bytes 786432 | tf_op jit(solution)/shard_map/squeeze | solution.py:263
  1.1 0.0 copy-start.2
  1.1 12.0 %collective-permute-start = (f32[6,16,512]{2,1,0:T(8,128)S(1)}, f32[6,16,512]{2,1,0:T(8,128)S(1)}, u32[]{:S(2)}, u32[]{:S(2)}) collective-permute-start(f32[6,16,512]{2,1,0:T(8,128)S(1)} %pad_maximum_fusion.4), channel_id=1, source_target_pairs={{0,4},{4,8},{8,12},{12,16},{16,20},{20,24},{24,28},{28,32},{32,36}... | collective-permute-start | bytes 589832 | tf_op jit(solution)/shard_map/ppermute | solution.py:16
  13.2 1.9 %collective-permute-start.1 = (f32[6,16,512]{2,1,0:T(8,128)S(1)}, f32[6,16,512]{2,1,0:T(8,128)S(1)}, u32[]{:S(2)}, u32[]{:S(2)}) collective-permute-start(f32[6,16,512]{2,1,0:T(8,128)S(1)} %pad_maximum_fusion.5), channel_id=1, source_target_pairs={{0,508},{4,0},{8,4},{12,8},{16,12},{20,16},{24,20},{28,24},{32,28}... | collective-permute-start | bytes 589832 | tf_op jit(solution)/shard_map/ppermute | solution.py:16
  15.1 1.6 %fusion.1 = (f32[3,16,1,512]{3,2,1,0:T(1,128)S(1)}, f32[3,16,1,512]{3,2,1,0:T(1,128)S(1)}) fusion(f32[3,16,16,512]{3,2,1,0:T(8,128)} %v_hbm.3), kind=kLoop, calls=%fused_computation.17 | loop fusion | bytes 393216 | tf_op jit(solution)/shard_map/slice | solution.py:269
  16.6 0.0 copy-start.3
  16.7 1.6 %fusion = (f32[3,16,1,512]{3,2,1,0:T(1,128)S(1)}, f32[3,16,1,512]{3,2,1,0:T(1,128)S(1)}) fusion(f32[3,16,16,512]{3,2,1,0:T(8,128)} %f_hbm.3), kind=kLoop, calls=%fused_computation.16 | loop fusion | bytes 393216 | tf_op jit(solution)/shard_map/slice | solution.py:269
  18.3 8.1 %collective-permute-done.1 = f32[6,16,512]{2,1,0:T(8,128)S(1)} collective-permute-done((f32[6,16,512]{2,1,0:T(8,128)S(1)}, f32[6,16,512]{2,1,0:T(8,128)S(1)}, u32[]{:S(2)}, u32[]{:S(2)}) %collective-permute-start.1) | collective-permute-done | bytes 196640 | tf_op jit(solution)/shard_map/ppermute | solution.py:16
  26.4 0.0 collective-permute-done
  26.4 0.1 pad_maximum_fusion.1
  26.5 3.4 %collective-permute-start.3 = (f32[6,26,512]{2,1,0:T(8,128)S(1)}, f32[6,26,512]{2,1,0:T(8,128)S(1)}, u32[]{:S(2)}, u32[]{:S(2)}) collective-permute-start(f32[6,26,512]{2,1,0:T(8,128)S(1)} %pad_maximum_fusion.1), channel_id=1, source_target_pairs={{0,3},{1,0},{2,1},{3,2},{4,7},{5,4},{6,5},{7,6},{8,11},{9,8},{10,9... | collective-permute-start | bytes 958472 | tf_op jit(solution)/shard_map/ppermute | solution.py:18
  29.9 0.0 copy-done.2
  29.9 0.6 fusion.7
  35.6 0.1 pad_maximum_fusion
  35.7 1.9 %collective-permute-start.2 = (f32[6,26,512]{2,1,0:T(8,128)S(1)}, f32[6,26,512]{2,1,0:T(8,128)S(1)}, u32[]{:S(2)}, u32[]{:S(2)}) collective-permute-start(f32[6,26,512]{2,1,0:T(8,128)S(1)} %pad_maximum_fusion), channel_id=1, source_target_pairs={{0,1},{1,2},{2,3},{3,0},{4,5},{5,6},{6,7},{7,4},{8,9},{9,10},{10,1... | collective-permute-start | bytes 958472 | tf_op jit(solution)/shard_map/ppermute | solution.py:18
  37.6 0.0 copy-done.3
  37.6 0.6 fusion.6
  40.3 0.0 collective-permute-done.3.hcol_ref
  40.3 0.0 copy-start
  40.3 9.0 %collective-permute-done.2.lcol_ref = f32[6,26,512]{2,1,0:T(8,128)S(1)} collective-permute-done((f32[6,26,512]{2,1,0:T(8,128)S(1)}, f32[6,26,512]{2,1,0:T(8,128)S(1)}, u32[]{:S(2)}, u32[]{:S(2)}) %collective-permute-start.2) | collective-permute-done | bytes 319520 | tf_op jit(solution)/shard_map/ppermute | solution.py:18
  49.4 0.1 pad_maximum_fusion.3
  49.5 1.6 %maximum_select_fusion.1.high_ref = f32[6,18,512]{2,1,0:T(8,128)} fusion(f32[6,1,512]{2,1,0:T(1,128)S(1)} %get-tuple-element.19, f32[6,16,512]{2,1,0:T(8,128)S(1)} %collective-permute-done.1, f32[6,1,512]{2,1,0:T(1,128)S(1)} %get-tuple-element.17, f32[6,25,512]{2,1,0:T(8,128)S(1)} %pad_maximum_fusion.3, s32[]{:T(128)S(6)} %select_n.32, s32[]{:T(128)S(6)} %select_n.31, ...), kind=kLoop, calls=%fused_computation.5 | loop fusion | flops 331776 | bytes 884753 | tf_op jit(solution)/shard_map/jit(_where)/select_n | solution.py:303
  51.0 1.5 %maximum_select_fusion.low_ref = f32[6,18,512]{2,1,0:T(8,128)} fusion(f32[6,1,512]{2,1,0:T(1,128)S(1)} %get-tuple-element.20, f32[6,16,512]{2,1,0:T(8,128)S(1)} %collective-permute-done, f32[6,1,512]{2,1,0:T(1,128)S(1)} %get-tuple-element.18, f32[6,25,512]{2,1,0:T(8,128)S(1)} %pad_maximum_fusion.2, s32[]{:T(128)S(6)} %select_n.28, s32[]{:T(128)S(6)} %select_n.27, ...), kind=kLoop, calls=%fused_computation.4 | loop fusion | flops 331776 | bytes 884753 | tf_op jit(solution)/shard_map/jit(_where)/select_n | solution.py:295
  52.5 0.0 copy-done
  52.5 0.0 copy-done.1
  52.5 6.5 %shard_map.64.top_ref = f32[3,16,7,512]{3,2,1,0:T(8,128)} custom-call(f32[3,16,16,512]{3,2,1,0:T(8,128)} %f_hbm.3, f32[3,16,16,512]{3,2,1,0:T(8,128)} %v_hbm.3, f32[6,18,512]{2,1,0:T(8,128)} %maximum_select_fusion.low_ref, f32[6,18,512]{2,1,0:T(8,128)} %maximum_select_fusion.1.high_ref, f32[6,26,512]{2,1,0:T(8,128)} %copy-done), custom_call_target="tpu_custom_call" | custom-call | flops 6881280 | bytes 2064384 | tf_op jit(solution)/shard_map/pallas_call | solution.py:160
  59.0 1.5 %copy.23 = f32[3,16,7,512]{3,1,2,0:T(8,128)S(1)} copy(f32[3,16,7,512]{3,2,1,0:T(8,128)} %shard_map.64.top_ref) | data formatting | bytes 1376256 | tf_op jit(solution)/shard_map/pallas_call | solution.py:160
  60.6 1.9 %collective-permute-start.4 = (f32[3,16,7,512]{3,1,2,0:T(8,128)S(1)}, f32[3,16,7,512]{3,1,2,0:T(8,128)S(1)}, u32[]{:S(2)}, u32[]{:S(2)}) collective-permute-start(f32[3,16,7,512]{3,1,2,0:T(8,128)S(1)} %copy.23), channel_id=1, source_target_pairs={{0,1},{1,2},{2,3},{3,0},{4,5},{5,6},{6,7},{7,4},{8,9},{9,10},{10,1... | collective-permute-start | bytes 2064392 | tf_op jit(solution)/shard_map/ppermute | solution.py:18
  62.5 9.5 %shard_map.65 = (f32[3,16,16,512]{3,2,1,0:T(8,128)}, f32[3,16,8,512]{3,2,1,0:T(8,128)}) custom-call(s32[16]{0:T(128)} %shift_ref.3, f32[16]{0:T(128)} %frac_ref.3, f32[3,16,16,512]{3,2,1,0:T(8,128)} %f_hbm.3, f32[3,16,16,512]{3,2,1,0:T(8,128)} %v_hbm.3, f32[6,18,512]{2,1,0:T(8,128)} %maximum_select_fusion.low_ref, ...), custom_call_target="tpu_custom_call" | custom-call | flops 9584640 | bytes 6291456 | tf_op jit(solution)/shard_map/pallas_call | solution.py:209
  72.0 9.5 %collective-permute-done.4 = f32[3,16,7,512]{3,1,2,0:T(8,128)S(1)} collective-permute-done((f32[3,16,7,512]{3,1,2,0:T(8,128)S(1)}, f32[3,16,7,512]{3,1,2,0:T(8,128)S(1)}, u32[]{:S(2)}, u32[]{:S(2)}) %collective-permute-start.4) | collective-permute-done | bytes 688160 | tf_op jit(solution)/shard_map/ppermute | solution.py:18
  81.5 1.3 %copy.24.rec_ref = f32[3,16,7,512]{3,2,1,0:T(8,128)} copy(f32[3,16,7,512]{3,1,2,0:T(8,128)S(1)} %collective-permute-done.4) | data formatting | bytes 1376256 | tf_op jit(solution)/shard_map/ppermute | solution.py:18
  82.8 4.3 %shard_map.66 = f32[3,16,16,512]{3,2,1,0:T(8,128)} custom-call(s32[16]{0:T(128)} %shift_ref.3, f32[16]{0:T(128)} %frac_ref.3, f32[3,16,7,512]{3,2,1,0:T(8,128)} %copy.24.rec_ref, f32[3,16,8,512]{3,2,1,0:T(8,128)} %get-tuple-element.7.low_u_ref, f32[3,16,16,512]{3,2,1,0:T(8,128)} %get-tuple-element.8.part_ref), custom_call_target="tpu_custom_call" | custom-call | flops 516096 | bytes 2064384 | tf_op jit(solution)/shard_map/pallas_call | solution.py:245
  (14 shorter events, 0.2 us)
Async XLA Ops:
  1.1 28.8 %copy-start.2 = (s32[2]{0:T(128)S(1)}, s32[2]{0:T(128)}, u32[]{:S(2)}) copy-start(s32[2]{0:T(128)} %param.10) | copy-start | bytes 28
  1.1 25.3 %collective-permute-start = (f32[6,16,512]{2,1,0:T(8,128)S(1)}, f32[6,16,512]{2,1,0:T(8,128)S(1)}, u32[]{:S(2)}, u32[]{:S(2)}) collective-permute-start(f32[6,16,512]{2,1,0:T(8,128)S(1)} %pad_maximum_fusion.4), channel_id=1, source_target_pairs={{0,4},{4,8},{8,12},{12,16},{16,20},{20,24},{24,28},{28,32},{32,36}... | collective-permute-start | bytes 589832 | tf_op jit(solution)/shard_map/ppermute | solution.py:16
  13.2 13.2 %collective-permute-start.1 = (f32[6,16,512]{2,1,0:T(8,128)S(1)}, f32[6,16,512]{2,1,0:T(8,128)S(1)}, u32[]{:S(2)}, u32[]{:S(2)}) collective-permute-start(f32[6,16,512]{2,1,0:T(8,128)S(1)} %pad_maximum_fusion.5), channel_id=1, source_target_pairs={{0,508},{4,0},{8,4},{12,8},{16,12},{20,16},{24,20},{28,24},{32,28}... | collective-permute-start | bytes 589832 | tf_op jit(solution)/shard_map/ppermute | solution.py:16
  16.6 21.0 %copy-start.3 = (f32[2]{0:T(128)S(1)}, f32[2]{0:T(128)}, u32[]{:S(2)}) copy-start(f32[2]{0:T(128)} %param.11) | copy-start | bytes 28
  26.5 13.8 %collective-permute-start.3 = (f32[6,26,512]{2,1,0:T(8,128)S(1)}, f32[6,26,512]{2,1,0:T(8,128)S(1)}, u32[]{:S(2)}, u32[]{:S(2)}) collective-permute-start(f32[6,26,512]{2,1,0:T(8,128)S(1)} %pad_maximum_fusion.1), channel_id=1, source_target_pairs={{0,3},{1,0},{2,1},{3,2},{4,7},{5,4},{6,5},{7,6},{8,11},{9,8},{10,9... | collective-permute-start | bytes 958472 | tf_op jit(solution)/shard_map/ppermute | solution.py:18
  35.7 13.6 %collective-permute-start.2 = (f32[6,26,512]{2,1,0:T(8,128)S(1)}, f32[6,26,512]{2,1,0:T(8,128)S(1)}, u32[]{:S(2)}, u32[]{:S(2)}) collective-permute-start(f32[6,26,512]{2,1,0:T(8,128)S(1)} %pad_maximum_fusion), channel_id=1, source_target_pairs={{0,1},{1,2},{2,3},{3,0},{4,5},{5,6},{6,7},{7,4},{8,9},{9,10},{10,1... | collective-permute-start | bytes 958472 | tf_op jit(solution)/shard_map/ppermute | solution.py:18
  40.3 12.2 %copy-start = (f32[6,26,512]{2,1,0:T(8,128)}, f32[6,26,512]{2,1,0:T(8,128)S(1)}, u32[]{:S(2)}) copy-start(f32[6,26,512]{2,1,0:T(8,128)S(1)} %collective-permute-done.3.hcol_ref) | copy-start | bytes 958468
  49.3 3.2 %copy-start.1 = (f32[6,26,512]{2,1,0:T(8,128)}, f32[6,26,512]{2,1,0:T(8,128)S(1)}, u32[]{:S(2)}) copy-start(f32[6,26,512]{2,1,0:T(8,128)S(1)} %collective-permute-done.2.lcol_ref) | copy-start | bytes 958468
  60.6 20.9 %collective-permute-start.4 = (f32[3,16,7,512]{3,1,2,0:T(8,128)S(1)}, f32[3,16,7,512]{3,1,2,0:T(8,128)S(1)}, u32[]{:S(2)}, u32[]{:S(2)}) collective-permute-start(f32[3,16,7,512]{3,1,2,0:T(8,128)S(1)} %copy.23), channel_id=1, source_target_pairs={{0,1},{1,2},{2,3},{3,0},{4,5},{5,6},{6,7},{7,4},{8,9},{9,10},{10,1... | collective-permute-start | bytes 2064392 | tf_op jit(solution)/shard_map/ppermute | solution.py:18

commit v5 on v3

--- a/solution.py
+++ b/solution.py
@@ -35,8 +35,22 @@
 OFF = 7
 
 
-def ct_kernel(f_hbm, v_hbm, low_ref, high_ref, lcol_ref, hcol_ref, u_ref, top_ref,
-              p_ref, ez_s, ey_s, ex_s, sem):
+def edge_row(dst, line, plain, ghost_on, shift, weight, base, sign):
+    span = dst.shape[1]
+
+    @pl.when(ghost_on == 0)
+    def _():
+        dst[...] = plain
+
+    for k in range(KMAX + 1):
+        @pl.when(jnp.logical_and(ghost_on != 0, shift == k))
+        def _():
+            lead = base + sign * k
+            dst[...] = (1.0 - weight) * line[:, pl.ds(lead, span), :] + weight * line[:, pl.ds(lead + sign, span), :]
+
+
+def ct_kernel(eshift_ref, efrac_ref, flag_ref, f_hbm, v_hbm, xm_ref, xp_ref, lcol_ref, hcol_ref,
+              u_ref, top_ref, p_ref, ez_s, ey_s, ex_s, line, sem):
     rows = u_ref.shape[1]
     ny = u_ref.shape[2]
     copies = [
@@ -45,11 +59,23 @@
     ]
     for c in copies:
         c.start()
-    p_ref[:, 0, pl.ds(OFF, ny + 2), :] = low_ref[...]
-    p_ref[:, rows + 1, pl.ds(OFF, ny + 2), :] = high_ref[...]
     for a in range(rows):
         p_ref[:, a + 1, OFF, :] = lcol_ref[:, WIDE + 1 + a, :]
         p_ref[:, a + 1, OFF + ny + 1, :] = hcol_ref[:, WIDE + 1 + a, :]
+
+    line[:, pl.ds(0, WIDE), :] = lcol_ref[:, pl.ds(0, WIDE), :]
+    line[:, pl.ds(WIDE, ny), :] = xm_ref[...]
+    line[:, WIDE + ny, :] = hcol_ref[:, WIDE, :]
+    low_plain = line[:, pl.ds(WIDE - 1, ny + 2), :]
+    edge_row(p_ref.at[:, 0, pl.ds(OFF, ny + 2)], line, low_plain, flag_ref[0],
+             eshift_ref[0], efrac_ref[0], WIDE - 1, -1)
+
+    line[:, 0, :] = lcol_ref[:, WIDE + rows + 1, :]
+    line[:, pl.ds(1, ny), :] = xp_ref[...]
+    line[:, pl.ds(ny + 1, WIDE), :] = hcol_ref[:, pl.ds(0, WIDE), :]
+    high_plain = line[:, pl.ds(0, ny + 2), :]
+    edge_row(p_ref.at[:, rows + 1, pl.ds(OFF, ny + 2)], line, high_plain, flag_ref[1],
+             eshift_ref[1], efrac_ref[1], 0, 1)
     for c in copies:
         c.wait()
 
@@ -127,10 +153,11 @@
             top_ref[pl.ds((c * rows + r) * keep, keep), :] = u_ref[c, r, pl.ds(ny - keep, keep), :]
 
 
-def ct_update(field, velocity, low_row, high_row, low_col, high_col):
+def ct_update(eshift, efrac, flags, field, velocity, xm, xp, low_col, high_col):
     _, rows, ny, nz = field.shape
     keep = KMAX + 1
     vmem = pl.BlockSpec(memory_space=pltpu.VMEM)
+    smem = pl.BlockSpec(memory_space=pltpu.SMEM)
     hbm = pl.BlockSpec(memory_space=pl.ANY)
     return pl.pallas_call(
         ct_kernel,
@@ -138,20 +165,21 @@
             jax.ShapeDtypeStruct((3, rows, ny, nz), field.dtype),
             jax.ShapeDtypeStruct((3 * rows * keep, nz), field.dtype),
         ),
-        in_specs=[hbm, hbm, vmem, vmem, vmem, vmem],
+        in_specs=[smem, smem, smem, hbm, hbm, vmem, vmem, vmem, vmem],
         out_specs=(vmem, vmem),
         scratch_shapes=[
             pltpu.VMEM((6, rows + 2, OFF + ny + 2, nz), jnp.float32),
             pltpu.VMEM((rows + 1, ny + 8, nz), jnp.float32),
             pltpu.VMEM((rows + 1, ny, nz), jnp.float32),
             pltpu.VMEM((rows + 1, ny + 8, nz), jnp.float32),
+            pltpu.VMEM((6, ny + WIDE + 8, nz), jnp.float32),
             pltpu.SemaphoreType.DMA((2,)),
         ],
         cost_estimate=pl.CostEstimate(
             flops=120 * rows * ny * nz, transcendentals=0,
             bytes_accessed=4 * (6 * rows * ny + 3 * rows * ny) * nz,
         ),
-    )(field, velocity, low_row, high_row, low_col, high_col)
+    )(eshift, efrac, flags, field, velocity, xm, xp, low_col, high_col)
 
 
 def advect_kernel(shift_ref, frac_ref, u_ref, rec_ref, o_ref, ext):
@@ -221,27 +249,8 @@
     )
     from_low = shifted(low_col, 0, 1)
     from_high = shifted(high_col, 0, -1)
-    ym = from_low[:, WIDE:]
-    yp = from_high[:, WIDE:]
-
-    span = ny + 2
-    low_line = jnp.concatenate([from_low[:, :WIDE], xm, yp[:, 0:1]], axis=1)
-    inner = edge_shift[0]
-    low_ghost = (1.0 - edge_frac[0]) * lax.dynamic_slice_in_dim(
-        low_line, WIDE - 1 - inner, span, axis=1
-    ) + edge_frac[0] * lax.dynamic_slice_in_dim(low_line, WIDE - 2 - inner, span, axis=1)
-    low_plain = jnp.concatenate([ym[:, 0:1], xm, yp[:, 0:1]], axis=1)
-    low_row = jnp.where(b == 0, low_ghost, low_plain)
-
-    high_line = jnp.concatenate([ym[:, nx + 1 :], xp, from_high[:, :WIDE]], axis=1)
-    outer = edge_shift[1]
-    high_ghost = (1.0 - edge_frac[1]) * lax.dynamic_slice_in_dim(
-        high_line, outer, span, axis=1
-    ) + edge_frac[1] * lax.dynamic_slice_in_dim(high_line, outer + 1, span, axis=1)
-    high_plain = jnp.concatenate([ym[:, nx + 1 :], xp, yp[:, nx + 1 :]], axis=1)
-    high_row = jnp.where(b == nb - 1, high_ghost, high_plain)
-
-    updated, top = ct_update(field, velocity, low_row, high_row, from_low, from_high)
+    flags = jnp.stack([b == 0, b == nb - 1]).astype(jnp.int32)
+    updated, top = ct_update(edge_shift, edge_frac, flags, field, velocity, xm, xp, from_low, from_high)
     received = shifted(top, 0, 1)
     return advect(updated, received, strip_shift, strip_frac)
 

time: 86.4 us -> 82.4 us (0.954)
  the two profiles are of different devices: /device:TPU:56 before, /device:TPU:1 now
where the time goes in v5:
time: 82.4 us; the launch traced here: 82 us
  waiting for transfers between devices  40.2 us (49%)
  starting transfers between devices  22.5 us (27%)
  Pallas kernels  12.6 us (15%)
  local copies, waits for them, and re-layouts  5.85 us (7%)
    ppermute x3, waiting for transfers between devices, shifted(): return lax.ppermute(x, 'phi', [(q, (q + dp) % nq) for q in range(nq)])  32.1 us
    ppermute x2, starting transfers between devices, shifted(): return lax.ppermute(x, 'blocks', [(b, (b + db) % nb) for b in range(nb)])  13.9 us
    ppermute x3, starting transfers between devices, shifted(): return lax.ppermute(x, 'phi', [(q, (q + dp) % nq) for q in range(nq)])  8.51 us
    pallas_call x1, Pallas kernels, ct_update(): pl.pallas_call(ct_kernel, out_shape=(jax.ShapeDtypeStruct((3, rows, ny, n...  8.45 us
    ppermute x2, waiting for transfers between devices, shifted(): return lax.ppermute(x, 'blocks', [(b, (b + db) % nb) for b in range(nb)])  8.1 us
    pallas_call x1, Pallas kernels, advect(): pl.pallas_call(advect_kernel, out_shape=jax.ShapeDtypeStruct(updated.shap...  4.16 us
  transfers between devices with their start and end apart: 5, of which 4 were waited for; matrix products, arithmetic and copies ran while one was open for 5% of the time, Pallas kernels for 0%

profile of v5, /device:TPU:1, one launch (start us, length us, event | category | flops | bytes accessed | tf_op | source)
XLA Modules:
  0.0 82.0 jit_solution(17785721602068353194)
XLA Ops:
  0.0 1.1 %slice_bitcast_fusion = (f32[3,16,512]{2,1,0:T(8,128)S(1)}, f32[3,16,512]{2,1,0:T(8,128)S(1)}, f32[3,16,512]{2,1,0:T(8,128)S(1)}, f32[3,16,512]{2,1,0:T(8,128)S(1)}) fusion(f32[3,16,16,512]{3,2,1,0:T(8,128)} %v_hbm.1, f32[3,16,16,512]{3,2,1,0:T(8,128)} %f_hbm.1), kind=kLoop, calls=%fused_computation.8 | loop fusion | bytes 786432 | tf_op jit(solution)/shard_map/squeeze | solution.py:231
  1.1 12.0 %collective-permute-start = (f32[6,16,512]{2,1,0:T(8,128)S(1)}, f32[6,16,512]{2,1,0:T(8,128)S(1)}, u32[]{:S(2)}, u32[]{:S(2)}) collective-permute-start(f32[6,16,512]{2,1,0:T(8,128)S(1)} %pad_maximum_fusion.2), channel_id=1, source_target_pairs={{0,4},{4,8},{8,12},{12,16},{16,20},{20,24},{24,28},{28,32},{32,36}... | collective-permute-start | bytes 589832 | tf_op jit(solution)/shard_map/ppermute | solution.py:16
  13.1 1.9 %collective-permute-start.1 = (f32[6,16,512]{2,1,0:T(8,128)S(1)}, f32[6,16,512]{2,1,0:T(8,128)S(1)}, u32[]{:S(2)}, u32[]{:S(2)}) collective-permute-start(f32[6,16,512]{2,1,0:T(8,128)S(1)} %pad_maximum_fusion.3), channel_id=1, source_target_pairs={{0,508},{4,0},{8,4},{12,8},{16,12},{20,16},{24,20},{28,24},{32,28}... | collective-permute-start | bytes 589832 | tf_op jit(solution)/shard_map/ppermute | solution.py:16
  15.1 1.6 %fusion = (f32[3,16,1,512]{3,2,1,0:T(1,128)S(1)}, f32[3,16,1,512]{3,2,1,0:T(1,128)S(1)}) fusion(f32[3,16,16,512]{3,2,1,0:T(8,128)} %f_hbm.1), kind=kLoop, calls=%fused_computation.13 | loop fusion | bytes 393216 | tf_op jit(solution)/shard_map/slice | solution.py:245
  16.6 1.6 %fusion.1 = (f32[3,16,1,512]{3,2,1,0:T(1,128)S(1)}, f32[3,16,1,512]{3,2,1,0:T(1,128)S(1)}) fusion(f32[3,16,16,512]{3,2,1,0:T(8,128)} %v_hbm.1), kind=kLoop, calls=%fused_computation.14 | loop fusion | bytes 393216 | tf_op jit(solution)/shard_map/slice | solution.py:245
  18.2 8.1 %collective-permute-done.1.xp_ref = f32[6,16,512]{2,1,0:T(8,128)S(1)} collective-permute-done((f32[6,16,512]{2,1,0:T(8,128)S(1)}, f32[6,16,512]{2,1,0:T(8,128)S(1)}, u32[]{:S(2)}, u32[]{:S(2)}) %collective-permute-start.1) | collective-permute-done | bytes 196640 | tf_op jit(solution)/shard_map/ppermute | solution.py:16
  26.3 0.0 copy-start.2
  26.4 0.0 collective-permute-done.xm_ref
  26.4 0.0 copy-start.1
  26.4 0.1 pad_maximum_fusion.1
  26.5 3.4 %collective-permute-start.3 = (f32[6,26,512]{2,1,0:T(8,128)S(1)}, f32[6,26,512]{2,1,0:T(8,128)S(1)}, u32[]{:S(2)}, u32[]{:S(2)}) collective-permute-start(f32[6,26,512]{2,1,0:T(8,128)S(1)} %pad_maximum_fusion.1), channel_id=1, source_target_pairs={{0,3},{1,0},{2,1},{3,2},{4,7},{5,4},{6,5},{7,6},{8,11},{9,8},{10,9... | collective-permute-start | bytes 958472 | tf_op jit(solution)/shard_map/ppermute | solution.py:18
  30.0 0.1 pad_maximum_fusion
  30.0 1.9 %collective-permute-start.2 = (f32[6,26,512]{2,1,0:T(8,128)S(1)}, f32[6,26,512]{2,1,0:T(8,128)S(1)}, u32[]{:S(2)}, u32[]{:S(2)}) collective-permute-start(f32[6,26,512]{2,1,0:T(8,128)S(1)} %pad_maximum_fusion), channel_id=1, source_target_pairs={{0,1},{1,2},{2,3},{3,0},{4,5},{5,6},{6,7},{7,4},{8,9},{9,10},{10,1... | collective-permute-start | bytes 958472 | tf_op jit(solution)/shard_map/ppermute | solution.py:18
  31.9 0.6 add_convert_fusion.flag_ref
  32.5 8.0 %collective-permute-done.3.hcol_ref = f32[6,26,512]{2,1,0:T(8,128)S(1)} collective-permute-done((f32[6,26,512]{2,1,0:T(8,128)S(1)}, f32[6,26,512]{2,1,0:T(8,128)S(1)}, u32[]{:S(2)}, u32[]{:S(2)}) %collective-permute-start.3) | collective-permute-done | bytes 319520 | tf_op jit(solution)/shard_map/ppermute | solution.py:18
  40.5 0.0 copy-start.3
  40.5 6.3 %collective-permute-done.2.lcol_ref = f32[6,26,512]{2,1,0:T(8,128)S(1)} collective-permute-done((f32[6,26,512]{2,1,0:T(8,128)S(1)}, f32[6,26,512]{2,1,0:T(8,128)S(1)}, u32[]{:S(2)}, u32[]{:S(2)}) %collective-permute-start.2) | collective-permute-done | bytes 319520 | tf_op jit(solution)/shard_map/ppermute | solution.py:18
  46.8 0.0 copy-done.2
  46.8 0.0 copy-done.1
  46.8 0.0 copy-done.3
  46.8 0.0 copy-start.4
  46.8 0.7 copy-done.4
  47.5 8.5 %shard_map.64 = (f32[3,16,16,512]{3,2,1,0:T(8,128)}, f32[336,512]{1,0:T(8,128)}) custom-call(s32[2]{0:T(128)} %eshift_ref.1, f32[2]{0:T(128)} %efrac_ref.1, s32[2]{0:T(128)} %add_convert_fusion.flag_ref, f32[3,16,16,512]{3,2,1,0:T(8,128)} %f_hbm.1, f32[3,16,16,512]{3,2,1,0:T(8,128)} %v_hbm.1, f32[6,16,512]{2,1,0:T(8,128)} %copy-done.1, ...), custom_call_target="tpu_custom_call" | custom-call | flops 15728640 | bytes 4718592 | tf_op jit(solution)/shard_map/pallas_call | solution.py:162
  56.0 3.1 %collective-permute-start.4 = (f32[336,512]{1,0:T(8,128)}, f32[336,512]{1,0:T(8,128)S(1)}, u32[]{:S(2)}, u32[]{:S(2)}) collective-permute-start(f32[336,512]{1,0:T(8,128)} %get-tuple-element.8), channel_id=1, source_target_pairs={{0,1},{1,2},{2,3},{3,0},{4,5},{5,6},{6,7},{7,4},{8,9},{9,10},{10,1... | collective-permute-start | bytes 2064392 | tf_op jit(solution)/shard_map/ppermute | solution.py:18
  59.2 17.8 %collective-permute-done.4.rec_ref = f32[336,512]{1,0:T(8,128)S(1)} collective-permute-done((f32[336,512]{1,0:T(8,128)}, f32[336,512]{1,0:T(8,128)S(1)}, u32[]{:S(2)}, u32[]{:S(2)}) %collective-permute-start.4) | collective-permute-done | bytes 688160 | tf_op jit(solution)/shard_map/ppermute | solution.py:18
  77.0 0.0 copy-start
  77.0 0.8 %copy-done = f32[336,512]{1,0:T(8,128)} copy-done((f32[336,512]{1,0:T(8,128)}, f32[336,512]{1,0:T(8,128)S(1)}, u32[]{:S(2)}) %copy-start) | copy-done | bytes 688152
  77.8 4.2 %shard_map.65 = f32[3,16,16,512]{3,2,1,0:T(8,128)} custom-call(s32[16]{0:T(128)} %shift_ref.1, f32[16]{0:T(128)} %frac_ref.1, f32[3,16,16,512]{3,2,1,0:T(8,128)} %get-tuple-element.7.u_ref, f32[336,512]{1,0:T(8,128)} %copy-done), custom_call_target="tpu_custom_call" | custom-call | flops 1179648 | bytes 3833856 | tf_op jit(solution)/shard_map/pallas_call | solution.py:212
  (8 shorter events, 0.1 us)
Async XLA Ops:
  1.1 25.3 %collective-permute-start = (f32[6,16,512]{2,1,0:T(8,128)S(1)}, f32[6,16,512]{2,1,0:T(8,128)S(1)}, u32[]{:S(2)}, u32[]{:S(2)}) collective-permute-start(f32[6,16,512]{2,1,0:T(8,128)S(1)} %pad_maximum_fusion.2), channel_id=1, source_target_pairs={{0,4},{4,8},{8,12},{12,16},{16,20},{20,24},{24,28},{28,32},{32,36}... | collective-permute-start | bytes 589832 | tf_op jit(solution)/shard_map/ppermute | solution.py:16
  13.1 13.2 %collective-permute-start.1 = (f32[6,16,512]{2,1,0:T(8,128)S(1)}, f32[6,16,512]{2,1,0:T(8,128)S(1)}, u32[]{:S(2)}, u32[]{:S(2)}) collective-permute-start(f32[6,16,512]{2,1,0:T(8,128)S(1)} %pad_maximum_fusion.3), channel_id=1, source_target_pairs={{0,508},{4,0},{8,4},{12,8},{16,12},{20,16},{24,20},{28,24},{32,28}... | collective-permute-start | bytes 589832 | tf_op jit(solution)/shard_map/ppermute | solution.py:16
  26.3 20.5 %copy-start.2 = (f32[6,16,512]{2,1,0:T(8,128)}, f32[6,16,512]{2,1,0:T(8,128)S(1)}, u32[]{:S(2)}) copy-start(f32[6,16,512]{2,1,0:T(8,128)S(1)} %collective-permute-done.1.xp_ref) | copy-start | bytes 589828
  26.4 20.4 %copy-start.1 = (f32[6,16,512]{2,1,0:T(8,128)}, f32[6,16,512]{2,1,0:T(8,128)S(1)}, u32[]{:S(2)}) copy-start(f32[6,16,512]{2,1,0:T(8,128)S(1)} %collective-permute-done.xm_ref) | copy-start | bytes 589828
  26.5 14.0 %collective-permute-start.3 = (f32[6,26,512]{2,1,0:T(8,128)S(1)}, f32[6,26,512]{2,1,0:T(8,128)S(1)}, u32[]{:S(2)}, u32[]{:S(2)}) collective-permute-start(f32[6,26,512]{2,1,0:T(8,128)S(1)} %pad_maximum_fusion.1), channel_id=1, source_target_pairs={{0,3},{1,0},{2,1},{3,2},{4,7},{5,4},{6,5},{7,6},{8,11},{9,8},{10,9... | collective-permute-start | bytes 958472 | tf_op jit(solution)/shard_map/ppermute | solution.py:18
  30.0 16.8 %collective-permute-start.2 = (f32[6,26,512]{2,1,0:T(8,128)S(1)}, f32[6,26,512]{2,1,0:T(8,128)S(1)}, u32[]{:S(2)}, u32[]{:S(2)}) collective-permute-start(f32[6,26,512]{2,1,0:T(8,128)S(1)} %pad_maximum_fusion), channel_id=1, source_target_pairs={{0,1},{1,2},{2,3},{3,0},{4,5},{5,6},{6,7},{7,4},{8,9},{9,10},{10,1... | collective-permute-start | bytes 958472 | tf_op jit(solution)/shard_map/ppermute | solution.py:18
  40.5 6.3 %copy-start.3 = (f32[6,26,512]{2,1,0:T(8,128)}, f32[6,26,512]{2,1,0:T(8,128)S(1)}, u32[]{:S(2)}) copy-start(f32[6,26,512]{2,1,0:T(8,128)S(1)} %collective-permute-done.3.hcol_ref) | copy-start | bytes 958468
  46.8 0.7 copy-start.4
  56.0 21.0 %collective-permute-start.4 = (f32[336,512]{1,0:T(8,128)}, f32[336,512]{1,0:T(8,128)S(1)}, u32[]{:S(2)}, u32[]{:S(2)}) collective-permute-start(f32[336,512]{1,0:T(8,128)} %get-tuple-element.8), channel_id=1, source_target_pairs={{0,1},{1,2},{2,3},{3,0},{4,5},{5,6},{6,7},{7,4},{8,9},{9,10},{10,1... | collective-permute-start | bytes 2064392 | tf_op jit(solution)/shard_map/ppermute | solution.py:18
  77.0 0.8 %copy-start = (f32[336,512]{1,0:T(8,128)}, f32[336,512]{1,0:T(8,128)S(1)}, u32[]{:S(2)}) copy-start(f32[336,512]{1,0:T(8,128)S(1)} %collective-permute-done.4.rec_ref) | copy-start | bytes 2064388

commit v6 on v5

--- a/solution.py
+++ b/solution.py
@@ -49,7 +49,7 @@
             dst[...] = (1.0 - weight) * line[:, pl.ds(lead, span), :] + weight * line[:, pl.ds(lead + sign, span), :]
 
 
-def ct_kernel(eshift_ref, efrac_ref, flag_ref, f_hbm, v_hbm, xm_ref, xp_ref, lcol_ref, hcol_ref,
+def ct_kernel(eshift_ref, efrac_ref, flag_ref, f_hbm, v_hbm, xm_ref, xp_ref, lend_ref, lown_ref, hend_ref, hown_ref,
               u_ref, top_ref, p_ref, ez_s, ey_s, ex_s, line, sem):
     rows = u_ref.shape[1]
     ny = u_ref.shape[2]
@@ -60,19 +60,19 @@
     for c in copies:
         c.start()
     for a in range(rows):
-        p_ref[:, a + 1, OFF, :] = lcol_ref[:, WIDE + 1 + a, :]
-        p_ref[:, a + 1, OFF + ny + 1, :] = hcol_ref[:, WIDE + 1 + a, :]
-
-    line[:, pl.ds(0, WIDE), :] = lcol_ref[:, pl.ds(0, WIDE), :]
+        p_ref[:, a + 1, OFF, :] = lown_ref[:, a, :]
+        p_ref[:, a + 1, OFF + ny + 1, :] = hown_ref[:, a, :]
+
+    line[:, pl.ds(0, WIDE), :] = lend_ref[:, pl.ds(0, WIDE), :]
     line[:, pl.ds(WIDE, ny), :] = xm_ref[...]
-    line[:, WIDE + ny, :] = hcol_ref[:, WIDE, :]
+    line[:, WIDE + ny, :] = hend_ref[:, WIDE, :]
     low_plain = line[:, pl.ds(WIDE - 1, ny + 2), :]
     edge_row(p_ref.at[:, 0, pl.ds(OFF, ny + 2)], line, low_plain, flag_ref[0],
              eshift_ref[0], efrac_ref[0], WIDE - 1, -1)
 
-    line[:, 0, :] = lcol_ref[:, WIDE + rows + 1, :]
+    line[:, 0, :] = lend_ref[:, WIDE, :]
     line[:, pl.ds(1, ny), :] = xp_ref[...]
-    line[:, pl.ds(ny + 1, WIDE), :] = hcol_ref[:, pl.ds(0, WIDE), :]
+    line[:, pl.ds(ny + 1, WIDE), :] = hend_ref[:, pl.ds(0, WIDE), :]
     high_plain = line[:, pl.ds(0, ny + 2), :]
     edge_row(p_ref.at[:, rows + 1, pl.ds(OFF, ny + 2)], line, high_plain, flag_ref[1],
              eshift_ref[1], efrac_ref[1], 0, 1)
@@ -153,7 +153,7 @@
             top_ref[pl.ds((c * rows + r) * keep, keep), :] = u_ref[c, r, pl.ds(ny - keep, keep), :]
 
 
-def ct_update(eshift, efrac, flags, field, velocity, xm, xp, low_col, high_col):
+def ct_update(eshift, efrac, flags, field, velocity, xm, xp, low_in, high_in):
     _, rows, ny, nz = field.shape
     keep = KMAX + 1
     vmem = pl.BlockSpec(memory_space=pltpu.VMEM)
@@ -165,7 +165,7 @@
             jax.ShapeDtypeStruct((3, rows, ny, nz), field.dtype),
             jax.ShapeDtypeStruct((3 * rows * keep, nz), field.dtype),
         ),
-        in_specs=[smem, smem, smem, hbm, hbm, vmem, vmem, vmem, vmem],
+        in_specs=[smem, smem, smem, hbm, hbm, vmem, vmem, vmem, vmem, vmem, vmem],
         out_specs=(vmem, vmem),
         scratch_shapes=[
             pltpu.VMEM((6, rows + 2, OFF + ny + 2, nz), jnp.float32),
@@ -179,7 +179,7 @@
             flops=120 * rows * ny * nz, transcendentals=0,
             bytes_accessed=4 * (6 * rows * ny + 3 * rows * ny) * nz,
         ),
-    )(eshift, efrac, flags, field, velocity, xm, xp, low_col, high_col)
+    )(eshift, efrac, flags, field, velocity, xm, xp, *low_in, *high_in)
 
 
 def advect_kernel(shift_ref, frac_ref, u_ref, rec_ref, o_ref, ext):
@@ -229,26 +229,12 @@
 
     xm = shifted(jnp.concatenate([field[:, nx - 1], velocity[:, nx - 1]], axis=0), 1, 0)
     xp = shifted(jnp.concatenate([field[:, 0], velocity[:, 0]], axis=0), -1, 0)
-    low_col = jnp.concatenate(
-        [
-            xm[:, ny - WIDE :],
-            xm[:, ny - 1 : ny],
-            jnp.concatenate([field[:, :, ny - 1], velocity[:, :, ny - 1]], axis=0),
-            xp[:, ny - 1 : ny],
-        ],
-        axis=1,
-    )
-    high_col = jnp.concatenate(
-        [
-            xp[:, :WIDE],
-            xm[:, 0:1],
-            jnp.concatenate([field[:, :, 0], velocity[:, :, 0]], axis=0),
-            xp[:, 0:1],
-        ],
-        axis=1,
-    )
-    from_low = shifted(low_col, 0, 1)
-    from_high = shifted(high_col, 0, -1)
+    own_low = jnp.concatenate([field[:, :, ny - 1], velocity[:, :, ny - 1]], axis=0)
+    own_high = jnp.concatenate([field[:, :, 0], velocity[:, :, 0]], axis=0)
+    low_ends = jnp.concatenate([xm[:, ny - WIDE :], xp[:, ny - 1 : ny]], axis=1)
+    high_ends = jnp.concatenate([xp[:, :WIDE], xm[:, 0:1]], axis=1)
+    from_low = shifted((low_ends, own_low), 0, 1)
+    from_high = shifted((high_ends, own_high), 0, -1)
     flags = jnp.stack([b == 0, b == nb - 1]).astype(jnp.int32)
     updated, top = ct_update(edge_shift, edge_frac, flags, field, velocity, xm, xp, from_low, from_high)
     received = shifted(top, 0, 1)

time: 82.4 us -> 81.7 us (level)
  waiting for transfers between devices: 40.2 us -> 32.7 us
  starting transfers between devices: 22.5 us -> 29.2 us
    ppermute x3 -> x5, starting transfers between devices: 8.51 us -> 16.7 us  [shifted(): return lax.ppermute(x, 'phi', [(q, (q + dp) % nq) for q in range(nq)])]
    ppermute x3 -> x5, waiting for transfers between devices: 32.1 us -> 24.3 us  [shifted(): return lax.ppermute(x, 'phi', [(q, (q + dp) % nq) for q in range(nq)])]
    ppermute x2, starting transfers between devices: 13.9 us -> 12.5 us  [shifted(): return lax.ppermute(x, 'blocks', [(b, (b + db) % nb) for b in range(nb)])]
  transfers between devices with their start and end apart: 5 -> 7, of which waited for: 4 -> 4; matrix products, arithmetic and copies ran while one was open for 5% -> 2% of each run, Pallas kernels for 0% -> 0%
where the time goes in v6:
time: 81.7 us; the launch traced here: 81.2 us
  waiting for transfers between devices  32.7 us (40%)
  starting transfers between devices  29.2 us (36%)
  Pallas kernels  12.6 us (15%)
  local copies, waits for them, and re-layouts  5.77 us (7%)
    ppermute x5, waiting for transfers between devices, shifted(): return lax.ppermute(x, 'phi', [(q, (q + dp) % nq) for q in range(nq)])  24.3 us
    ppermute x5, starting transfers between devices, shifted(): return lax.ppermute(x, 'phi', [(q, (q + dp) % nq) for q in range(nq)])  16.7 us
    ppermute x2, starting transfers between devices, shifted(): return lax.ppermute(x, 'blocks', [(b, (b + db) % nb) for b in range(nb)])  12.5 us
    pallas_call x1, Pallas kernels, ct_update(): pl.pallas_call(ct_kernel, out_shape=(jax.ShapeDtypeStruct((3, rows, ny, n...  8.48 us
    ppermute x2, waiting for transfers between devices, shifted(): return lax.ppermute(x, 'blocks', [(b, (b + db) % nb) for b in range(nb)])  8.36 us
    pallas_call x1, Pallas kernels, advect(): pl.pallas_call(advect_kernel, out_shape=jax.ShapeDtypeStruct(updated.shap...  4.13 us
    slice x2, local copies, waits for them, and re-layouts, body(): own_high = jnp.concatenate([field[:, :, 0], velocity[:, :, 0]], axis=0)  3.1 us
  transfers between devices with their start and end apart: 7, of which 4 were waited for; matrix products, arithmetic and copies ran while one was open for 2% of the time, Pallas kernels for 0%

profile of v6, /device:TPU:1, one launch (start us, length us, event | category | flops | bytes accessed | tf_op | source)
XLA Modules:
  0.0 81.2 jit_solution(5569970851355960039)
XLA Ops:
  0.0 1.6 %fusion = (f32[3,16,1,512]{3,2,1,0:T(1,128)S(1)}, f32[3,16,1,512]{3,2,1,0:T(1,128)S(1)}) fusion(f32[3,16,16,512]{3,2,1,0:T(8,128)} %f_hbm.1), kind=kLoop, calls=%fused_computation.15 | loop fusion | bytes 393216 | tf_op jit(solution)/shard_map/slice | solution.py:233
  1.6 1.6 %fusion.1 = (f32[3,16,1,512]{3,2,1,0:T(1,128)S(1)}, f32[3,16,1,512]{3,2,1,0:T(1,128)S(1)}) fusion(f32[3,16,16,512]{3,2,1,0:T(8,128)} %v_hbm.1), kind=kLoop, calls=%fused_computation.16 | loop fusion | bytes 393216 | tf_op jit(solution)/shard_map/slice | solution.py:233
  3.2 4.8 %collective-permute-start.3 = (f32[6,16,512]{2,1,0:T(8,128)S(1)}, f32[6,16,512]{2,1,0:T(8,128)S(1)}, u32[]{:S(2)}, u32[]{:S(2)}) collective-permute-start(f32[6,16,512]{2,1,0:T(8,128)S(1)} %pad_maximum_fusion.3), channel_id=1, source_target_pairs={{0,1},{1,2},{2,3},{3,0},{4,5},{5,6},{6,7},{7,4},{8,9},{9,10},{10,1... | collective-permute-start | bytes 589832 | tf_op jit(solution)/shard_map/ppermute | solution.py:18
  8.0 1.1 %slice_bitcast_fusion = (f32[3,16,512]{2,1,0:T(8,128)S(1)}, f32[3,16,512]{2,1,0:T(8,128)S(1)}, f32[3,16,512]{2,1,0:T(8,128)S(1)}, f32[3,16,512]{2,1,0:T(8,128)S(1)}) fusion(f32[3,16,16,512]{3,2,1,0:T(8,128)} %v_hbm.1, f32[3,16,16,512]{3,2,1,0:T(8,128)} %f_hbm.1), kind=kLoop, calls=%fused_computation.10 | loop fusion | bytes 786432 | tf_op jit(solution)/shard_map/squeeze | solution.py:231
  9.1 10.6 %collective-permute-start = (f32[6,16,512]{2,1,0:T(8,128)S(1)}, f32[6,16,512]{2,1,0:T(8,128)S(1)}, u32[]{:S(2)}, u32[]{:S(2)}) collective-permute-start(f32[6,16,512]{2,1,0:T(8,128)S(1)} %pad_maximum_fusion), channel_id=1, source_target_pairs={{0,4},{4,8},{8,12},{12,16},{16,20},{20,24},{24,28},{28,32},{32,36}... | collective-permute-start | bytes 589832 | tf_op jit(solution)/shard_map/ppermute | solution.py:16
  19.7 1.9 %collective-permute-start.1 = (f32[6,16,512]{2,1,0:T(8,128)S(1)}, f32[6,16,512]{2,1,0:T(8,128)S(1)}, u32[]{:S(2)}, u32[]{:S(2)}) collective-permute-start(f32[6,16,512]{2,1,0:T(8,128)S(1)} %pad_maximum_fusion.1), channel_id=1, source_target_pairs={{0,508},{4,0},{8,4},{12,8},{16,12},{20,16},{24,20},{28,24},{32,28}... | collective-permute-start | bytes 589832 | tf_op jit(solution)/shard_map/ppermute | solution.py:16
  21.7 4.0 %collective-permute-start.5 = (f32[6,16,512]{2,1,0:T(8,128)S(1)}, f32[6,16,512]{2,1,0:T(8,128)S(1)}, u32[]{:S(2)}, u32[]{:S(2)}) collective-permute-start(f32[6,16,512]{2,1,0:T(8,128)S(1)} %pad_maximum_fusion.5), channel_id=1, source_target_pairs={{0,3},{1,0},{2,1},{3,2},{4,7},{5,4},{6,5},{7,6},{8,11},{9,8},{10,9... | collective-permute-start | bytes 589832 | tf_op jit(solution)/shard_map/ppermute | solution.py:18
  25.7 0.0 collective-permute-done.xm_ref
  25.7 0.0 copy-start.1
  25.7 8.4 %collective-permute-done.1.xp_ref = f32[6,16,512]{2,1,0:T(8,128)S(1)} collective-permute-done((f32[6,16,512]{2,1,0:T(8,128)S(1)}, f32[6,16,512]{2,1,0:T(8,128)S(1)}, u32[]{:S(2)}, u32[]{:S(2)}) %collective-permute-start.1) | collective-permute-done | bytes 196640 | tf_op jit(solution)/shard_map/ppermute | solution.py:16
  34.1 0.0 copy-start.2
  34.1 3.9 %collective-permute-start.4 = (f32[6,9,512]{2,1,0:T(8,128)S(1)}, f32[6,9,512]{2,1,0:T(8,128)S(1)}, u32[]{:S(2)}, u32[]{:S(2)}) collective-permute-start(f32[6,9,512]{2,1,0:T(8,128)S(1)} %pad_maximum_fusion.4), channel_id=1, source_target_pairs={{0,3},{1,0},{2,1},{3,2},{4,7},{5,4},{6,5},{7,6},{8,11},{9,8},{10,9... | collective-permute-start | bytes 331784 | tf_op jit(solution)/shard_map/ppermute | solution.py:18
  38.1 1.9 %collective-permute-start.2 = (f32[6,9,512]{2,1,0:T(8,128)S(1)}, f32[6,9,512]{2,1,0:T(8,128)S(1)}, u32[]{:S(2)}, u32[]{:S(2)}) collective-permute-start(f32[6,9,512]{2,1,0:T(8,128)S(1)} %pad_maximum_fusion.2), channel_id=1, source_target_pairs={{0,1},{1,2},{2,3},{3,0},{4,5},{5,6},{6,7},{7,4},{8,9},{9,10},{10,1... | collective-permute-start | bytes 331784 | tf_op jit(solution)/shard_map/ppermute | solution.py:18
  40.0 0.6 add_convert_fusion.flag_ref
  40.6 0.0 collective-permute-done.3.lown_ref
  40.6 0.0 copy-start.3
  40.6 0.0 collective-permute-done.5.hown_ref
  40.6 0.0 copy-start.4
  40.6 1.4 %collective-permute-done.4.hend_ref = f32[6,9,512]{2,1,0:T(8,128)S(1)} collective-permute-done((f32[6,9,512]{2,1,0:T(8,128)S(1)}, f32[6,9,512]{2,1,0:T(8,128)S(1)}, u32[]{:S(2)}, u32[]{:S(2)}) %collective-permute-start.4) | collective-permute-done | bytes 110624 | tf_op jit(solution)/shard_map/ppermute | solution.py:18
  42.0 4.5 %collective-permute-done.2.lend_ref = f32[6,9,512]{2,1,0:T(8,128)S(1)} collective-permute-done((f32[6,9,512]{2,1,0:T(8,128)S(1)}, f32[6,9,512]{2,1,0:T(8,128)S(1)}, u32[]{:S(2)}, u32[]{:S(2)}) %collective-permute-start.2) | collective-permute-done | bytes 110624 | tf_op jit(solution)/shard_map/ppermute | solution.py:18
  46.6 0.0 copy-done.1
  46.6 0.0 copy-done.2
  46.6 0.0 copy-done.3
  46.6 0.0 copy-done.4
  46.6 0.0 copy-done.5
  46.6 0.0 copy-start.6
  46.6 0.7 copy-done.6
  47.3 8.5 %shard_map.64 = (f32[3,16,16,512]{3,2,1,0:T(8,128)}, f32[336,512]{1,0:T(8,128)}) custom-call(s32[2]{0:T(128)} %eshift_ref.1, f32[2]{0:T(128)} %efrac_ref.1, s32[2]{0:T(128)} %add_convert_fusion.flag_ref, f32[3,16,16,512]{3,2,1,0:T(8,128)} %f_hbm.1, f32[3,16,16,512]{3,2,1,0:T(8,128)} %v_hbm.1, f32[6,16,512]{2,1,0:T(8,128)} %copy-done.1, ...), custom_call_target="tpu_custom_call" | custom-call | flops 15728640 | bytes 4718592 | tf_op jit(solution)/shard_map/pallas_call | solution.py:162
  55.8 2.1 %collective-permute-start.6 = (f32[336,512]{1,0:T(8,128)}, f32[336,512]{1,0:T(8,128)S(1)}, u32[]{:S(2)}, u32[]{:S(2)}) collective-permute-start(f32[336,512]{1,0:T(8,128)} %get-tuple-element.8), channel_id=1, source_target_pairs={{0,1},{1,2},{2,3},{3,0},{4,5},{5,6},{6,7},{7,4},{8,9},{9,10},{10,1... | collective-permute-start | bytes 2064392 | tf_op jit(solution)/shard_map/ppermute | solution.py:18
  57.9 18.4 %collective-permute-done.6.rec_ref = f32[336,512]{1,0:T(8,128)S(1)} collective-permute-done((f32[336,512]{1,0:T(8,128)}, f32[336,512]{1,0:T(8,128)S(1)}, u32[]{:S(2)}, u32[]{:S(2)}) %collective-permute-start.6) | collective-permute-done | bytes 688160 | tf_op jit(solution)/shard_map/ppermute | solution.py:18
  76.3 0.8 %copy-done = f32[336,512]{1,0:T(8,128)} copy-done((f32[336,512]{1,0:T(8,128)}, f32[336,512]{1,0:T(8,128)S(1)}, u32[]{:S(2)}) %copy-start) | copy-done | bytes 688152
  77.1 4.1 %shard_map.65 = f32[3,16,16,512]{3,2,1,0:T(8,128)} custom-call(s32[16]{0:T(128)} %shift_ref.1, f32[16]{0:T(128)} %frac_ref.1, f32[3,16,16,512]{3,2,1,0:T(8,128)} %get-tuple-element.7.u_ref, f32[336,512]{1,0:T(8,128)} %copy-done), custom_call_target="tpu_custom_call" | custom-call | flops 1179648 | bytes 3833856 | tf_op jit(solution)/shard_map/pallas_call | solution.py:212
  (14 shorter events, 0.2 us)
Async XLA Ops:
  3.2 37.5 %collective-permute-start.3 = (f32[6,16,512]{2,1,0:T(8,128)S(1)}, f32[6,16,512]{2,1,0:T(8,128)S(1)}, u32[]{:S(2)}, u32[]{:S(2)}) collective-permute-start(f32[6,16,512]{2,1,0:T(8,128)S(1)} %pad_maximum_fusion.3), channel_id=1, source_target_pairs={{0,1},{1,2},{2,3},{3,0},{4,5},{5,6},{6,7},{7,4},{8,9},{9,10},{10,1... | collective-permute-start | bytes 589832 | tf_op jit(solution)/shard_map/ppermute | solution.py:18
  9.1 16.6 %collective-permute-start = (f32[6,16,512]{2,1,0:T(8,128)S(1)}, f32[6,16,512]{2,1,0:T(8,128)S(1)}, u32[]{:S(2)}, u32[]{:S(2)}) collective-permute-start(f32[6,16,512]{2,1,0:T(8,128)S(1)} %pad_maximum_fusion), channel_id=1, source_target_pairs={{0,4},{4,8},{8,12},{12,16},{16,20},{20,24},{24,28},{28,32},{32,36}... | collective-permute-start | bytes 589832 | tf_op jit(solution)/shard_map/ppermute | solution.py:16
  19.7 14.4 %collective-permute-start.1 = (f32[6,16,512]{2,1,0:T(8,128)S(1)}, f32[6,16,512]{2,1,0:T(8,128)S(1)}, u32[]{:S(2)}, u32[]{:S(2)}) collective-permute-start(f32[6,16,512]{2,1,0:T(8,128)S(1)} %pad_maximum_fusion.1), channel_id=1, source_target_pairs={{0,508},{4,0},{8,4},{12,8},{16,12},{20,16},{24,20},{28,24},{32,28}... | collective-permute-start | bytes 589832 | tf_op jit(solution)/shard_map/ppermute | solution.py:16
  21.7 19.0 %collective-permute-start.5 = (f32[6,16,512]{2,1,0:T(8,128)S(1)}, f32[6,16,512]{2,1,0:T(8,128)S(1)}, u32[]{:S(2)}, u32[]{:S(2)}) collective-permute-start(f32[6,16,512]{2,1,0:T(8,128)S(1)} %pad_maximum_fusion.5), channel_id=1, source_target_pairs={{0,3},{1,0},{2,1},{3,2},{4,7},{5,4},{6,5},{7,6},{8,11},{9,8},{10,9... | collective-permute-start | bytes 589832 | tf_op jit(solution)/shard_map/ppermute | solution.py:18
  25.7 20.9 %copy-start.1 = (f32[6,16,512]{2,1,0:T(8,128)}, f32[6,16,512]{2,1,0:T(8,128)S(1)}, u32[]{:S(2)}) copy-start(f32[6,16,512]{2,1,0:T(8,128)S(1)} %collective-permute-done.xm_ref) | copy-start | bytes 589828
  34.1 12.5 %copy-start.2 = (f32[6,16,512]{2,1,0:T(8,128)}, f32[6,16,512]{2,1,0:T(8,128)S(1)}, u32[]{:S(2)}) copy-start(f32[6,16,512]{2,1,0:T(8,128)S(1)} %collective-permute-done.1.xp_ref) | copy-start | bytes 589828
  34.1 7.9 %collective-permute-start.4 = (f32[6,9,512]{2,1,0:T(8,128)S(1)}, f32[6,9,512]{2,1,0:T(8,128)S(1)}, u32[]{:S(2)}, u32[]{:S(2)}) collective-permute-start(f32[6,9,512]{2,1,0:T(8,128)S(1)} %pad_maximum_fusion.4), channel_id=1, source_target_pairs={{0,3},{1,0},{2,1},{3,2},{4,7},{5,4},{6,5},{7,6},{8,11},{9,8},{10,9... | collective-permute-start | bytes 331784 | tf_op jit(solution)/shard_map/ppermute | solution.py:18
  38.1 8.5 %collective-permute-start.2 = (f32[6,9,512]{2,1,0:T(8,128)S(1)}, f32[6,9,512]{2,1,0:T(8,128)S(1)}, u32[]{:S(2)}, u32[]{:S(2)}) collective-permute-start(f32[6,9,512]{2,1,0:T(8,128)S(1)} %pad_maximum_fusion.2), channel_id=1, source_target_pairs={{0,1},{1,2},{2,3},{3,0},{4,5},{5,6},{6,7},{7,4},{8,9},{9,10},{10,1... | collective-permute-start | bytes 331784 | tf_op jit(solution)/shard_map/ppermute | solution.py:18
  40.6 5.9 %copy-start.3 = (f32[6,16,512]{2,1,0:T(8,128)}, f32[6,16,512]{2,1,0:T(8,128)S(1)}, u32[]{:S(2)}) copy-start(f32[6,16,512]{2,1,0:T(8,128)S(1)} %collective-permute-done.3.lown_ref) | copy-start | bytes 589828
  40.6 5.9 %copy-start.4 = (f32[6,16,512]{2,1,0:T(8,128)}, f32[6,16,512]{2,1,0:T(8,128)S(1)}, u32[]{:S(2)}) copy-start(f32[6,16,512]{2,1,0:T(8,128)S(1)} %collective-permute-done.5.hown_ref) | copy-start | bytes 589828
  42.0 4.6 %copy-start.5 = (f32[6,9,512]{2,1,0:T(8,128)}, f32[6,9,512]{2,1,0:T(8,128)S(1)}, u32[]{:S(2)}) copy-start(f32[6,9,512]{2,1,0:T(8,128)S(1)} %collective-permute-done.4.hend_ref) | copy-start | bytes 331780
  46.6 0.7 copy-start.6
  55.8 20.5 %collective-permute-start.6 = (f32[336,512]{1,0:T(8,128)}, f32[336,512]{1,0:T(8,128)S(1)}, u32[]{:S(2)}, u32[]{:S(2)}) collective-permute-start(f32[336,512]{1,0:T(8,128)} %get-tuple-element.8), channel_id=1, source_target_pairs={{0,1},{1,2},{2,3},{3,0},{4,5},{5,6},{6,7},{7,4},{8,9},{9,10},{10,1... | collective-permute-start | bytes 2064392 | tf_op jit(solution)/shard_map/ppermute | solution.py:18
  76.2 0.8 %copy-start = (f32[336,512]{1,0:T(8,128)}, f32[336,512]{1,0:T(8,128)S(1)}, u32[]{:S(2)}) copy-start(f32[336,512]{1,0:T(8,128)S(1)} %collective-permute-done.6.rec_ref) | copy-start | bytes 2064388

commit v7 on v6

--- a/solution.py
+++ b/solution.py
@@ -80,46 +80,42 @@
         c.wait()
 
     def emf_row(a, carry):
-        fx_a = p_ref[0, a, pl.ds(OFF + 1, ny + 1), :]
-        fx_ab = p_ref[0, a, pl.ds(OFF, ny + 1), :]
-        fy_a = p_ref[1, a, pl.ds(OFF + 1, ny + 1), :]
-        fy_m = p_ref[1, a - 1, pl.ds(OFF + 1, ny + 1), :]
-        vx = (
-            p_ref[3, a, pl.ds(OFF + 1, ny + 1), :]
-            + p_ref[3, a - 1, pl.ds(OFF + 1, ny + 1), :]
-            + p_ref[3, a, pl.ds(OFF, ny + 1), :]
-            + p_ref[3, a - 1, pl.ds(OFF, ny + 1), :]
-        )
-        vy = (
-            p_ref[4, a, pl.ds(OFF + 1, ny + 1), :]
-            + p_ref[4, a - 1, pl.ds(OFF + 1, ny + 1), :]
-            + p_ref[4, a, pl.ds(OFF, ny + 1), :]
-            + p_ref[4, a - 1, pl.ds(OFF, ny + 1), :]
-        )
-        ez = (0.25 * vy) * (0.5 * (fx_a + fx_ab)) - (0.25 * vx) * (0.5 * (fy_a + fy_m))
+        hi, lo, m = pl.ds(OFF + 1, ny + 1), pl.ds(OFF, ny + 1), a - 1
+        fx_hi, fx_lo = p_ref[0, a, hi, :], p_ref[0, a, lo, :]
+        fy_hi, fy_m = p_ref[1, a, hi, :], p_ref[1, m, hi, :]
+        fz_hi, fz_lo, fz_m = p_ref[2, a, hi, :], p_ref[2, a, lo, :], p_ref[2, m, hi, :]
+        vx_hi, vx_lo = p_ref[3, a, hi, :], p_ref[3, a, lo, :]
+        vxm_hi, vxm_lo = p_ref[3, m, hi, :], p_ref[3, m, lo, :]
+        vy_hi, vy_lo = p_ref[4, a, hi, :], p_ref[4, a, lo, :]
+        vym_hi, vym_lo = p_ref[4, m, hi, :], p_ref[4, m, lo, :]
+        vz_hi, vz_lo, vzm_hi = p_ref[5, a, hi, :], p_ref[5, a, lo, :], p_ref[5, m, hi, :]
+
+        pair_x = vx_hi + vxm_hi
+        pair_y = vy_hi + vym_hi
+        vx = pair_x + (vx_lo + vxm_lo)
+        vy = pair_y + (vy_lo + vym_lo)
+        ez = (0.25 * vy) * (0.5 * (fx_hi + fx_lo)) - (0.25 * vx) * (0.5 * (fy_hi + fy_m))
         ez_s[a - 1, pl.ds(0, ny + 1), :] = ez
 
-        mfx = p_ref[0, a, pl.ds(OFF + 1, ny), :]
-        mfz = p_ref[2, a, pl.ds(OFF + 1, ny), :]
-        mfz_m = p_ref[2, a - 1, pl.ds(OFF + 1, ny), :]
-        pvx = p_ref[3, a, pl.ds(OFF + 1, ny), :] + p_ref[3, a - 1, pl.ds(OFF + 1, ny), :]
-        pvz = p_ref[5, a, pl.ds(OFF + 1, ny), :] + p_ref[5, a - 1, pl.ds(OFF + 1, ny), :]
+        mfx = fx_hi[:ny]
+        pvx = pair_x[:ny]
+        pvz = (vz_hi + vzm_hi)[:ny]
         yfx = 0.5 * (mfx + below(mfx))
-        yfz = 0.5 * (mfz + mfz_m)
+        yfz = 0.5 * (fz_hi[:ny] + fz_m[:ny])
         yvx = 0.25 * (pvx + below(pvx))
         yvz = 0.25 * (pvz + below(pvz))
         ey_s[a - 1] = yvx * yfz - yvz * yfx
 
-        rfy = p_ref[1, a, pl.ds(OFF + 1, ny + 1), :]
-        rfz = p_ref[2, a, pl.ds(OFF + 1, ny + 1), :]
-        rfz_b = p_ref[2, a, pl.ds(OFF, ny + 1), :]
-        cvy = p_ref[4, a, pl.ds(OFF + 1, ny + 1), :] + p_ref[4, a, pl.ds(OFF, ny + 1), :]
-        cvz = p_ref[5, a, pl.ds(OFF + 1, ny + 1), :] + p_ref[5, a, pl.ds(OFF, ny + 1), :]
-        xfy = 0.5 * (rfy + below(rfy))
-        xfz = 0.5 * (rfz + rfz_b)
-        xvy = 0.25 * (cvy + below(cvy))
-        xvz = 0.25 * (cvz + below(cvz))
-        ex_s[a - 1, pl.ds(0, ny + 1), :] = xvz * xfy - xvy * xfz
+        @pl.when(a <= rows)
+        def _():
+            cvy = vy_hi + vy_lo
+            cvz = vz_hi + vz_lo
+            xfy = 0.5 * (fy_hi + below(fy_hi))
+            xfz = 0.5 * (fz_hi + fz_lo)
+            xvy = 0.25 * (cvy + below(cvy))
+            xvz = 0.25 * (cvz + below(cvz))
+            ex_s[a - 1, pl.ds(0, ny + 1), :] = xvz * xfy - xvy * xfz
+
         return carry
 
     lax.fori_loop(1, rows + 2, emf_row, 0)

time: 81.7 us -> 83 us (1.016)
  Pallas kernels: 12.6 us -> 13.9 us
    pallas_call x1, Pallas kernels: 8.48 us -> 9.79 us  [ct_update(): pl.pallas_call(ct_kernel, out_shape=(jax.ShapeDtypeStruct((3, rows, ny, n...]
where the time goes in v7:
time: 83 us; the launch traced here: 82.5 us
  waiting for transfers between devices  32.7 us (39%)
  starting transfers between devices  29.2 us (35%)
  Pallas kernels  13.9 us (17%)
  local copies, waits for them, and re-layouts  5.77 us (7%)
    ppermute x5, waiting for transfers between devices, shifted(): return lax.ppermute(x, 'phi', [(q, (q + dp) % nq) for q in range(nq)])  24.3 us
    ppermute x5, starting transfers between devices, shifted(): return lax.ppermute(x, 'phi', [(q, (q + dp) % nq) for q in range(nq)])  16.7 us
    ppermute x2, starting transfers between devices, shifted(): return lax.ppermute(x, 'blocks', [(b, (b + db) % nb) for b in range(nb)])  12.5 us
    pallas_call x1, Pallas kernels, ct_update(): pl.pallas_call(ct_kernel, out_shape=(jax.ShapeDtypeStruct((3, rows, ny, n...  9.79 us
    ppermute x2, waiting for transfers between devices, shifted(): return lax.ppermute(x, 'blocks', [(b, (b + db) % nb) for b in range(nb)])  8.36 us
    pallas_call x1, Pallas kernels, advect(): pl.pallas_call(advect_kernel, out_shape=jax.ShapeDtypeStruct(updated.shap...  4.12 us
    slice x2, local copies, waits for them, and re-layouts, body(): own_high = jnp.concatenate([field[:, :, 0], velocity[:, :, 0]], axis=0)  3.1 us
  transfers between devices with their start and end apart: 7, of which 4 were waited for; matrix products, arithmetic and copies ran while one was open for 2% of the time, Pallas kernels for 0%

profile of v7, /device:TPU:1, one launch (start us, length us, event | category | flops | bytes accessed | tf_op | source)
XLA Modules:
  0.0 82.5 jit_solution(785802880812018514)
XLA Ops:
  0.0 1.6 %fusion = (f32[3,16,1,512]{3,2,1,0:T(1,128)S(1)}, f32[3,16,1,512]{3,2,1,0:T(1,128)S(1)}) fusion(f32[3,16,16,512]{3,2,1,0:T(8,128)} %f_hbm.1), kind=kLoop, calls=%fused_computation.15 | loop fusion | bytes 393216 | tf_op jit(solution)/shard_map/slice | solution.py:229
  1.6 1.6 %fusion.1 = (f32[3,16,1,512]{3,2,1,0:T(1,128)S(1)}, f32[3,16,1,512]{3,2,1,0:T(1,128)S(1)}) fusion(f32[3,16,16,512]{3,2,1,0:T(8,128)} %v_hbm.1), kind=kLoop, calls=%fused_computation.16 | loop fusion | bytes 393216 | tf_op jit(solution)/shard_map/slice | solution.py:229
  3.2 4.8 %collective-permute-start.3 = (f32[6,16,512]{2,1,0:T(8,128)S(1)}, f32[6,16,512]{2,1,0:T(8,128)S(1)}, u32[]{:S(2)}, u32[]{:S(2)}) collective-permute-start(f32[6,16,512]{2,1,0:T(8,128)S(1)} %pad_maximum_fusion.3), channel_id=1, source_target_pairs={{0,1},{1,2},{2,3},{3,0},{4,5},{5,6},{6,7},{7,4},{8,9},{9,10},{10,1... | collective-permute-start | bytes 589832 | tf_op jit(solution)/shard_map/ppermute | solution.py:18
  8.0 1.1 %slice_bitcast_fusion = (f32[3,16,512]{2,1,0:T(8,128)S(1)}, f32[3,16,512]{2,1,0:T(8,128)S(1)}, f32[3,16,512]{2,1,0:T(8,128)S(1)}, f32[3,16,512]{2,1,0:T(8,128)S(1)}) fusion(f32[3,16,16,512]{3,2,1,0:T(8,128)} %v_hbm.1, f32[3,16,16,512]{3,2,1,0:T(8,128)} %f_hbm.1), kind=kLoop, calls=%fused_computation.10 | loop fusion | bytes 786432 | tf_op jit(solution)/shard_map/squeeze | solution.py:227
  9.1 10.6 %collective-permute-start = (f32[6,16,512]{2,1,0:T(8,128)S(1)}, f32[6,16,512]{2,1,0:T(8,128)S(1)}, u32[]{:S(2)}, u32[]{:S(2)}) collective-permute-start(f32[6,16,512]{2,1,0:T(8,128)S(1)} %pad_maximum_fusion), channel_id=1, source_target_pairs={{0,4},{4,8},{8,12},{12,16},{16,20},{20,24},{24,28},{28,32},{32,36}... | collective-permute-start | bytes 589832 | tf_op jit(solution)/shard_map/ppermute | solution.py:16
  19.7 1.9 %collective-permute-start.1 = (f32[6,16,512]{2,1,0:T(8,128)S(1)}, f32[6,16,512]{2,1,0:T(8,128)S(1)}, u32[]{:S(2)}, u32[]{:S(2)}) collective-permute-start(f32[6,16,512]{2,1,0:T(8,128)S(1)} %pad_maximum_fusion.1), channel_id=1, source_target_pairs={{0,508},{4,0},{8,4},{12,8},{16,12},{20,16},{24,20},{28,24},{32,28}... | collective-permute-start | bytes 589832 | tf_op jit(solution)/shard_map/ppermute | solution.py:16
  21.7 4.0 %collective-permute-start.5 = (f32[6,16,512]{2,1,0:T(8,128)S(1)}, f32[6,16,512]{2,1,0:T(8,128)S(1)}, u32[]{:S(2)}, u32[]{:S(2)}) collective-permute-start(f32[6,16,512]{2,1,0:T(8,128)S(1)} %pad_maximum_fusion.5), channel_id=1, source_target_pairs={{0,3},{1,0},{2,1},{3,2},{4,7},{5,4},{6,5},{7,6},{8,11},{9,8},{10,9... | collective-permute-start | bytes 589832 | tf_op jit(solution)/shard_map/ppermute | solution.py:18
  25.7 0.0 collective-permute-done.xm_ref
  25.7 0.0 copy-start.1
  25.7 8.4 %collective-permute-done.1.xp_ref = f32[6,16,512]{2,1,0:T(8,128)S(1)} collective-permute-done((f32[6,16,512]{2,1,0:T(8,128)S(1)}, f32[6,16,512]{2,1,0:T(8,128)S(1)}, u32[]{:S(2)}, u32[]{:S(2)}) %collective-permute-start.1) | collective-permute-done | bytes 196640 | tf_op jit(solution)/shard_map/ppermute | solution.py:16
  34.1 0.0 copy-start.2
  34.1 3.9 %collective-permute-start.4 = (f32[6,9,512]{2,1,0:T(8,128)S(1)}, f32[6,9,512]{2,1,0:T(8,128)S(1)}, u32[]{:S(2)}, u32[]{:S(2)}) collective-permute-start(f32[6,9,512]{2,1,0:T(8,128)S(1)} %pad_maximum_fusion.4), channel_id=1, source_target_pairs={{0,3},{1,0},{2,1},{3,2},{4,7},{5,4},{6,5},{7,6},{8,11},{9,8},{10,9... | collective-permute-start | bytes 331784 | tf_op jit(solution)/shard_map/ppermute | solution.py:18
  38.1 1.9 %collective-permute-start.2 = (f32[6,9,512]{2,1,0:T(8,128)S(1)}, f32[6,9,512]{2,1,0:T(8,128)S(1)}, u32[]{:S(2)}, u32[]{:S(2)}) collective-permute-start(f32[6,9,512]{2,1,0:T(8,128)S(1)} %pad_maximum_fusion.2), channel_id=1, source_target_pairs={{0,1},{1,2},{2,3},{3,0},{4,5},{5,6},{6,7},{7,4},{8,9},{9,10},{10,1... | collective-permute-start | bytes 331784 | tf_op jit(solution)/shard_map/ppermute | solution.py:18
  40.0 0.6 add_convert_fusion.flag_ref
  40.6 0.0 collective-permute-done.3.lown_ref
  40.6 0.0 copy-start.3
  40.6 0.0 collective-permute-done.5.hown_ref
  40.6 0.0 copy-start.4
  40.6 1.4 %collective-permute-done.4.hend_ref = f32[6,9,512]{2,1,0:T(8,128)S(1)} collective-permute-done((f32[6,9,512]{2,1,0:T(8,128)S(1)}, f32[6,9,512]{2,1,0:T(8,128)S(1)}, u32[]{:S(2)}, u32[]{:S(2)}) %collective-permute-start.4) | collective-permute-done | bytes 110624 | tf_op jit(solution)/shard_map/ppermute | solution.py:18
  42.0 4.5 %collective-permute-done.2.lend_ref = f32[6,9,512]{2,1,0:T(8,128)S(1)} collective-permute-done((f32[6,9,512]{2,1,0:T(8,128)S(1)}, f32[6,9,512]{2,1,0:T(8,128)S(1)}, u32[]{:S(2)}, u32[]{:S(2)}) %collective-permute-start.2) | collective-permute-done | bytes 110624 | tf_op jit(solution)/shard_map/ppermute | solution.py:18
  46.6 0.0 copy-done.1
  46.6 0.0 copy-done.2
  46.6 0.0 copy-done.3
  46.6 0.0 copy-done.4
  46.6 0.0 copy-done.5
  46.6 0.0 copy-start.6
  46.6 0.7 copy-done.6
  47.3 9.8 %shard_map.64 = (f32[3,16,16,512]{3,2,1,0:T(8,128)}, f32[336,512]{1,0:T(8,128)}) custom-call(s32[2]{0:T(128)} %eshift_ref.1, f32[2]{0:T(128)} %efrac_ref.1, s32[2]{0:T(128)} %add_convert_fusion.flag_ref, f32[3,16,16,512]{3,2,1,0:T(8,128)} %f_hbm.1, f32[3,16,16,512]{3,2,1,0:T(8,128)} %v_hbm.1, f32[6,16,512]{2,1,0:T(8,128)} %copy-done.1, ...), custom_call_target="tpu_custom_call" | custom-call | flops 15728640 | bytes 4718592 | tf_op jit(solution)/shard_map/pallas_call | solution.py:158
  57.1 2.1 %collective-permute-start.6 = (f32[336,512]{1,0:T(8,128)}, f32[336,512]{1,0:T(8,128)S(1)}, u32[]{:S(2)}, u32[]{:S(2)}) collective-permute-start(f32[336,512]{1,0:T(8,128)} %get-tuple-element.8), channel_id=1, source_target_pairs={{0,1},{1,2},{2,3},{3,0},{4,5},{5,6},{6,7},{7,4},{8,9},{9,10},{10,1... | collective-permute-start | bytes 2064392 | tf_op jit(solution)/shard_map/ppermute | solution.py:18
  59.2 18.4 %collective-permute-done.6.rec_ref = f32[336,512]{1,0:T(8,128)S(1)} collective-permute-done((f32[336,512]{1,0:T(8,128)}, f32[336,512]{1,0:T(8,128)S(1)}, u32[]{:S(2)}, u32[]{:S(2)}) %collective-permute-start.6) | collective-permute-done | bytes 688160 | tf_op jit(solution)/shard_map/ppermute | solution.py:18
  77.6 0.8 %copy-done = f32[336,512]{1,0:T(8,128)} copy-done((f32[336,512]{1,0:T(8,128)}, f32[336,512]{1,0:T(8,128)S(1)}, u32[]{:S(2)}) %copy-start) | copy-done | bytes 688152
  78.4 4.1 %shard_map.65 = f32[3,16,16,512]{3,2,1,0:T(8,128)} custom-call(s32[16]{0:T(128)} %shift_ref.1, f32[16]{0:T(128)} %frac_ref.1, f32[3,16,16,512]{3,2,1,0:T(8,128)} %get-tuple-element.7.u_ref, f32[336,512]{1,0:T(8,128)} %copy-done), custom_call_target="tpu_custom_call" | custom-call | flops 1179648 | bytes 3833856 | tf_op jit(solution)/shard_map/pallas_call | solution.py:208
  (14 shorter events, 0.2 us)
Async XLA Ops:
  3.2 37.5 %collective-permute-start.3 = (f32[6,16,512]{2,1,0:T(8,128)S(1)}, f32[6,16,512]{2,1,0:T(8,128)S(1)}, u32[]{:S(2)}, u32[]{:S(2)}) collective-permute-start(f32[6,16,512]{2,1,0:T(8,128)S(1)} %pad_maximum_fusion.3), channel_id=1, source_target_pairs={{0,1},{1,2},{2,3},{3,0},{4,5},{5,6},{6,7},{7,4},{8,9},{9,10},{10,1... | collective-permute-start | bytes 589832 | tf_op jit(solution)/shard_map/ppermute | solution.py:18
  9.1 16.6 %collective-permute-start = (f32[6,16,512]{2,1,0:T(8,128)S(1)}, f32[6,16,512]{2,1,0:T(8,128)S(1)}, u32[]{:S(2)}, u32[]{:S(2)}) collective-permute-start(f32[6,16,512]{2,1,0:T(8,128)S(1)} %pad_maximum_fusion), channel_id=1, source_target_pairs={{0,4},{4,8},{8,12},{12,16},{16,20},{20,24},{24,28},{28,32},{32,36}... | collective-permute-start | bytes 589832 | tf_op jit(solution)/shard_map/ppermute | solution.py:16
  19.7 14.4 %collective-permute-start.1 = (f32[6,16,512]{2,1,0:T(8,128)S(1)}, f32[6,16,512]{2,1,0:T(8,128)S(1)}, u32[]{:S(2)}, u32[]{:S(2)}) collective-permute-start(f32[6,16,512]{2,1,0:T(8,128)S(1)} %pad_maximum_fusion.1), channel_id=1, source_target_pairs={{0,508},{4,0},{8,4},{12,8},{16,12},{20,16},{24,20},{28,24},{32,28}... | collective-permute-start | bytes 589832 | tf_op jit(solution)/shard_map/ppermute | solution.py:16
  21.7 19.0 %collective-permute-start.5 = (f32[6,16,512]{2,1,0:T(8,128)S(1)}, f32[6,16,512]{2,1,0:T(8,128)S(1)}, u32[]{:S(2)}, u32[]{:S(2)}) collective-permute-start(f32[6,16,512]{2,1,0:T(8,128)S(1)} %pad_maximum_fusion.5), channel_id=1, source_target_pairs={{0,3},{1,0},{2,1},{3,2},{4,7},{5,4},{6,5},{7,6},{8,11},{9,8},{10,9... | collective-permute-start | bytes 589832 | tf_op jit(solution)/shard_map/ppermute | solution.py:18
  25.7 20.9 %copy-start.1 = (f32[6,16,512]{2,1,0:T(8,128)}, f32[6,16,512]{2,1,0:T(8,128)S(1)}, u32[]{:S(2)}) copy-start(f32[6,16,512]{2,1,0:T(8,128)S(1)} %collective-permute-done.xm_ref) | copy-start | bytes 589828
  34.1 12.5 %copy-start.2 = (f32[6,16,512]{2,1,0:T(8,128)}, f32[6,16,512]{2,1,0:T(8,128)S(1)}, u32[]{:S(2)}) copy-start(f32[6,16,512]{2,1,0:T(8,128)S(1)} %collective-permute-done.1.xp_ref) | copy-start | bytes 589828
  34.1 7.9 %collective-permute-start.4 = (f32[6,9,512]{2,1,0:T(8,128)S(1)}, f32[6,9,512]{2,1,0:T(8,128)S(1)}, u32[]{:S(2)}, u32[]{:S(2)}) collective-permute-start(f32[6,9,512]{2,1,0:T(8,128)S(1)} %pad_maximum_fusion.4), channel_id=1, source_target_pairs={{0,3},{1,0},{2,1},{3,2},{4,7},{5,4},{6,5},{7,6},{8,11},{9,8},{10,9... | collective-permute-start | bytes 331784 | tf_op jit(solution)/shard_map/ppermute | solution.py:18
  38.1 8.5 %collective-permute-start.2 = (f32[6,9,512]{2,1,0:T(8,128)S(1)}, f32[6,9,512]{2,1,0:T(8,128)S(1)}, u32[]{:S(2)}, u32[]{:S(2)}) collective-permute-start(f32[6,9,512]{2,1,0:T(8,128)S(1)} %pad_maximum_fusion.2), channel_id=1, source_target_pairs={{0,1},{1,2},{2,3},{3,0},{4,5},{5,6},{6,7},{7,4},{8,9},{9,10},{10,1... | collective-permute-start | bytes 331784 | tf_op jit(solution)/shard_map/ppermute | solution.py:18
  40.6 5.9 %copy-start.3 = (f32[6,16,512]{2,1,0:T(8,128)}, f32[6,16,512]{2,1,0:T(8,128)S(1)}, u32[]{:S(2)}) copy-start(f32[6,16,512]{2,1,0:T(8,128)S(1)} %collective-permute-done.3.lown_ref) | copy-start | bytes 589828
  40.6 5.9 %copy-start.4 = (f32[6,16,512]{2,1,0:T(8,128)}, f32[6,16,512]{2,1,0:T(8,128)S(1)}, u32[]{:S(2)}) copy-start(f32[6,16,512]{2,1,0:T(8,128)S(1)} %collective-permute-done.5.hown_ref) | copy-start | bytes 589828
  42.0 4.6 %copy-start.5 = (f32[6,9,512]{2,1,0:T(8,128)}, f32[6,9,512]{2,1,0:T(8,128)S(1)}, u32[]{:S(2)}) copy-start(f32[6,9,512]{2,1,0:T(8,128)S(1)} %collective-permute-done.4.hend_ref) | copy-start | bytes 331780
  46.6 0.7 copy-start.6
  57.1 20.5 %collective-permute-start.6 = (f32[336,512]{1,0:T(8,128)}, f32[336,512]{1,0:T(8,128)S(1)}, u32[]{:S(2)}, u32[]{:S(2)}) collective-permute-start(f32[336,512]{1,0:T(8,128)} %get-tuple-element.8), channel_id=1, source_target_pairs={{0,1},{1,2},{2,3},{3,0},{4,5},{5,6},{6,7},{7,4},{8,9},{9,10},{10,1... | collective-permute-start | bytes 2064392 | tf_op jit(solution)/shard_map/ppermute | solution.py:18
  77.6 0.8 %copy-start = (f32[336,512]{1,0:T(8,128)}, f32[336,512]{1,0:T(8,128)S(1)}, u32[]{:S(2)}) copy-start(f32[336,512]{1,0:T(8,128)S(1)} %collective-permute-done.6.rec_ref) | copy-start | bytes 2064388

commit v8 on v6

--- a/solution.py
+++ b/solution.py
@@ -182,39 +182,60 @@
     )(eshift, efrac, flags, field, velocity, xm, xp, *low_in, *high_in)
 
 
-def advect_kernel(shift_ref, frac_ref, u_ref, rec_ref, o_ref, ext):
+def advect_kernel(shift_ref, frac_ref, u_ref, rec_hbm, o_ref, flat, ext, sem):
     rows, ny = u_ref.shape[1], u_ref.shape[2]
     lead = 8
     keep = KMAX + 1
-    for c in range(3):
-        for x in range(rows):
-            ext[c, x, pl.ds(lead - keep, keep), :] = rec_ref[pl.ds((c * rows + x) * keep, keep), :]
-    ext[:, :, pl.ds(lead, ny), :] = u_ref[...]
-
-    def strip(x, carry):
+    fetch = pltpu.make_async_copy(rec_hbm, flat, sem.at[0])
+    fetch.start()
+
+    def inner(x, carry):
         s = shift_ref[x]
         w = frac_ref[x]
         for k in range(KMAX + 1):
             @pl.when(s == k)
             def _():
-                near = ext[:, x, pl.ds(lead - k, ny), :]
-                far = ext[:, x, pl.ds(lead - k - 1, ny), :]
-                o_ref[:, x] = (1.0 - w) * near + w * far
-        return carry
-
-    lax.fori_loop(0, rows, strip, 0)
+                near = u_ref[:, x, pl.ds(keep - k, ny - keep), :]
+                far = u_ref[:, x, pl.ds(keep - k - 1, ny - keep), :]
+                o_ref[:, x, pl.ds(keep, ny - keep), :] = (1.0 - w) * near + w * far
+        return carry
+
+    lax.fori_loop(0, rows, inner, 0)
+    ext[:, :, pl.ds(lead, lead), :] = u_ref[:, :, pl.ds(0, lead), :]
+    fetch.wait()
+    for c in range(3):
+        for x in range(rows):
+            ext[c, x, pl.ds(lead - keep, keep), :] = flat[pl.ds((c * rows + x) * keep, keep), :]
+
+    def edge(x, carry):
+        s = shift_ref[x]
+        w = frac_ref[x]
+        for k in range(KMAX + 1):
+            @pl.when(s == k)
+            def _():
+                near = ext[:, x, pl.ds(lead - k, keep), :]
+                far = ext[:, x, pl.ds(lead - k - 1, keep), :]
+                o_ref[:, x, pl.ds(0, keep), :] = (1.0 - w) * near + w * far
+        return carry
+
+    lax.fori_loop(0, rows, edge, 0)
 
 
 def advect(updated, received, strip_shift, strip_frac):
     _, rows, ny, nz = updated.shape
     vmem = pl.BlockSpec(memory_space=pltpu.VMEM)
     smem = pl.BlockSpec(memory_space=pltpu.SMEM)
+    hbm = pl.BlockSpec(memory_space=pl.ANY)
     return pl.pallas_call(
         advect_kernel,
         out_shape=jax.ShapeDtypeStruct(updated.shape, updated.dtype),
-        in_specs=[smem, smem, vmem, vmem],
+        in_specs=[smem, smem, vmem, hbm],
         out_specs=vmem,
-        scratch_shapes=[pltpu.VMEM((3, rows, ny + 8, nz), jnp.float32)],
+        scratch_shapes=[
+            pltpu.VMEM(received.shape, jnp.float32),
+            pltpu.VMEM((3, rows, 2 * 8, nz), jnp.float32),
+            pltpu.SemaphoreType.DMA((1,)),
+        ],
         cost_estimate=pl.CostEstimate(
             flops=3 * 3 * rows * ny * nz, transcendentals=0,
             bytes_accessed=4 * 3 * rows * (2 * ny + KMAX + 1) * nz,

time: 81.7 us -> 82.4 us (level)
  no operation moved by 1% of the time
where the time goes in v8:
time: 82.4 us; the launch traced here: 81.9 us
  waiting for transfers between devices  32.7 us (40%)
  starting transfers between devices  29.2 us (35%)
  Pallas kernels  13.3 us (16%)
  local copies, waits for them, and re-layouts  5.77 us (7%)
    ppermute x5, waiting for transfers between devices, shifted(): return lax.ppermute(x, 'phi', [(q, (q + dp) % nq) for q in range(nq)])  24.3 us
    ppermute x5, starting transfers between devices, shifted(): return lax.ppermute(x, 'phi', [(q, (q + dp) % nq) for q in range(nq)])  16.7 us
    ppermute x2, starting transfers between devices, shifted(): return lax.ppermute(x, 'blocks', [(b, (b + db) % nb) for b in range(nb)])  12.5 us
    pallas_call x1, Pallas kernels, ct_update(): pl.pallas_call(ct_kernel, out_shape=(jax.ShapeDtypeStruct((3, rows, ny, n...  8.48 us
    ppermute x2, waiting for transfers between devices, shifted(): return lax.ppermute(x, 'blocks', [(b, (b + db) % nb) for b in range(nb)])  8.36 us
    pallas_call x1, Pallas kernels, advect(): pl.pallas_call(advect_kernel, out_shape=jax.ShapeDtypeStruct(updated.shap...  4.8 us
    slice x2, local copies, waits for them, and re-layouts, body(): own_high = jnp.concatenate([field[:, :, 0], velocity[:, :, 0]], axis=0)  3.1 us
  transfers between devices with their start and end apart: 7, of which 4 were waited for; matrix products, arithmetic and copies ran while one was open for 2% of the time, Pallas kernels for 0%

profile of v8, /device:TPU:1, one launch (start us, length us, event | category | flops | bytes accessed | tf_op | source)
XLA Modules:
  0.0 81.9 jit_solution(16918851912845628773)
XLA Ops:
  0.0 1.6 %fusion = (f32[3,16,1,512]{3,2,1,0:T(1,128)S(1)}, f32[3,16,1,512]{3,2,1,0:T(1,128)S(1)}) fusion(f32[3,16,16,512]{3,2,1,0:T(8,128)} %f_hbm.1), kind=kLoop, calls=%fused_computation.15 | loop fusion | bytes 393216 | tf_op jit(solution)/shard_map/slice | solution.py:254
  1.6 1.6 %fusion.1 = (f32[3,16,1,512]{3,2,1,0:T(1,128)S(1)}, f32[3,16,1,512]{3,2,1,0:T(1,128)S(1)}) fusion(f32[3,16,16,512]{3,2,1,0:T(8,128)} %v_hbm.1), kind=kLoop, calls=%fused_computation.16 | loop fusion | bytes 393216 | tf_op jit(solution)/shard_map/slice | solution.py:254
  3.2 4.8 %collective-permute-start.3 = (f32[6,16,512]{2,1,0:T(8,128)S(1)}, f32[6,16,512]{2,1,0:T(8,128)S(1)}, u32[]{:S(2)}, u32[]{:S(2)}) collective-permute-start(f32[6,16,512]{2,1,0:T(8,128)S(1)} %pad_maximum_fusion.3), channel_id=1, source_target_pairs={{0,1},{1,2},{2,3},{3,0},{4,5},{5,6},{6,7},{7,4},{8,9},{9,10},{10,1... | collective-permute-start | bytes 589832 | tf_op jit(solution)/shard_map/ppermute | solution.py:18
  8.0 1.1 %slice_bitcast_fusion = (f32[3,16,512]{2,1,0:T(8,128)S(1)}, f32[3,16,512]{2,1,0:T(8,128)S(1)}, f32[3,16,512]{2,1,0:T(8,128)S(1)}, f32[3,16,512]{2,1,0:T(8,128)S(1)}) fusion(f32[3,16,16,512]{3,2,1,0:T(8,128)} %v_hbm.1, f32[3,16,16,512]{3,2,1,0:T(8,128)} %f_hbm.1), kind=kLoop, calls=%fused_computation.10 | loop fusion | bytes 786432 | tf_op jit(solution)/shard_map/squeeze | solution.py:252
  9.1 10.6 %collective-permute-start = (f32[6,16,512]{2,1,0:T(8,128)S(1)}, f32[6,16,512]{2,1,0:T(8,128)S(1)}, u32[]{:S(2)}, u32[]{:S(2)}) collective-permute-start(f32[6,16,512]{2,1,0:T(8,128)S(1)} %pad_maximum_fusion), channel_id=1, source_target_pairs={{0,4},{4,8},{8,12},{12,16},{16,20},{20,24},{24,28},{28,32},{32,36}... | collective-permute-start | bytes 589832 | tf_op jit(solution)/shard_map/ppermute | solution.py:16
  19.7 1.9 %collective-permute-start.1 = (f32[6,16,512]{2,1,0:T(8,128)S(1)}, f32[6,16,512]{2,1,0:T(8,128)S(1)}, u32[]{:S(2)}, u32[]{:S(2)}) collective-permute-start(f32[6,16,512]{2,1,0:T(8,128)S(1)} %pad_maximum_fusion.1), channel_id=1, source_target_pairs={{0,508},{4,0},{8,4},{12,8},{16,12},{20,16},{24,20},{28,24},{32,28}... | collective-permute-start | bytes 589832 | tf_op jit(solution)/shard_map/ppermute | solution.py:16
  21.7 4.0 %collective-permute-start.5 = (f32[6,16,512]{2,1,0:T(8,128)S(1)}, f32[6,16,512]{2,1,0:T(8,128)S(1)}, u32[]{:S(2)}, u32[]{:S(2)}) collective-permute-start(f32[6,16,512]{2,1,0:T(8,128)S(1)} %pad_maximum_fusion.5), channel_id=1, source_target_pairs={{0,3},{1,0},{2,1},{3,2},{4,7},{5,4},{6,5},{7,6},{8,11},{9,8},{10,9... | collective-permute-start | bytes 589832 | tf_op jit(solution)/shard_map/ppermute | solution.py:18
  25.7 0.0 collective-permute-done.xm_ref
  25.7 0.0 copy-start.1
  25.7 8.4 %collective-permute-done.1.xp_ref = f32[6,16,512]{2,1,0:T(8,128)S(1)} collective-permute-done((f32[6,16,512]{2,1,0:T(8,128)S(1)}, f32[6,16,512]{2,1,0:T(8,128)S(1)}, u32[]{:S(2)}, u32[]{:S(2)}) %collective-permute-start.1) | collective-permute-done | bytes 196640 | tf_op jit(solution)/shard_map/ppermute | solution.py:16
  34.1 0.0 copy-start.2
  34.1 3.9 %collective-permute-start.4 = (f32[6,9,512]{2,1,0:T(8,128)S(1)}, f32[6,9,512]{2,1,0:T(8,128)S(1)}, u32[]{:S(2)}, u32[]{:S(2)}) collective-permute-start(f32[6,9,512]{2,1,0:T(8,128)S(1)} %pad_maximum_fusion.4), channel_id=1, source_target_pairs={{0,3},{1,0},{2,1},{3,2},{4,7},{5,4},{6,5},{7,6},{8,11},{9,8},{10,9... | collective-permute-start | bytes 331784 | tf_op jit(solution)/shard_map/ppermute | solution.py:18
  38.1 1.9 %collective-permute-start.2 = (f32[6,9,512]{2,1,0:T(8,128)S(1)}, f32[6,9,512]{2,1,0:T(8,128)S(1)}, u32[]{:S(2)}, u32[]{:S(2)}) collective-permute-start(f32[6,9,512]{2,1,0:T(8,128)S(1)} %pad_maximum_fusion.2), channel_id=1, source_target_pairs={{0,1},{1,2},{2,3},{3,0},{4,5},{5,6},{6,7},{7,4},{8,9},{9,10},{10,1... | collective-permute-start | bytes 331784 | tf_op jit(solution)/shard_map/ppermute | solution.py:18
  40.0 0.6 add_convert_fusion.flag_ref
  40.6 0.0 collective-permute-done.3.lown_ref
  40.6 0.0 copy-start.3
  40.6 0.0 collective-permute-done.5.hown_ref
  40.6 0.0 copy-start.4
  40.6 1.4 %collective-permute-done.4.hend_ref = f32[6,9,512]{2,1,0:T(8,128)S(1)} collective-permute-done((f32[6,9,512]{2,1,0:T(8,128)S(1)}, f32[6,9,512]{2,1,0:T(8,128)S(1)}, u32[]{:S(2)}, u32[]{:S(2)}) %collective-permute-start.4) | collective-permute-done | bytes 110624 | tf_op jit(solution)/shard_map/ppermute | solution.py:18
  42.0 4.5 %collective-permute-done.2.lend_ref = f32[6,9,512]{2,1,0:T(8,128)S(1)} collective-permute-done((f32[6,9,512]{2,1,0:T(8,128)S(1)}, f32[6,9,512]{2,1,0:T(8,128)S(1)}, u32[]{:S(2)}, u32[]{:S(2)}) %collective-permute-start.2) | collective-permute-done | bytes 110624 | tf_op jit(solution)/shard_map/ppermute | solution.py:18
  46.6 0.0 copy-done.1
  46.6 0.0 copy-done.2
  46.6 0.0 copy-done.3
  46.6 0.0 copy-done.4
  46.6 0.0 copy-done.5
  46.6 0.0 copy-start.6
  46.6 0.7 copy-done.6
  47.3 8.5 %shard_map.64 = (f32[3,16,16,512]{3,2,1,0:T(8,128)}, f32[336,512]{1,0:T(8,128)}) custom-call(s32[2]{0:T(128)} %eshift_ref.1, f32[2]{0:T(128)} %efrac_ref.1, s32[2]{0:T(128)} %add_convert_fusion.flag_ref, f32[3,16,16,512]{3,2,1,0:T(8,128)} %f_hbm.1, f32[3,16,16,512]{3,2,1,0:T(8,128)} %v_hbm.1, f32[6,16,512]{2,1,0:T(8,128)} %copy-done.1, ...), custom_call_target="tpu_custom_call" | custom-call | flops 15728640 | bytes 4718592 | tf_op jit(solution)/shard_map/pallas_call | solution.py:162
  55.8 2.1 %collective-permute-start.6 = (f32[336,512]{1,0:T(8,128)}, f32[336,512]{1,0:T(8,128)S(1)}, u32[]{:S(2)}, u32[]{:S(2)}) collective-permute-start(f32[336,512]{1,0:T(8,128)} %get-tuple-element.8), channel_id=1, source_target_pairs={{0,1},{1,2},{2,3},{3,0},{4,5},{5,6},{6,7},{7,4},{8,9},{9,10},{10,1... | collective-permute-start | bytes 2064392 | tf_op jit(solution)/shard_map/ppermute | solution.py:18
  57.9 18.4 %collective-permute-done.6.rec_hbm = f32[336,512]{1,0:T(8,128)S(1)} collective-permute-done((f32[336,512]{1,0:T(8,128)}, f32[336,512]{1,0:T(8,128)S(1)}, u32[]{:S(2)}, u32[]{:S(2)}) %collective-permute-start.6) | collective-permute-done | bytes 688160 | tf_op jit(solution)/shard_map/ppermute | solution.py:18
  76.3 0.8 %copy-done = f32[336,512]{1,0:T(8,128)} copy-done((f32[336,512]{1,0:T(8,128)}, f32[336,512]{1,0:T(8,128)S(1)}, u32[]{:S(2)}) %copy-start) | copy-done | bytes 688152
  77.1 4.8 %shard_map.65 = f32[3,16,16,512]{3,2,1,0:T(8,128)} custom-call(s32[16]{0:T(128)} %shift_ref.1, f32[16]{0:T(128)} %frac_ref.1, f32[3,16,16,512]{3,2,1,0:T(8,128)} %get-tuple-element.7.u_ref, f32[336,512]{1,0:T(8,128)} %copy-done), custom_call_target="tpu_custom_call" | custom-call | flops 1179648 | bytes 3833856 | tf_op jit(solution)/shard_map/pallas_call | solution.py:229
  (14 shorter events, 0.2 us)
Async XLA Ops:
  3.2 37.5 %collective-permute-start.3 = (f32[6,16,512]{2,1,0:T(8,128)S(1)}, f32[6,16,512]{2,1,0:T(8,128)S(1)}, u32[]{:S(2)}, u32[]{:S(2)}) collective-permute-start(f32[6,16,512]{2,1,0:T(8,128)S(1)} %pad_maximum_fusion.3), channel_id=1, source_target_pairs={{0,1},{1,2},{2,3},{3,0},{4,5},{5,6},{6,7},{7,4},{8,9},{9,10},{10,1... | collective-permute-start | bytes 589832 | tf_op jit(solution)/shard_map/ppermute | solution.py:18
  9.1 16.6 %collective-permute-start = (f32[6,16,512]{2,1,0:T(8,128)S(1)}, f32[6,16,512]{2,1,0:T(8,128)S(1)}, u32[]{:S(2)}, u32[]{:S(2)}) collective-permute-start(f32[6,16,512]{2,1,0:T(8,128)S(1)} %pad_maximum_fusion), channel_id=1, source_target_pairs={{0,4},{4,8},{8,12},{12,16},{16,20},{20,24},{24,28},{28,32},{32,36}... | collective-permute-start | bytes 589832 | tf_op jit(solution)/shard_map/ppermute | solution.py:16
  19.7 14.4 %collective-permute-start.1 = (f32[6,16,512]{2,1,0:T(8,128)S(1)}, f32[6,16,512]{2,1,0:T(8,128)S(1)}, u32[]{:S(2)}, u32[]{:S(2)}) collective-permute-start(f32[6,16,512]{2,1,0:T(8,128)S(1)} %pad_maximum_fusion.1), channel_id=1, source_target_pairs={{0,508},{4,0},{8,4},{12,8},{16,12},{20,16},{24,20},{28,24},{32,28}... | collective-permute-start | bytes 589832 | tf_op jit(solution)/shard_map/ppermute | solution.py:16
  21.7 19.0 %collective-permute-start.5 = (f32[6,16,512]{2,1,0:T(8,128)S(1)}, f32[6,16,512]{2,1,0:T(8,128)S(1)}, u32[]{:S(2)}, u32[]{:S(2)}) collective-permute-start(f32[6,16,512]{2,1,0:T(8,128)S(1)} %pad_maximum_fusion.5), channel_id=1, source_target_pairs={{0,3},{1,0},{2,1},{3,2},{4,7},{5,4},{6,5},{7,6},{8,11},{9,8},{10,9... | collective-permute-start | bytes 589832 | tf_op jit(solution)/shard_map/ppermute | solution.py:18
  25.7 20.9 %copy-start.1 = (f32[6,16,512]{2,1,0:T(8,128)}, f32[6,16,512]{2,1,0:T(8,128)S(1)}, u32[]{:S(2)}) copy-start(f32[6,16,512]{2,1,0:T(8,128)S(1)} %collective-permute-done.xm_ref) | copy-start | bytes 589828
  34.1 12.5 %copy-start.2 = (f32[6,16,512]{2,1,0:T(8,128)}, f32[6,16,512]{2,1,0:T(8,128)S(1)}, u32[]{:S(2)}) copy-start(f32[6,16,512]{2,1,0:T(8,128)S(1)} %collective-permute-done.1.xp_ref) | copy-start | bytes 589828
  34.1 7.9 %collective-permute-start.4 = (f32[6,9,512]{2,1,0:T(8,128)S(1)}, f32[6,9,512]{2,1,0:T(8,128)S(1)}, u32[]{:S(2)}, u32[]{:S(2)}) collective-permute-start(f32[6,9,512]{2,1,0:T(8,128)S(1)} %pad_maximum_fusion.4), channel_id=1, source_target_pairs={{0,3},{1,0},{2,1},{3,2},{4,7},{5,4},{6,5},{7,6},{8,11},{9,8},{10,9... | collective-permute-start | bytes 331784 | tf_op jit(solution)/shard_map/ppermute | solution.py:18
  38.1 8.5 %collective-permute-start.2 = (f32[6,9,512]{2,1,0:T(8,128)S(1)}, f32[6,9,512]{2,1,0:T(8,128)S(1)}, u32[]{:S(2)}, u32[]{:S(2)}) collective-permute-start(f32[6,9,512]{2,1,0:T(8,128)S(1)} %pad_maximum_fusion.2), channel_id=1, source_target_pairs={{0,1},{1,2},{2,3},{3,0},{4,5},{5,6},{6,7},{7,4},{8,9},{9,10},{10,1... | collective-permute-start | bytes 331784 | tf_op jit(solution)/shard_map/ppermute | solution.py:18
  40.6 5.9 %copy-start.3 = (f32[6,16,512]{2,1,0:T(8,128)}, f32[6,16,512]{2,1,0:T(8,128)S(1)}, u32[]{:S(2)}) copy-start(f32[6,16,512]{2,1,0:T(8,128)S(1)} %collective-permute-done.3.lown_ref) | copy-start | bytes 589828
  40.6 5.9 %copy-start.4 = (f32[6,16,512]{2,1,0:T(8,128)}, f32[6,16,512]{2,1,0:T(8,128)S(1)}, u32[]{:S(2)}) copy-start(f32[6,16,512]{2,1,0:T(8,128)S(1)} %collective-permute-done.5.hown_ref) | copy-start | bytes 589828
  42.0 4.6 %copy-start.5 = (f32[6,9,512]{2,1,0:T(8,128)}, f32[6,9,512]{2,1,0:T(8,128)S(1)}, u32[]{:S(2)}) copy-start(f32[6,9,512]{2,1,0:T(8,128)S(1)} %collective-permute-done.4.hend_ref) | copy-start | bytes 331780
  46.6 0.7 copy-start.6
  55.8 20.5 %collective-permute-start.6 = (f32[336,512]{1,0:T(8,128)}, f32[336,512]{1,0:T(8,128)S(1)}, u32[]{:S(2)}, u32[]{:S(2)}) collective-permute-start(f32[336,512]{1,0:T(8,128)} %get-tuple-element.8), channel_id=1, source_target_pairs={{0,1},{1,2},{2,3},{3,0},{4,5},{5,6},{6,7},{7,4},{8,9},{9,10},{10,1... | collective-permute-start | bytes 2064392 | tf_op jit(solution)/shard_map/ppermute | solution.py:18
  76.2 0.8 %copy-start = (f32[336,512]{1,0:T(8,128)}, f32[336,512]{1,0:T(8,128)S(1)}, u32[]{:S(2)}) copy-start(f32[336,512]{1,0:T(8,128)S(1)} %collective-permute-done.6.rec_hbm) | copy-start | bytes 2064388

commit v9 on v6

--- a/solution.py
+++ b/solution.py
@@ -182,44 +182,94 @@
     )(eshift, efrac, flags, field, velocity, xm, xp, *low_in, *high_in)
 
 
-def advect_kernel(shift_ref, frac_ref, u_ref, rec_ref, o_ref, ext):
+def blend(src, o_ref, x, s, w, src_start, dst_start, count):
+    for k in range(KMAX + 1):
+        @pl.when(s == k)
+        def _():
+            near = src[:, x, pl.ds(src_start - k, count), :]
+            far = src[:, x, pl.ds(src_start - k - 1, count), :]
+            o_ref[:, x, pl.ds(dst_start, count), :] = (1.0 - w) * near + w * far
+
+
+def local_kernel(shift_ref, frac_ref, u_ref, o_hbm, out, sem):
     rows, ny = u_ref.shape[1], u_ref.shape[2]
-    lead = 8
     keep = KMAX + 1
-    for c in range(3):
-        for x in range(rows):
-            ext[c, x, pl.ds(lead - keep, keep), :] = rec_ref[pl.ds((c * rows + x) * keep, keep), :]
-    ext[:, :, pl.ds(lead, ny), :] = u_ref[...]
 
     def strip(x, carry):
-        s = shift_ref[x]
-        w = frac_ref[x]
-        for k in range(KMAX + 1):
-            @pl.when(s == k)
-            def _():
-                near = ext[:, x, pl.ds(lead - k, ny), :]
-                far = ext[:, x, pl.ds(lead - k - 1, ny), :]
-                o_ref[:, x] = (1.0 - w) * near + w * far
+        blend(u_ref, out, x, shift_ref[x], frac_ref[x], keep, keep, ny - keep)
         return carry
 
     lax.fori_loop(0, rows, strip, 0)
-
-
-def advect(updated, received, strip_shift, strip_frac):
+    put = pltpu.make_async_copy(out, o_hbm, sem.at[0])
+    put.start()
+    put.wait()
+
+
+def advect_local(updated, strip_shift, strip_frac):
     _, rows, ny, nz = updated.shape
     vmem = pl.BlockSpec(memory_space=pltpu.VMEM)
     smem = pl.BlockSpec(memory_space=pltpu.SMEM)
+    hbm = pl.BlockSpec(memory_space=pl.ANY)
     return pl.pallas_call(
-        advect_kernel,
+        local_kernel,
         out_shape=jax.ShapeDtypeStruct(updated.shape, updated.dtype),
-        in_specs=[smem, smem, vmem, vmem],
-        out_specs=vmem,
-        scratch_shapes=[pltpu.VMEM((3, rows, ny + 8, nz), jnp.float32)],
+        in_specs=[smem, smem, vmem],
+        out_specs=hbm,
+        scratch_shapes=[pltpu.VMEM(updated.shape, jnp.float32), pltpu.SemaphoreType.DMA((1,))],
         cost_estimate=pl.CostEstimate(
             flops=3 * 3 * rows * ny * nz, transcendentals=0,
-            bytes_accessed=4 * 3 * rows * (2 * ny + KMAX + 1) * nz,
+            bytes_accessed=4 * 3 * rows * 2 * ny * nz,
         ),
-    )(strip_shift, strip_frac, updated, received)
+    )(strip_shift, strip_frac, updated)
+
+
+def edge_kernel(shift_ref, frac_ref, u_ref, rec_hbm, part_hbm, o_hbm, flat, ext, tile, sem):
+    rows = u_ref.shape[1]
+    lead = 8
+    keep = KMAX + 1
+    fetch = pltpu.make_async_copy(rec_hbm, flat, sem.at[0])
+    fetch.start()
+    head = pltpu.make_async_copy(part_hbm.at[:, :, pl.ds(0, lead), :], tile, sem.at[1])
+    head.start()
+    ext[:, :, pl.ds(lead, lead), :] = u_ref[:, :, pl.ds(0, lead), :]
+    fetch.wait()
+    for c in range(3):
+        for x in range(rows):
+            ext[c, x, pl.ds(lead - keep, keep), :] = flat[pl.ds((c * rows + x) * keep, keep), :]
+    head.wait()
+
+    def strip(x, carry):
+        blend(ext, tile, x, shift_ref[x], frac_ref[x], lead, 0, keep)
+        return carry
+
+    lax.fori_loop(0, rows, strip, 0)
+    put = pltpu.make_async_copy(tile, o_hbm.at[:, :, pl.ds(0, lead), :], sem.at[2])
+    put.start()
+    put.wait()
+
+
+def advect_edge(updated, received, partial, strip_shift, strip_frac):
+    _, rows, ny, nz = updated.shape
+    vmem = pl.BlockSpec(memory_space=pltpu.VMEM)
+    smem = pl.BlockSpec(memory_space=pltpu.SMEM)
+    hbm = pl.BlockSpec(memory_space=pl.ANY)
+    return pl.pallas_call(
+        edge_kernel,
+        out_shape=jax.ShapeDtypeStruct(updated.shape, updated.dtype),
+        in_specs=[smem, smem, vmem, hbm, hbm],
+        out_specs=hbm,
+        input_output_aliases={4: 0},
+        scratch_shapes=[
+            pltpu.VMEM(received.shape, jnp.float32),
+            pltpu.VMEM((3, rows, 16, nz), jnp.float32),
+            pltpu.VMEM((3, rows, 8, nz), jnp.float32),
+            pltpu.SemaphoreType.DMA((3,)),
+        ],
+        cost_estimate=pl.CostEstimate(
+            flops=9 * rows * (KMAX + 1) * nz, transcendentals=0,
+            bytes_accessed=4 * 3 * rows * 3 * 8 * nz,
+        ),
+    )(strip_shift, strip_frac, updated, received, partial)
 
 
 def body(field, velocity, strip_shift, strip_frac, edge_shift, edge_frac):
@@ -238,7 +288,8 @@
     flags = jnp.stack([b == 0, b == nb - 1]).astype(jnp.int32)
     updated, top = ct_update(edge_shift, edge_frac, flags, field, velocity, xm, xp, from_low, from_high)
     received = shifted(top, 0, 1)
-    return advect(updated, received, strip_shift, strip_frac)
+    partial = advect_local(updated, strip_shift, strip_frac)
+    return advect_edge(updated, received, partial, strip_shift, strip_frac)
 
 
 def solution(mesh):

time: 81.7 us -> 82.3 us (level)
  Pallas kernels: 12.6 us -> 16.8 us
  waiting for transfers between devices: 32.7 us -> 29.1 us
    pallas_call x1 -> x2, Pallas kernels: 4.13 us -> 8.26 us  [the longest x1 4.66 us: advect_edge(): pl.pallas_call(edge_kernel, out_shape=jax.ShapeDtypeStruct(updated.shape,...]
    ppermute x5, waiting for transfers between devices: 24.3 us -> 20.7 us  [shifted(): return lax.ppermute(x, 'phi', [(q, (q + dp) % nq) for q in range(nq)])]
  transfers between devices with their start and end apart: 7 -> 7, of which waited for: 4 -> 4; matrix products, arithmetic and copies ran while one was open for 2% -> 2% of each run, Pallas kernels for 0% -> 4%
where the time goes in v9:
time: 82.3 us; the launch traced here: 81.8 us
  starting transfers between devices  29.2 us (35%)
  waiting for transfers between devices  29.1 us (35%)
  Pallas kernels  16.8 us (20%)
  local copies, waits for them, and re-layouts  5.78 us (7%)
    ppermute x5, waiting for transfers between devices, shifted(): return lax.ppermute(x, 'phi', [(q, (q + dp) % nq) for q in range(nq)])  20.7 us
    ppermute x5, starting transfers between devices, shifted(): return lax.ppermute(x, 'phi', [(q, (q + dp) % nq) for q in range(nq)])  16.7 us
    ppermute x2, starting transfers between devices, shifted(): return lax.ppermute(x, 'blocks', [(b, (b + db) % nb) for b in range(nb)])  12.5 us
    pallas_call x1, Pallas kernels, ct_update(): pl.pallas_call(ct_kernel, out_shape=(jax.ShapeDtypeStruct((3, rows, ny, n...  8.5 us
    ppermute x2, waiting for transfers between devices, shifted(): return lax.ppermute(x, 'blocks', [(b, (b + db) % nb) for b in range(nb)])  8.36 us
    pallas_call x1, Pallas kernels, advect_edge(): pl.pallas_call(edge_kernel, out_shape=jax.ShapeDtypeStruct(updated.shape,...  4.66 us
    pallas_call x1, Pallas kernels, advect_local(): pl.pallas_call(local_kernel, out_shape=jax.ShapeDtypeStruct(updated.shape...  3.6 us
    slice x2, local copies, waits for them, and re-layouts, body(): own_high = jnp.concatenate([field[:, :, 0], velocity[:, :, 0]], axis=0)  3.1 us
  transfers between devices with their start and end apart: 7, of which 4 were waited for; matrix products, arithmetic and copies ran while one was open for 2% of the time, Pallas kernels for 4%

profile of v9, /device:TPU:1, one launch (start us, length us, event | category | flops | bytes accessed | tf_op | source)
XLA Modules:
  0.0 81.8 jit_solution(4205492215878529261)
XLA Ops:
  0.0 1.6 %fusion = (f32[3,16,1,512]{3,2,1,0:T(1,128)S(1)}, f32[3,16,1,512]{3,2,1,0:T(1,128)S(1)}) fusion(f32[3,16,16,512]{3,2,1,0:T(8,128)} %f_hbm.1), kind=kLoop, calls=%fused_computation.15 | loop fusion | bytes 393216 | tf_op jit(solution)/shard_map/slice | solution.py:283
  1.6 1.6 %fusion.1 = (f32[3,16,1,512]{3,2,1,0:T(1,128)S(1)}, f32[3,16,1,512]{3,2,1,0:T(1,128)S(1)}) fusion(f32[3,16,16,512]{3,2,1,0:T(8,128)} %v_hbm.1), kind=kLoop, calls=%fused_computation.16 | loop fusion | bytes 393216 | tf_op jit(solution)/shard_map/slice | solution.py:283
  3.2 4.8 %collective-permute-start.3 = (f32[6,16,512]{2,1,0:T(8,128)S(1)}, f32[6,16,512]{2,1,0:T(8,128)S(1)}, u32[]{:S(2)}, u32[]{:S(2)}) collective-permute-start(f32[6,16,512]{2,1,0:T(8,128)S(1)} %pad_maximum_fusion.3), channel_id=1, source_target_pairs={{0,1},{1,2},{2,3},{3,0},{4,5},{5,6},{6,7},{7,4},{8,9},{9,10},{10,1... | collective-permute-start | bytes 589832 | tf_op jit(solution)/shard_map/ppermute | solution.py:18
  8.0 1.1 %slice_bitcast_fusion = (f32[3,16,512]{2,1,0:T(8,128)S(1)}, f32[3,16,512]{2,1,0:T(8,128)S(1)}, f32[3,16,512]{2,1,0:T(8,128)S(1)}, f32[3,16,512]{2,1,0:T(8,128)S(1)}) fusion(f32[3,16,16,512]{3,2,1,0:T(8,128)} %v_hbm.1, f32[3,16,16,512]{3,2,1,0:T(8,128)} %f_hbm.1), kind=kLoop, calls=%fused_computation.10 | loop fusion | bytes 786432 | tf_op jit(solution)/shard_map/squeeze | solution.py:281
  9.1 10.6 %collective-permute-start = (f32[6,16,512]{2,1,0:T(8,128)S(1)}, f32[6,16,512]{2,1,0:T(8,128)S(1)}, u32[]{:S(2)}, u32[]{:S(2)}) collective-permute-start(f32[6,16,512]{2,1,0:T(8,128)S(1)} %pad_maximum_fusion), channel_id=1, source_target_pairs={{0,4},{4,8},{8,12},{12,16},{16,20},{20,24},{24,28},{28,32},{32,36}... | collective-permute-start | bytes 589832 | tf_op jit(solution)/shard_map/ppermute | solution.py:16
  19.7 1.9 %collective-permute-start.1 = (f32[6,16,512]{2,1,0:T(8,128)S(1)}, f32[6,16,512]{2,1,0:T(8,128)S(1)}, u32[]{:S(2)}, u32[]{:S(2)}) collective-permute-start(f32[6,16,512]{2,1,0:T(8,128)S(1)} %pad_maximum_fusion.1), channel_id=1, source_target_pairs={{0,508},{4,0},{8,4},{12,8},{16,12},{20,16},{24,20},{28,24},{32,28}... | collective-permute-start | bytes 589832 | tf_op jit(solution)/shard_map/ppermute | solution.py:16
  21.7 4.0 %collective-permute-start.5 = (f32[6,16,512]{2,1,0:T(8,128)S(1)}, f32[6,16,512]{2,1,0:T(8,128)S(1)}, u32[]{:S(2)}, u32[]{:S(2)}) collective-permute-start(f32[6,16,512]{2,1,0:T(8,128)S(1)} %pad_maximum_fusion.5), channel_id=1, source_target_pairs={{0,3},{1,0},{2,1},{3,2},{4,7},{5,4},{6,5},{7,6},{8,11},{9,8},{10,9... | collective-permute-start | bytes 589832 | tf_op jit(solution)/shard_map/ppermute | solution.py:18
  25.7 0.0 collective-permute-done.xm_ref
  25.7 0.0 copy-start.1
  25.7 8.4 %collective-permute-done.1.xp_ref = f32[6,16,512]{2,1,0:T(8,128)S(1)} collective-permute-done((f32[6,16,512]{2,1,0:T(8,128)S(1)}, f32[6,16,512]{2,1,0:T(8,128)S(1)}, u32[]{:S(2)}, u32[]{:S(2)}) %collective-permute-start.1) | collective-permute-done | bytes 196640 | tf_op jit(solution)/shard_map/ppermute | solution.py:16
  34.1 0.0 copy-start.2
  34.1 3.9 %collective-permute-start.4 = (f32[6,9,512]{2,1,0:T(8,128)S(1)}, f32[6,9,512]{2,1,0:T(8,128)S(1)}, u32[]{:S(2)}, u32[]{:S(2)}) collective-permute-start(f32[6,9,512]{2,1,0:T(8,128)S(1)} %pad_maximum_fusion.4), channel_id=1, source_target_pairs={{0,3},{1,0},{2,1},{3,2},{4,7},{5,4},{6,5},{7,6},{8,11},{9,8},{10,9... | collective-permute-start | bytes 331784 | tf_op jit(solution)/shard_map/ppermute | solution.py:18
  38.1 1.9 %collective-permute-start.2 = (f32[6,9,512]{2,1,0:T(8,128)S(1)}, f32[6,9,512]{2,1,0:T(8,128)S(1)}, u32[]{:S(2)}, u32[]{:S(2)}) collective-permute-start(f32[6,9,512]{2,1,0:T(8,128)S(1)} %pad_maximum_fusion.2), channel_id=1, source_target_pairs={{0,1},{1,2},{2,3},{3,0},{4,5},{5,6},{6,7},{7,4},{8,9},{9,10},{10,1... | collective-permute-start | bytes 331784 | tf_op jit(solution)/shard_map/ppermute | solution.py:18
  40.0 0.6 add_convert_fusion.flag_ref
  40.6 0.0 collective-permute-done.3.lown_ref
  40.6 0.0 collective-permute-done.5.hown_ref
  40.6 0.0 copy-start.4
  40.6 1.4 %collective-permute-done.4.hend_ref = f32[6,9,512]{2,1,0:T(8,128)S(1)} collective-permute-done((f32[6,9,512]{2,1,0:T(8,128)S(1)}, f32[6,9,512]{2,1,0:T(8,128)S(1)}, u32[]{:S(2)}, u32[]{:S(2)}) %collective-permute-start.4) | collective-permute-done | bytes 110624 | tf_op jit(solution)/shard_map/ppermute | solution.py:18
  42.0 4.5 %collective-permute-done.2.lend_ref = f32[6,9,512]{2,1,0:T(8,128)S(1)} collective-permute-done((f32[6,9,512]{2,1,0:T(8,128)S(1)}, f32[6,9,512]{2,1,0:T(8,128)S(1)}, u32[]{:S(2)}, u32[]{:S(2)}) %collective-permute-start.2) | collective-permute-done | bytes 110624 | tf_op jit(solution)/shard_map/ppermute | solution.py:18
  46.6 0.0 copy-done.1
  46.6 0.0 copy-done.2
  46.6 0.0 copy-done.3
  46.6 0.0 copy-done.4
  46.6 0.0 copy-done.5
  46.6 0.0 copy-start.6
  46.6 0.7 copy-done.6
  47.3 8.5 %shard_map.64 = (f32[3,16,16,512]{3,2,1,0:T(8,128)}, f32[336,512]{1,0:T(8,128)}) custom-call(s32[2]{0:T(128)} %eshift_ref.1, f32[2]{0:T(128)} %efrac_ref.1, s32[2]{0:T(128)} %add_convert_fusion.flag_ref, f32[3,16,16,512]{3,2,1,0:T(8,128)} %f_hbm.1, f32[3,16,16,512]{3,2,1,0:T(8,128)} %v_hbm.1, f32[6,16,512]{2,1,0:T(8,128)} %copy-done.1, ...), custom_call_target="tpu_custom_call" | custom-call | flops 15728640 | bytes 4718592 | tf_op jit(solution)/shard_map/pallas_call | solution.py:162
  55.8 2.1 %collective-permute-start.6 = (f32[336,512]{1,0:T(8,128)}, f32[336,512]{1,0:T(8,128)S(1)}, u32[]{:S(2)}, u32[]{:S(2)}) collective-permute-start(f32[336,512]{1,0:T(8,128)} %get-tuple-element.8), channel_id=1, source_target_pairs={{0,1},{1,2},{2,3},{3,0},{4,5},{5,6},{6,7},{7,4},{8,9},{9,10},{10,1... | collective-permute-start | bytes 2064392 | tf_op jit(solution)/shard_map/ppermute | solution.py:18
  57.9 3.6 %shard_map.65.part_hbm = f32[3,16,16,512]{3,2,1,0:T(8,128)} custom-call(s32[16]{0:T(128)} %shift_ref.3, f32[16]{0:T(128)} %frac_ref.3, f32[3,16,16,512]{3,2,1,0:T(8,128)} %get-tuple-element.7.u_ref), custom_call_target="tpu_custom_call" | custom-call | flops 1179648 | bytes 3145728 | tf_op jit(solution)/shard_map/pallas_call | solution.py:213
  61.5 14.8 %collective-permute-done.6.rec_hbm = f32[336,512]{1,0:T(8,128)S(1)} collective-permute-done((f32[336,512]{1,0:T(8,128)}, f32[336,512]{1,0:T(8,128)S(1)}, u32[]{:S(2)}, u32[]{:S(2)}) %collective-permute-start.6) | collective-permute-done | bytes 688160 | tf_op jit(solution)/shard_map/ppermute | solution.py:18
  76.3 0.8 %copy-done = f32[336,512]{1,0:T(8,128)} copy-done((f32[336,512]{1,0:T(8,128)}, f32[336,512]{1,0:T(8,128)S(1)}, u32[]{:S(2)}) %copy-start) | copy-done | bytes 688152
  77.1 4.7 %shard_map.66 = f32[3,16,16,512]{3,2,1,0:T(8,128)} custom-call(s32[16]{0:T(128)} %shift_ref.3, f32[16]{0:T(128)} %frac_ref.3, f32[3,16,16,512]{3,2,1,0:T(8,128)} %get-tuple-element.7.u_ref, f32[336,512]{1,0:T(8,128)} %copy-done, f32[3,16,16,512]{3,2,1,0:T(8,128)} %shard_map.65.part_hbm), custom_call_target="tpu_custom_call", output_to_operand_aliasing={{}: (4, {})} | custom-call | flops 516096 | bytes 2359296 | tf_op jit(solution)/shard_map/pallas_call | solution.py:256
  (15 shorter events, 0.2 us)
Async XLA Ops:
  3.2 37.4 %collective-permute-start.3 = (f32[6,16,512]{2,1,0:T(8,128)S(1)}, f32[6,16,512]{2,1,0:T(8,128)S(1)}, u32[]{:S(2)}, u32[]{:S(2)}) collective-permute-start(f32[6,16,512]{2,1,0:T(8,128)S(1)} %pad_maximum_fusion.3), channel_id=1, source_target_pairs={{0,1},{1,2},{2,3},{3,0},{4,5},{5,6},{6,7},{7,4},{8,9},{9,10},{10,1... | collective-permute-start | bytes 589832 | tf_op jit(solution)/shard_map/ppermute | solution.py:18
  9.1 16.6 %collective-permute-start = (f32[6,16,512]{2,1,0:T(8,128)S(1)}, f32[6,16,512]{2,1,0:T(8,128)S(1)}, u32[]{:S(2)}, u32[]{:S(2)}) collective-permute-start(f32[6,16,512]{2,1,0:T(8,128)S(1)} %pad_maximum_fusion), channel_id=1, source_target_pairs={{0,4},{4,8},{8,12},{12,16},{16,20},{20,24},{24,28},{28,32},{32,36}... | collective-permute-start | bytes 589832 | tf_op jit(solution)/shard_map/ppermute | solution.py:16
  19.7 14.4 %collective-permute-start.1 = (f32[6,16,512]{2,1,0:T(8,128)S(1)}, f32[6,16,512]{2,1,0:T(8,128)S(1)}, u32[]{:S(2)}, u32[]{:S(2)}) collective-permute-start(f32[6,16,512]{2,1,0:T(8,128)S(1)} %pad_maximum_fusion.1), channel_id=1, source_target_pairs={{0,508},{4,0},{8,4},{12,8},{16,12},{20,16},{24,20},{28,24},{32,28}... | collective-permute-start | bytes 589832 | tf_op jit(solution)/shard_map/ppermute | solution.py:16
  21.7 18.9 %collective-permute-start.5 = (f32[6,16,512]{2,1,0:T(8,128)S(1)}, f32[6,16,512]{2,1,0:T(8,128)S(1)}, u32[]{:S(2)}, u32[]{:S(2)}) collective-permute-start(f32[6,16,512]{2,1,0:T(8,128)S(1)} %pad_maximum_fusion.5), channel_id=1, source_target_pairs={{0,3},{1,0},{2,1},{3,2},{4,7},{5,4},{6,5},{7,6},{8,11},{9,8},{10,9... | collective-permute-start | bytes 589832 | tf_op jit(solution)/shard_map/ppermute | solution.py:18
  25.7 20.9 %copy-start.1 = (f32[6,16,512]{2,1,0:T(8,128)}, f32[6,16,512]{2,1,0:T(8,128)S(1)}, u32[]{:S(2)}) copy-start(f32[6,16,512]{2,1,0:T(8,128)S(1)} %collective-permute-done.xm_ref) | copy-start | bytes 589828
  34.1 12.5 %copy-start.2 = (f32[6,16,512]{2,1,0:T(8,128)}, f32[6,16,512]{2,1,0:T(8,128)S(1)}, u32[]{:S(2)}) copy-start(f32[6,16,512]{2,1,0:T(8,128)S(1)} %collective-permute-done.1.xp_ref) | copy-start | bytes 589828
  34.1 7.9 %collective-permute-start.4 = (f32[6,9,512]{2,1,0:T(8,128)S(1)}, f32[6,9,512]{2,1,0:T(8,128)S(1)}, u32[]{:S(2)}, u32[]{:S(2)}) collective-permute-start(f32[6,9,512]{2,1,0:T(8,128)S(1)} %pad_maximum_fusion.4), channel_id=1, source_target_pairs={{0,3},{1,0},{2,1},{3,2},{4,7},{5,4},{6,5},{7,6},{8,11},{9,8},{10,9... | collective-permute-start | bytes 331784 | tf_op jit(solution)/shard_map/ppermute | solution.py:18
  38.1 8.5 %collective-permute-start.2 = (f32[6,9,512]{2,1,0:T(8,128)S(1)}, f32[6,9,512]{2,1,0:T(8,128)S(1)}, u32[]{:S(2)}, u32[]{:S(2)}) collective-permute-start(f32[6,9,512]{2,1,0:T(8,128)S(1)} %pad_maximum_fusion.2), channel_id=1, source_target_pairs={{0,1},{1,2},{2,3},{3,0},{4,5},{5,6},{6,7},{7,4},{8,9},{9,10},{10,1... | collective-permute-start | bytes 331784 | tf_op jit(solution)/shard_map/ppermute | solution.py:18
  40.6 6.0 %copy-start.3 = (f32[6,16,512]{2,1,0:T(8,128)}, f32[6,16,512]{2,1,0:T(8,128)S(1)}, u32[]{:S(2)}) copy-start(f32[6,16,512]{2,1,0:T(8,128)S(1)} %collective-permute-done.3.lown_ref) | copy-start | bytes 589828
  40.6 6.0 %copy-start.4 = (f32[6,16,512]{2,1,0:T(8,128)}, f32[6,16,512]{2,1,0:T(8,128)S(1)}, u32[]{:S(2)}) copy-start(f32[6,16,512]{2,1,0:T(8,128)S(1)} %collective-permute-done.5.hown_ref) | copy-start | bytes 589828
  42.0 4.6 %copy-start.5 = (f32[6,9,512]{2,1,0:T(8,128)}, f32[6,9,512]{2,1,0:T(8,128)S(1)}, u32[]{:S(2)}) copy-start(f32[6,9,512]{2,1,0:T(8,128)S(1)} %collective-permute-done.4.hend_ref) | copy-start | bytes 331780
  46.6 0.7 copy-start.6
  55.8 20.5 %collective-permute-start.6 = (f32[336,512]{1,0:T(8,128)}, f32[336,512]{1,0:T(8,128)S(1)}, u32[]{:S(2)}, u32[]{:S(2)}) collective-permute-start(f32[336,512]{1,0:T(8,128)} %get-tuple-element.8), channel_id=1, source_target_pairs={{0,1},{1,2},{2,3},{3,0},{4,5},{5,6},{6,7},{7,4},{8,9},{9,10},{10,1... | collective-permute-start | bytes 2064392 | tf_op jit(solution)/shard_map/ppermute | solution.py:18
  76.3 0.8 %copy-start = (f32[336,512]{1,0:T(8,128)}, f32[336,512]{1,0:T(8,128)S(1)}, u32[]{:S(2)}) copy-start(f32[336,512]{1,0:T(8,128)S(1)} %collective-permute-done.6.rec_hbm) | copy-start | bytes 2064388

commit v10 on v9

--- a/solution.py
+++ b/solution.py
@@ -223,20 +223,22 @@
     )(strip_shift, strip_frac, updated)
 
 
-def edge_kernel(shift_ref, frac_ref, u_ref, rec_hbm, part_hbm, o_hbm, flat, ext, tile, sem):
-    rows = u_ref.shape[1]
+def edge_kernel(shift_ref, frac_ref, u_hbm, rec_hbm, part_hbm, o_hbm, flat, ext, tile, sem):
+    rows = u_hbm.shape[1]
     lead = 8
     keep = KMAX + 1
     fetch = pltpu.make_async_copy(rec_hbm, flat, sem.at[0])
     fetch.start()
     head = pltpu.make_async_copy(part_hbm.at[:, :, pl.ds(0, lead), :], tile, sem.at[1])
     head.start()
-    ext[:, :, pl.ds(lead, lead), :] = u_ref[:, :, pl.ds(0, lead), :]
+    low = pltpu.make_async_copy(u_hbm.at[:, :, pl.ds(0, lead), :], ext.at[:, :, pl.ds(lead, lead), :], sem.at[3])
+    low.start()
     fetch.wait()
     for c in range(3):
         for x in range(rows):
             ext[c, x, pl.ds(lead - keep, keep), :] = flat[pl.ds((c * rows + x) * keep, keep), :]
     head.wait()
+    low.wait()
 
     def strip(x, carry):
         blend(ext, tile, x, shift_ref[x], frac_ref[x], lead, 0, keep)
@@ -256,14 +258,14 @@
     return pl.pallas_call(
         edge_kernel,
         out_shape=jax.ShapeDtypeStruct(updated.shape, updated.dtype),
-        in_specs=[smem, smem, vmem, hbm, hbm],
+        in_specs=[smem, smem, hbm, hbm, hbm],
         out_specs=hbm,
         input_output_aliases={4: 0},
         scratch_shapes=[
             pltpu.VMEM(received.shape, jnp.float32),
             pltpu.VMEM((3, rows, 16, nz), jnp.float32),
             pltpu.VMEM((3, rows, 8, nz), jnp.float32),
-            pltpu.SemaphoreType.DMA((3,)),
+            pltpu.SemaphoreType.DMA((4,)),
         ],
         cost_estimate=pl.CostEstimate(
             flops=9 * rows * (KMAX + 1) * nz, transcendentals=0,

time: 82.3 us -> 81.7 us (level)
  no operation moved by 1% of the time
where the time goes in v10:
time: 81.7 us; the launch traced here: 81.3 us
  starting transfers between devices  29.2 us (36%)
  waiting for transfers between devices  29.1 us (36%)
  Pallas kernels  16.2 us (20%)
  local copies, waits for them, and re-layouts  5.78 us (7%)
    ppermute x5, waiting for transfers between devices, shifted(): return lax.ppermute(x, 'phi', [(q, (q + dp) % nq) for q in range(nq)])  20.8 us
    ppermute x5, starting transfers between devices, shifted(): return lax.ppermute(x, 'phi', [(q, (q + dp) % nq) for q in range(nq)])  16.7 us
    ppermute x2, starting transfers between devices, shifted(): return lax.ppermute(x, 'blocks', [(b, (b + db) % nb) for b in range(nb)])  12.5 us
    pallas_call x1, Pallas kernels, ct_update(): pl.pallas_call(ct_kernel, out_shape=(jax.ShapeDtypeStruct((3, rows, ny, n...  8.5 us
    ppermute x2, waiting for transfers between devices, shifted(): return lax.ppermute(x, 'blocks', [(b, (b + db) % nb) for b in range(nb)])  8.36 us
    pallas_call x1, Pallas kernels, advect_edge(): pl.pallas_call(edge_kernel, out_shape=jax.ShapeDtypeStruct(updated.shape,...  4.13 us
    pallas_call x1, Pallas kernels, advect_local(): pl.pallas_call(local_kernel, out_shape=jax.ShapeDtypeStruct(updated.shape...  3.6 us
    slice x2, local copies, waits for them, and re-layouts, body(): own_high = jnp.concatenate([field[:, :, 0], velocity[:, :, 0]], axis=0)  3.1 us
  transfers between devices with their start and end apart: 7, of which 4 were waited for; matrix products, arithmetic and copies ran while one was open for 2% of the time, Pallas kernels for 4%

profile of v10, /device:TPU:1, one launch (start us, length us, event | category | flops | bytes accessed | tf_op | source)
XLA Modules:
  0.0 81.3 jit_solution(8891947021644912922)
XLA Ops:
  0.0 1.6 %fusion = (f32[3,16,1,512]{3,2,1,0:T(1,128)S(1)}, f32[3,16,1,512]{3,2,1,0:T(1,128)S(1)}) fusion(f32[3,16,16,512]{3,2,1,0:T(8,128)} %f_hbm.1), kind=kLoop, calls=%fused_computation.15 | loop fusion | bytes 393216 | tf_op jit(solution)/shard_map/slice | solution.py:285
  1.6 1.6 %fusion.1 = (f32[3,16,1,512]{3,2,1,0:T(1,128)S(1)}, f32[3,16,1,512]{3,2,1,0:T(1,128)S(1)}) fusion(f32[3,16,16,512]{3,2,1,0:T(8,128)} %v_hbm.1), kind=kLoop, calls=%fused_computation.16 | loop fusion | bytes 393216 | tf_op jit(solution)/shard_map/slice | solution.py:285
  3.2 4.8 %collective-permute-start.3 = (f32[6,16,512]{2,1,0:T(8,128)S(1)}, f32[6,16,512]{2,1,0:T(8,128)S(1)}, u32[]{:S(2)}, u32[]{:S(2)}) collective-permute-start(f32[6,16,512]{2,1,0:T(8,128)S(1)} %pad_maximum_fusion.3), channel_id=1, source_target_pairs={{0,1},{1,2},{2,3},{3,0},{4,5},{5,6},{6,7},{7,4},{8,9},{9,10},{10,1... | collective-permute-start | bytes 589832 | tf_op jit(solution)/shard_map/ppermute | solution.py:18
  8.0 1.1 %slice_bitcast_fusion = (f32[3,16,512]{2,1,0:T(8,128)S(1)}, f32[3,16,512]{2,1,0:T(8,128)S(1)}, f32[3,16,512]{2,1,0:T(8,128)S(1)}, f32[3,16,512]{2,1,0:T(8,128)S(1)}) fusion(f32[3,16,16,512]{3,2,1,0:T(8,128)} %v_hbm.1, f32[3,16,16,512]{3,2,1,0:T(8,128)} %f_hbm.1), kind=kLoop, calls=%fused_computation.10 | loop fusion | bytes 786432 | tf_op jit(solution)/shard_map/squeeze | solution.py:283
  9.1 10.6 %collective-permute-start = (f32[6,16,512]{2,1,0:T(8,128)S(1)}, f32[6,16,512]{2,1,0:T(8,128)S(1)}, u32[]{:S(2)}, u32[]{:S(2)}) collective-permute-start(f32[6,16,512]{2,1,0:T(8,128)S(1)} %pad_maximum_fusion), channel_id=1, source_target_pairs={{0,4},{4,8},{8,12},{12,16},{16,20},{20,24},{24,28},{28,32},{32,36}... | collective-permute-start | bytes 589832 | tf_op jit(solution)/shard_map/ppermute | solution.py:16
  19.7 1.9 %collective-permute-start.1 = (f32[6,16,512]{2,1,0:T(8,128)S(1)}, f32[6,16,512]{2,1,0:T(8,128)S(1)}, u32[]{:S(2)}, u32[]{:S(2)}) collective-permute-start(f32[6,16,512]{2,1,0:T(8,128)S(1)} %pad_maximum_fusion.1), channel_id=1, source_target_pairs={{0,508},{4,0},{8,4},{12,8},{16,12},{20,16},{24,20},{28,24},{32,28}... | collective-permute-start | bytes 589832 | tf_op jit(solution)/shard_map/ppermute | solution.py:16
  21.7 4.0 %collective-permute-start.5 = (f32[6,16,512]{2,1,0:T(8,128)S(1)}, f32[6,16,512]{2,1,0:T(8,128)S(1)}, u32[]{:S(2)}, u32[]{:S(2)}) collective-permute-start(f32[6,16,512]{2,1,0:T(8,128)S(1)} %pad_maximum_fusion.5), channel_id=1, source_target_pairs={{0,3},{1,0},{2,1},{3,2},{4,7},{5,4},{6,5},{7,6},{8,11},{9,8},{10,9... | collective-permute-start | bytes 589832 | tf_op jit(solution)/shard_map/ppermute | solution.py:18
  25.7 0.0 collective-permute-done.xm_ref
  25.7 0.0 copy-start.1
  25.7 8.4 %collective-permute-done.1.xp_ref = f32[6,16,512]{2,1,0:T(8,128)S(1)} collective-permute-done((f32[6,16,512]{2,1,0:T(8,128)S(1)}, f32[6,16,512]{2,1,0:T(8,128)S(1)}, u32[]{:S(2)}, u32[]{:S(2)}) %collective-permute-start.1) | collective-permute-done | bytes 196640 | tf_op jit(solution)/shard_map/ppermute | solution.py:16
  34.1 0.0 copy-start.2
  34.1 3.9 %collective-permute-start.4 = (f32[6,9,512]{2,1,0:T(8,128)S(1)}, f32[6,9,512]{2,1,0:T(8,128)S(1)}, u32[]{:S(2)}, u32[]{:S(2)}) collective-permute-start(f32[6,9,512]{2,1,0:T(8,128)S(1)} %pad_maximum_fusion.4), channel_id=1, source_target_pairs={{0,3},{1,0},{2,1},{3,2},{4,7},{5,4},{6,5},{7,6},{8,11},{9,8},{10,9... | collective-permute-start | bytes 331784 | tf_op jit(solution)/shard_map/ppermute | solution.py:18
  38.1 1.9 %collective-permute-start.2 = (f32[6,9,512]{2,1,0:T(8,128)S(1)}, f32[6,9,512]{2,1,0:T(8,128)S(1)}, u32[]{:S(2)}, u32[]{:S(2)}) collective-permute-start(f32[6,9,512]{2,1,0:T(8,128)S(1)} %pad_maximum_fusion.2), channel_id=1, source_target_pairs={{0,1},{1,2},{2,3},{3,0},{4,5},{5,6},{6,7},{7,4},{8,9},{9,10},{10,1... | collective-permute-start | bytes 331784 | tf_op jit(solution)/shard_map/ppermute | solution.py:18
  40.0 0.6 add_convert_fusion.flag_ref
  40.6 0.0 collective-permute-done.3.lown_ref
  40.6 0.0 collective-permute-done.5.hown_ref
  40.6 0.0 copy-start.4
  40.6 1.4 %collective-permute-done.4.hend_ref = f32[6,9,512]{2,1,0:T(8,128)S(1)} collective-permute-done((f32[6,9,512]{2,1,0:T(8,128)S(1)}, f32[6,9,512]{2,1,0:T(8,128)S(1)}, u32[]{:S(2)}, u32[]{:S(2)}) %collective-permute-start.4) | collective-permute-done | bytes 110624 | tf_op jit(solution)/shard_map/ppermute | solution.py:18
  42.0 4.5 %collective-permute-done.2.lend_ref = f32[6,9,512]{2,1,0:T(8,128)S(1)} collective-permute-done((f32[6,9,512]{2,1,0:T(8,128)S(1)}, f32[6,9,512]{2,1,0:T(8,128)S(1)}, u32[]{:S(2)}, u32[]{:S(2)}) %collective-permute-start.2) | collective-permute-done | bytes 110624 | tf_op jit(solution)/shard_map/ppermute | solution.py:18
  46.6 0.0 copy-done.1
  46.6 0.0 copy-done.2
  46.6 0.0 copy-done.3
  46.6 0.0 copy-done.4
  46.6 0.0 copy-done.5
  46.6 0.0 copy-start.6
  46.6 0.7 copy-done.6
  47.3 8.5 %shard_map.64 = (f32[3,16,16,512]{3,2,1,0:T(8,128)}, f32[336,512]{1,0:T(8,128)}) custom-call(s32[2]{0:T(128)} %eshift_ref.1, f32[2]{0:T(128)} %efrac_ref.1, s32[2]{0:T(128)} %add_convert_fusion.flag_ref, f32[3,16,16,512]{3,2,1,0:T(8,128)} %f_hbm.1, f32[3,16,16,512]{3,2,1,0:T(8,128)} %v_hbm.1, f32[6,16,512]{2,1,0:T(8,128)} %copy-done.1, ...), custom_call_target="tpu_custom_call" | custom-call | flops 15728640 | bytes 4718592 | tf_op jit(solution)/shard_map/pallas_call | solution.py:162
  55.8 2.1 %collective-permute-start.6 = (f32[336,512]{1,0:T(8,128)}, f32[336,512]{1,0:T(8,128)S(1)}, u32[]{:S(2)}, u32[]{:S(2)}) collective-permute-start(f32[336,512]{1,0:T(8,128)} %get-tuple-element.8), channel_id=1, source_target_pairs={{0,1},{1,2},{2,3},{3,0},{4,5},{5,6},{6,7},{7,4},{8,9},{9,10},{10,1... | collective-permute-start | bytes 2064392 | tf_op jit(solution)/shard_map/ppermute | solution.py:18
  57.9 3.6 %shard_map.65.part_hbm = f32[3,16,16,512]{3,2,1,0:T(8,128)} custom-call(s32[16]{0:T(128)} %shift_ref.3, f32[16]{0:T(128)} %frac_ref.3, f32[3,16,16,512]{3,2,1,0:T(8,128)} %get-tuple-element.7.u_ref.u_hbm), custom_call_target="tpu_custom_call" | custom-call | flops 1179648 | bytes 3145728 | tf_op jit(solution)/shard_map/pallas_call | solution.py:213
  61.5 14.8 %collective-permute-done.6.rec_hbm = f32[336,512]{1,0:T(8,128)S(1)} collective-permute-done((f32[336,512]{1,0:T(8,128)}, f32[336,512]{1,0:T(8,128)S(1)}, u32[]{:S(2)}, u32[]{:S(2)}) %collective-permute-start.6) | collective-permute-done | bytes 688160 | tf_op jit(solution)/shard_map/ppermute | solution.py:18
  76.3 0.8 %copy-done = f32[336,512]{1,0:T(8,128)} copy-done((f32[336,512]{1,0:T(8,128)}, f32[336,512]{1,0:T(8,128)S(1)}, u32[]{:S(2)}) %copy-start) | copy-done | bytes 688152
  77.1 4.1 %shard_map.66 = f32[3,16,16,512]{3,2,1,0:T(8,128)} custom-call(s32[16]{0:T(128)} %shift_ref.3, f32[16]{0:T(128)} %frac_ref.3, f32[3,16,16,512]{3,2,1,0:T(8,128)} %get-tuple-element.7.u_ref.u_hbm, f32[336,512]{1,0:T(8,128)} %copy-done, f32[3,16,16,512]{3,2,1,0:T(8,128)} %shard_map.65.part_hbm), custom_call_target="tpu_custom_call", output_to_operand_aliasing={{}: (4, {})} | custom-call | flops 516096 | bytes 2359296 | tf_op jit(solution)/shard_map/pallas_call | solution.py:258
  (15 shorter events, 0.2 us)
Async XLA Ops:
  3.2 37.4 %collective-permute-start.3 = (f32[6,16,512]{2,1,0:T(8,128)S(1)}, f32[6,16,512]{2,1,0:T(8,128)S(1)}, u32[]{:S(2)}, u32[]{:S(2)}) collective-permute-start(f32[6,16,512]{2,1,0:T(8,128)S(1)} %pad_maximum_fusion.3), channel_id=1, source_target_pairs={{0,1},{1,2},{2,3},{3,0},{4,5},{5,6},{6,7},{7,4},{8,9},{9,10},{10,1... | collective-permute-start | bytes 589832 | tf_op jit(solution)/shard_map/ppermute | solution.py:18
  9.1 16.6 %collective-permute-start = (f32[6,16,512]{2,1,0:T(8,128)S(1)}, f32[6,16,512]{2,1,0:T(8,128)S(1)}, u32[]{:S(2)}, u32[]{:S(2)}) collective-permute-start(f32[6,16,512]{2,1,0:T(8,128)S(1)} %pad_maximum_fusion), channel_id=1, source_target_pairs={{0,4},{4,8},{8,12},{12,16},{16,20},{20,24},{24,28},{28,32},{32,36}... | collective-permute-start | bytes 589832 | tf_op jit(solution)/shard_map/ppermute | solution.py:16
  19.7 14.4 %collective-permute-start.1 = (f32[6,16,512]{2,1,0:T(8,128)S(1)}, f32[6,16,512]{2,1,0:T(8,128)S(1)}, u32[]{:S(2)}, u32[]{:S(2)}) collective-permute-start(f32[6,16,512]{2,1,0:T(8,128)S(1)} %pad_maximum_fusion.1), channel_id=1, source_target_pairs={{0,508},{4,0},{8,4},{12,8},{16,12},{20,16},{24,20},{28,24},{32,28}... | collective-permute-start | bytes 589832 | tf_op jit(solution)/shard_map/ppermute | solution.py:16
  21.7 18.9 %collective-permute-start.5 = (f32[6,16,512]{2,1,0:T(8,128)S(1)}, f32[6,16,512]{2,1,0:T(8,128)S(1)}, u32[]{:S(2)}, u32[]{:S(2)}) collective-permute-start(f32[6,16,512]{2,1,0:T(8,128)S(1)} %pad_maximum_fusion.5), channel_id=1, source_target_pairs={{0,3},{1,0},{2,1},{3,2},{4,7},{5,4},{6,5},{7,6},{8,11},{9,8},{10,9... | collective-permute-start | bytes 589832 | tf_op jit(solution)/shard_map/ppermute | solution.py:18
  25.7 20.9 %copy-start.1 = (f32[6,16,512]{2,1,0:T(8,128)}, f32[6,16,512]{2,1,0:T(8,128)S(1)}, u32[]{:S(2)}) copy-start(f32[6,16,512]{2,1,0:T(8,128)S(1)} %collective-permute-done.xm_ref) | copy-start | bytes 589828
  34.1 12.5 %copy-start.2 = (f32[6,16,512]{2,1,0:T(8,128)}, f32[6,16,512]{2,1,0:T(8,128)S(1)}, u32[]{:S(2)}) copy-start(f32[6,16,512]{2,1,0:T(8,128)S(1)} %collective-permute-done.1.xp_ref) | copy-start | bytes 589828
  34.1 7.9 %collective-permute-start.4 = (f32[6,9,512]{2,1,0:T(8,128)S(1)}, f32[6,9,512]{2,1,0:T(8,128)S(1)}, u32[]{:S(2)}, u32[]{:S(2)}) collective-permute-start(f32[6,9,512]{2,1,0:T(8,128)S(1)} %pad_maximum_fusion.4), channel_id=1, source_target_pairs={{0,3},{1,0},{2,1},{3,2},{4,7},{5,4},{6,5},{7,6},{8,11},{9,8},{10,9... | collective-permute-start | bytes 331784 | tf_op jit(solution)/shard_map/ppermute | solution.py:18
  38.1 8.5 %collective-permute-start.2 = (f32[6,9,512]{2,1,0:T(8,128)S(1)}, f32[6,9,512]{2,1,0:T(8,128)S(1)}, u32[]{:S(2)}, u32[]{:S(2)}) collective-permute-start(f32[6,9,512]{2,1,0:T(8,128)S(1)} %pad_maximum_fusion.2), channel_id=1, source_target_pairs={{0,1},{1,2},{2,3},{3,0},{4,5},{5,6},{6,7},{7,4},{8,9},{9,10},{10,1... | collective-permute-start | bytes 331784 | tf_op jit(solution)/shard_map/ppermute | solution.py:18
  40.6 6.0 %copy-start.3 = (f32[6,16,512]{2,1,0:T(8,128)}, f32[6,16,512]{2,1,0:T(8,128)S(1)}, u32[]{:S(2)}) copy-start(f32[6,16,512]{2,1,0:T(8,128)S(1)} %collective-permute-done.3.lown_ref) | copy-start | bytes 589828
  40.6 6.0 %copy-start.4 = (f32[6,16,512]{2,1,0:T(8,128)}, f32[6,16,512]{2,1,0:T(8,128)S(1)}, u32[]{:S(2)}) copy-start(f32[6,16,512]{2,1,0:T(8,128)S(1)} %collective-permute-done.5.hown_ref) | copy-start | bytes 589828
  42.0 4.6 %copy-start.5 = (f32[6,9,512]{2,1,0:T(8,128)}, f32[6,9,512]{2,1,0:T(8,128)S(1)}, u32[]{:S(2)}) copy-start(f32[6,9,512]{2,1,0:T(8,128)S(1)} %collective-permute-done.4.hend_ref) | copy-start | bytes 331780
  46.6 0.7 copy-start.6
  55.8 20.5 %collective-permute-start.6 = (f32[336,512]{1,0:T(8,128)}, f32[336,512]{1,0:T(8,128)S(1)}, u32[]{:S(2)}, u32[]{:S(2)}) collective-permute-start(f32[336,512]{1,0:T(8,128)} %get-tuple-element.8), channel_id=1, source_target_pairs={{0,1},{1,2},{2,3},{3,0},{4,5},{5,6},{6,7},{7,4},{8,9},{9,10},{10,1... | collective-permute-start | bytes 2064392 | tf_op jit(solution)/shard_map/ppermute | solution.py:18
  76.3 0.8 %copy-start = (f32[336,512]{1,0:T(8,128)}, f32[336,512]{1,0:T(8,128)S(1)}, u32[]{:S(2)}) copy-start(f32[336,512]{1,0:T(8,128)S(1)} %collective-permute-done.6.rec_hbm) | copy-start | bytes 2064388

commit v11 on v6

--- a/solution.py
+++ b/solution.py
@@ -227,7 +227,8 @@
     nb = lax.axis_size("blocks")
     b = lax.axis_index("blocks")
 
-    xm = shifted(jnp.concatenate([field[:, nx - 1], velocity[:, nx - 1]], axis=0), 1, 0)
+    xm = shifted(jnp.concatenate([field[1:, nx - 1], velocity[:, nx - 1]], axis=0), 1, 0)
+    xm = jnp.concatenate([jnp.zeros_like(xm[:1]), xm], axis=0)
     xp = shifted(jnp.concatenate([field[:, 0], velocity[:, 0]], axis=0), -1, 0)
     own_low = jnp.concatenate([field[:, :, ny - 1], velocity[:, :, ny - 1]], axis=0)
     own_high = jnp.concatenate([field[:, :, 0], velocity[:, :, 0]], axis=0)

time: 81.7 us -> 85.3 us (1.044)
  local copies, waits for them, and re-layouts: 5.77 us -> 8.13 us
  waiting for transfers between devices: 32.7 us -> 34.8 us
  starting transfers between devices: 29.2 us -> 28.3 us
    ppermute x5, starting transfers between devices: 16.7 us -> 14.3 us  [shifted(): return lax.ppermute(x, 'phi', [(q, (q + dp) % nq) for q in range(nq)])]
    ppermute x2, waiting for transfers between devices: 8.36 us -> 9.96 us  [shifted(): return lax.ppermute(x, 'blocks', [(b, (b + db) % nb) for b in range(nb)])]
    ppermute x2, starting transfers between devices: 12.5 us -> 13.9 us  [shifted(): return lax.ppermute(x, 'blocks', [(b, (b + db) % nb) for b in range(nb)])]
    squeeze x1 -> x2, local copies, waits for them, and re-layouts: 1.07 us -> 1.86 us  [body(): xp = shifted(jnp.concatenate([field[:, 0], velocity[:, 0]], axis=0), -1, 0)]
  transfers between devices with their start and end apart: 7 -> 7, of which waited for: 4 -> 4; matrix products, arithmetic and copies ran while one was open for 2% -> 7% of each run, Pallas kernels for 0% -> 0%
where the time goes in v11:
time: 85.3 us; the launch traced here: 84.8 us
  waiting for transfers between devices  34.8 us (41%)
  starting transfers between devices  28.3 us (33%)
  Pallas kernels  12.6 us (15%)
  local copies, waits for them, and re-layouts  8.13 us (10%)
    ppermute x5, waiting for transfers between devices, shifted(): return lax.ppermute(x, 'phi', [(q, (q + dp) % nq) for q in range(nq)])  24.8 us
    ppermute x5, starting transfers between devices, shifted(): return lax.ppermute(x, 'phi', [(q, (q + dp) % nq) for q in range(nq)])  14.3 us
    ppermute x2, starting transfers between devices, shifted(): return lax.ppermute(x, 'blocks', [(b, (b + db) % nb) for b in range(nb)])  13.9 us
    ppermute x2, waiting for transfers between devices, shifted(): return lax.ppermute(x, 'blocks', [(b, (b + db) % nb) for b in range(nb)])  9.96 us
    pallas_call x1, Pallas kernels, ct_update(): pl.pallas_call(ct_kernel, out_shape=(jax.ShapeDtypeStruct((3, rows, ny, n...  8.48 us
    pallas_call x1, Pallas kernels, advect(): pl.pallas_call(advect_kernel, out_shape=jax.ShapeDtypeStruct(updated.shap...  4.14 us
    slice x2, local copies, waits for them, and re-layouts, body(): own_high = jnp.concatenate([field[:, :, 0], velocity[:, :, 0]], axis=0)  3.11 us
    squeeze x2, local copies, waits for them, and re-layouts, body(): xp = shifted(jnp.concatenate([field[:, 0], velocity[:, 0]], axis=0), -1, 0)  1.86 us
  transfers between devices with their start and end apart: 7, of which 4 were waited for; matrix products, arithmetic and copies ran while one was open for 7% of the time, Pallas kernels for 0%

profile of v11, /device:TPU:1, one launch (start us, length us, event | category | flops | bytes accessed | tf_op | source)
XLA Modules:
  0.0 84.8 jit_solution(8462146573709097819)
XLA Ops:
  0.0 0.8 slice_bitcast_fusion.3
  0.8 1.0 %slice_bitcast_fusion = (f32[3,16,512]{2,1,0:T(8,128)S(1)}, f32[3,16,512]{2,1,0:T(8,128)S(1)}) fusion(f32[3,16,16,512]{3,2,1,0:T(8,128)} %v_hbm.1), kind=kLoop, calls=%fused_computation.10 | loop fusion | bytes 393216 | tf_op jit(solution)/shard_map/squeeze | solution.py:232
  1.8 12.0 %collective-permute-start = (f32[5,16,512]{2,1,0:T(8,128)S(1)}, f32[5,16,512]{2,1,0:T(8,128)S(1)}, u32[]{:S(2)}, u32[]{:S(2)}) collective-permute-start(f32[5,16,512]{2,1,0:T(8,128)S(1)} %pad_maximum_fusion.5), channel_id=1, source_target_pairs={{0,4},{4,8},{8,12},{12,16},{16,20},{20,24},{24,28},{28,32},{32,36}... | collective-permute-start | bytes 491528 | tf_op jit(solution)/shard_map/ppermute | solution.py:16
  13.9 1.6 %fusion.1 = (f32[3,16,1,512]{3,2,1,0:T(1,128)S(1)}, f32[3,16,1,512]{3,2,1,0:T(1,128)S(1)}) fusion(f32[3,16,16,512]{3,2,1,0:T(8,128)} %v_hbm.1), kind=kLoop, calls=%fused_computation.18 | loop fusion | bytes 393216 | tf_op jit(solution)/shard_map/slice | solution.py:234
  15.4 1.6 %fusion = (f32[3,16,1,512]{3,2,1,0:T(1,128)S(1)}, f32[3,16,1,512]{3,2,1,0:T(1,128)S(1)}) fusion(f32[3,16,16,512]{3,2,1,0:T(8,128)} %f_hbm.1), kind=kLoop, calls=%fused_computation.17 | loop fusion | bytes 393216 | tf_op jit(solution)/shard_map/slice | solution.py:234
  17.0 3.1 %collective-permute-start.3 = (f32[6,16,512]{2,1,0:T(8,128)S(1)}, f32[6,16,512]{2,1,0:T(8,128)S(1)}, u32[]{:S(2)}, u32[]{:S(2)}) collective-permute-start(f32[6,16,512]{2,1,0:T(8,128)S(1)} %pad_maximum_fusion.2), channel_id=1, source_target_pairs={{0,1},{1,2},{2,3},{3,0},{4,5},{5,6},{6,7},{7,4},{8,9},{9,10},{10,1... | collective-permute-start | bytes 589832 | tf_op jit(solution)/shard_map/ppermute | solution.py:18
  20.2 4.0 %collective-permute-start.5 = (f32[6,16,512]{2,1,0:T(8,128)S(1)}, f32[6,16,512]{2,1,0:T(8,128)S(1)}, u32[]{:S(2)}, u32[]{:S(2)}) collective-permute-start(f32[6,16,512]{2,1,0:T(8,128)S(1)} %pad_maximum_fusion.4), channel_id=1, source_target_pairs={{0,3},{1,0},{2,1},{3,2},{4,7},{5,4},{6,5},{7,6},{8,11},{9,8},{10,9... | collective-permute-start | bytes 589832 | tf_op jit(solution)/shard_map/ppermute | solution.py:18
  24.2 0.9 %slice_bitcast_fusion.1 = f32[3,16,512]{2,1,0:T(8,128)S(1)} fusion(f32[3,16,16,512]{3,2,1,0:T(8,128)} %f_hbm.1), kind=kLoop, calls=%fused_computation.11 | loop fusion | bytes 196608 | tf_op jit(solution)/shard_map/squeeze | solution.py:232
  25.1 1.9 %collective-permute-start.1 = (f32[6,16,512]{2,1,0:T(8,128)S(1)}, f32[6,16,512]{2,1,0:T(8,128)S(1)}, u32[]{:S(2)}, u32[]{:S(2)}) collective-permute-start(f32[6,16,512]{2,1,0:T(8,128)S(1)} %pad_maximum_fusion), channel_id=1, source_target_pairs={{0,508},{4,0},{8,4},{12,8},{16,12},{20,16},{24,20},{28,24},{32,28}... | collective-permute-start | bytes 589832 | tf_op jit(solution)/shard_map/ppermute | solution.py:16
  27.0 0.0 collective-permute-done
  27.1 10.0 %collective-permute-done.1.xp_ref = f32[6,16,512]{2,1,0:T(8,128)S(1)} collective-permute-done((f32[6,16,512]{2,1,0:T(8,128)S(1)}, f32[6,16,512]{2,1,0:T(8,128)S(1)}, u32[]{:S(2)}, u32[]{:S(2)}) %collective-permute-start.1) | collective-permute-done | bytes 196640 | tf_op jit(solution)/shard_map/ppermute | solution.py:16
  37.0 0.0 copy-start.1
  37.1 2.5 %collective-permute-start.4 = (f32[6,9,512]{2,1,0:T(8,128)S(1)}, f32[6,9,512]{2,1,0:T(8,128)S(1)}, u32[]{:S(2)}, u32[]{:S(2)}) collective-permute-start(f32[6,9,512]{2,1,0:T(8,128)S(1)} %pad_maximum_fusion.3), channel_id=1, source_target_pairs={{0,3},{1,0},{2,1},{3,2},{4,7},{5,4},{6,5},{7,6},{8,11},{9,8},{10,9... | collective-permute-start | bytes 331784 | tf_op jit(solution)/shard_map/ppermute | solution.py:18
  39.6 2.7 %collective-permute-start.2 = (f32[6,9,512]{2,1,0:T(8,128)S(1)}, f32[6,9,512]{2,1,0:T(8,128)S(1)}, u32[]{:S(2)}, u32[]{:S(2)}) collective-permute-start(f32[6,9,512]{2,1,0:T(8,128)S(1)} %pad_maximum_fusion.1), channel_id=1, source_target_pairs={{0,1},{1,2},{2,3},{3,0},{4,5},{5,6},{6,7},{7,4},{8,9},{9,10},{10,1... | collective-permute-start | bytes 331784 | tf_op jit(solution)/shard_map/ppermute | solution.py:18
  42.4 0.7 add_convert_fusion.flag_ref
  43.1 0.7 concatenate.22.xm_ref
  43.8 0.0 collective-permute-done.3.lown_ref
  43.8 0.0 collective-permute-done.5.hown_ref
  43.8 0.0 copy-start.3
  43.8 1.8 %collective-permute-done.4.hend_ref = f32[6,9,512]{2,1,0:T(8,128)S(1)} collective-permute-done((f32[6,9,512]{2,1,0:T(8,128)S(1)}, f32[6,9,512]{2,1,0:T(8,128)S(1)}, u32[]{:S(2)}, u32[]{:S(2)}) %collective-permute-start.4) | collective-permute-done | bytes 110624 | tf_op jit(solution)/shard_map/ppermute | solution.py:18
  45.6 4.4 %collective-permute-done.2.lend_ref = f32[6,9,512]{2,1,0:T(8,128)S(1)} collective-permute-done((f32[6,9,512]{2,1,0:T(8,128)S(1)}, f32[6,9,512]{2,1,0:T(8,128)S(1)}, u32[]{:S(2)}, u32[]{:S(2)}) %collective-permute-start.2) | collective-permute-done | bytes 110624 | tf_op jit(solution)/shard_map/ppermute | solution.py:18
  50.1 0.0 copy-done.1
  50.1 0.0 copy-done.2
  50.1 0.0 copy-done.3
  50.1 0.0 copy-done.4
  50.1 0.0 copy-start.5
  50.1 0.7 copy-done.5
  50.8 8.5 %shard_map.64 = (f32[3,16,16,512]{3,2,1,0:T(8,128)}, f32[336,512]{1,0:T(8,128)}) custom-call(s32[2]{0:T(128)} %eshift_ref.1, f32[2]{0:T(128)} %efrac_ref.1, s32[2]{0:T(128)} %add_convert_fusion.flag_ref, f32[3,16,16,512]{3,2,1,0:T(8,128)} %f_hbm.1, f32[3,16,16,512]{3,2,1,0:T(8,128)} %v_hbm.1, f32[6,16,512]{2,1,0:T(8,128)} %concatenate.22.xm_ref, ...), custom_call_target="tpu_custom_call" | custom-call | flops 15728640 | bytes 4718592 | tf_op jit(solution)/shard_map/pallas_call | solution.py:162
  59.2 2.0 %collective-permute-start.6 = (f32[336,512]{1,0:T(8,128)}, f32[336,512]{1,0:T(8,128)S(1)}, u32[]{:S(2)}, u32[]{:S(2)}) collective-permute-start(f32[336,512]{1,0:T(8,128)} %get-tuple-element.8), channel_id=1, source_target_pairs={{0,1},{1,2},{2,3},{3,0},{4,5},{5,6},{6,7},{7,4},{8,9},{9,10},{10,1... | collective-permute-start | bytes 2064392 | tf_op jit(solution)/shard_map/ppermute | solution.py:18
  61.2 18.5 %collective-permute-done.6.rec_ref = f32[336,512]{1,0:T(8,128)S(1)} collective-permute-done((f32[336,512]{1,0:T(8,128)}, f32[336,512]{1,0:T(8,128)S(1)}, u32[]{:S(2)}, u32[]{:S(2)}) %collective-permute-start.6) | collective-permute-done | bytes 688160 | tf_op jit(solution)/shard_map/ppermute | solution.py:18
  79.8 0.8 %copy-done = f32[336,512]{1,0:T(8,128)} copy-done((f32[336,512]{1,0:T(8,128)}, f32[336,512]{1,0:T(8,128)S(1)}, u32[]{:S(2)}) %copy-start) | copy-done | bytes 688152
  80.6 4.1 %shard_map.65 = f32[3,16,16,512]{3,2,1,0:T(8,128)} custom-call(s32[16]{0:T(128)} %shift_ref.1, f32[16]{0:T(128)} %frac_ref.1, f32[3,16,16,512]{3,2,1,0:T(8,128)} %get-tuple-element.7.u_ref, f32[336,512]{1,0:T(8,128)} %copy-done), custom_call_target="tpu_custom_call" | custom-call | flops 1179648 | bytes 3833856 | tf_op jit(solution)/shard_map/pallas_call | solution.py:212
  (15 shorter events, 0.2 us)
Async XLA Ops:
  1.8 25.2 %collective-permute-start = (f32[5,16,512]{2,1,0:T(8,128)S(1)}, f32[5,16,512]{2,1,0:T(8,128)S(1)}, u32[]{:S(2)}, u32[]{:S(2)}) collective-permute-start(f32[5,16,512]{2,1,0:T(8,128)S(1)} %pad_maximum_fusion.5), channel_id=1, source_target_pairs={{0,4},{4,8},{8,12},{12,16},{16,20},{20,24},{24,28},{28,32},{32,36}... | collective-permute-start | bytes 491528 | tf_op jit(solution)/shard_map/ppermute | solution.py:16
  17.0 26.8 %collective-permute-start.3 = (f32[6,16,512]{2,1,0:T(8,128)S(1)}, f32[6,16,512]{2,1,0:T(8,128)S(1)}, u32[]{:S(2)}, u32[]{:S(2)}) collective-permute-start(f32[6,16,512]{2,1,0:T(8,128)S(1)} %pad_maximum_fusion.2), channel_id=1, source_target_pairs={{0,1},{1,2},{2,3},{3,0},{4,5},{5,6},{6,7},{7,4},{8,9},{9,10},{10,1... | collective-permute-start | bytes 589832 | tf_op jit(solution)/shard_map/ppermute | solution.py:18
  20.2 23.6 %collective-permute-start.5 = (f32[6,16,512]{2,1,0:T(8,128)S(1)}, f32[6,16,512]{2,1,0:T(8,128)S(1)}, u32[]{:S(2)}, u32[]{:S(2)}) collective-permute-start(f32[6,16,512]{2,1,0:T(8,128)S(1)} %pad_maximum_fusion.4), channel_id=1, source_target_pairs={{0,3},{1,0},{2,1},{3,2},{4,7},{5,4},{6,5},{7,6},{8,11},{9,8},{10,9... | collective-permute-start | bytes 589832 | tf_op jit(solution)/shard_map/ppermute | solution.py:18
  25.1 11.9 %collective-permute-start.1 = (f32[6,16,512]{2,1,0:T(8,128)S(1)}, f32[6,16,512]{2,1,0:T(8,128)S(1)}, u32[]{:S(2)}, u32[]{:S(2)}) collective-permute-start(f32[6,16,512]{2,1,0:T(8,128)S(1)} %pad_maximum_fusion), channel_id=1, source_target_pairs={{0,508},{4,0},{8,4},{12,8},{16,12},{20,16},{24,20},{28,24},{32,28}... | collective-permute-start | bytes 589832 | tf_op jit(solution)/shard_map/ppermute | solution.py:16
  37.0 13.0 %copy-start.1 = (f32[6,16,512]{2,1,0:T(8,128)}, f32[6,16,512]{2,1,0:T(8,128)S(1)}, u32[]{:S(2)}) copy-start(f32[6,16,512]{2,1,0:T(8,128)S(1)} %collective-permute-done.1.xp_ref) | copy-start | bytes 589828
  37.1 8.6 %collective-permute-start.4 = (f32[6,9,512]{2,1,0:T(8,128)S(1)}, f32[6,9,512]{2,1,0:T(8,128)S(1)}, u32[]{:S(2)}, u32[]{:S(2)}) collective-permute-start(f32[6,9,512]{2,1,0:T(8,128)S(1)} %pad_maximum_fusion.3), channel_id=1, source_target_pairs={{0,3},{1,0},{2,1},{3,2},{4,7},{5,4},{6,5},{7,6},{8,11},{9,8},{10,9... | collective-permute-start | bytes 331784 | tf_op jit(solution)/shard_map/ppermute | solution.py:18
  39.6 10.4 %collective-permute-start.2 = (f32[6,9,512]{2,1,0:T(8,128)S(1)}, f32[6,9,512]{2,1,0:T(8,128)S(1)}, u32[]{:S(2)}, u32[]{:S(2)}) collective-permute-start(f32[6,9,512]{2,1,0:T(8,128)S(1)} %pad_maximum_fusion.1), channel_id=1, source_target_pairs={{0,1},{1,2},{2,3},{3,0},{4,5},{5,6},{6,7},{7,4},{8,9},{9,10},{10,1... | collective-permute-start | bytes 331784 | tf_op jit(solution)/shard_map/ppermute | solution.py:18
  43.8 6.3 %copy-start.2 = (f32[6,16,512]{2,1,0:T(8,128)}, f32[6,16,512]{2,1,0:T(8,128)S(1)}, u32[]{:S(2)}) copy-start(f32[6,16,512]{2,1,0:T(8,128)S(1)} %collective-permute-done.3.lown_ref) | copy-start | bytes 589828
  43.8 6.3 %copy-start.3 = (f32[6,16,512]{2,1,0:T(8,128)}, f32[6,16,512]{2,1,0:T(8,128)S(1)}, u32[]{:S(2)}) copy-start(f32[6,16,512]{2,1,0:T(8,128)S(1)} %collective-permute-done.5.hown_ref) | copy-start | bytes 589828
  45.6 4.4 %copy-start.4 = (f32[6,9,512]{2,1,0:T(8,128)}, f32[6,9,512]{2,1,0:T(8,128)S(1)}, u32[]{:S(2)}) copy-start(f32[6,9,512]{2,1,0:T(8,128)S(1)} %collective-permute-done.4.hend_ref) | copy-start | bytes 331780
  50.1 0.7 copy-start.5
  59.2 20.5 %collective-permute-start.6 = (f32[336,512]{1,0:T(8,128)}, f32[336,512]{1,0:T(8,128)S(1)}, u32[]{:S(2)}, u32[]{:S(2)}) collective-permute-start(f32[336,512]{1,0:T(8,128)} %get-tuple-element.8), channel_id=1, source_target_pairs={{0,1},{1,2},{2,3},{3,0},{4,5},{5,6},{6,7},{7,4},{8,9},{9,10},{10,1... | collective-permute-start | bytes 2064392 | tf_op jit(solution)/shard_map/ppermute | solution.py:18
  79.8 0.9 %copy-start = (f32[336,512]{1,0:T(8,128)}, f32[336,512]{1,0:T(8,128)S(1)}, u32[]{:S(2)}) copy-start(f32[336,512]{1,0:T(8,128)S(1)} %collective-permute-done.6.rec_ref) | copy-start | bytes 2064388

commit v12 on v6

--- a/solution.py
+++ b/solution.py
@@ -57,11 +57,13 @@
         pltpu.make_async_copy(f_hbm, p_ref.at[0:3, 1 : rows + 1, pl.ds(OFF + 1, ny)], sem.at[0]),
         pltpu.make_async_copy(v_hbm, p_ref.at[3:6, 1 : rows + 1, pl.ds(OFF + 1, ny)], sem.at[1]),
     ]
+    for a in range(rows):
+        copies.append(pltpu.make_async_copy(
+            lown_ref.at[:, pl.ds(a, 1), :], p_ref.at[:, a + 1, pl.ds(OFF, 1), :], sem.at[2 + 2 * a]))
+        copies.append(pltpu.make_async_copy(
+            hown_ref.at[:, pl.ds(a, 1), :], p_ref.at[:, a + 1, pl.ds(OFF + ny + 1, 1), :], sem.at[3 + 2 * a]))
     for c in copies:
         c.start()
-    for a in range(rows):
-        p_ref[:, a + 1, OFF, :] = lown_ref[:, a, :]
-        p_ref[:, a + 1, OFF + ny + 1, :] = hown_ref[:, a, :]
 
     line[:, pl.ds(0, WIDE), :] = lend_ref[:, pl.ds(0, WIDE), :]
     line[:, pl.ds(WIDE, ny), :] = xm_ref[...]
@@ -173,7 +175,7 @@
             pltpu.VMEM((rows + 1, ny, nz), jnp.float32),
             pltpu.VMEM((rows + 1, ny + 8, nz), jnp.float32),
             pltpu.VMEM((6, ny + WIDE + 8, nz), jnp.float32),
-            pltpu.SemaphoreType.DMA((2,)),
+            pltpu.SemaphoreType.DMA((2 + 2 * rows,)),
         ],
         cost_estimate=pl.CostEstimate(
             flops=120 * rows * ny * nz, transcendentals=0,

time: 81.7 us -> 82 us (level)
  no operation moved by 1% of the time
where the time goes in v12:
time: 82 us; the launch traced here: 81.6 us
  waiting for transfers between devices  32.7 us (40%)
  starting transfers between devices  29.2 us (36%)
  Pallas kernels  13 us (16%)
  local copies, waits for them, and re-layouts  5.77 us (7%)
    ppermute x5, waiting for transfers between devices, shifted(): return lax.ppermute(x, 'phi', [(q, (q + dp) % nq) for q in range(nq)])  24.3 us
    ppermute x5, starting transfers between devices, shifted(): return lax.ppermute(x, 'phi', [(q, (q + dp) % nq) for q in range(nq)])  16.7 us
    ppermute x2, starting transfers between devices, shifted(): return lax.ppermute(x, 'blocks', [(b, (b + db) % nb) for b in range(nb)])  12.5 us
    pallas_call x1, Pallas kernels, ct_update(): pl.pallas_call(ct_kernel, out_shape=(jax.ShapeDtypeStruct((3, rows, ny, n...  8.82 us
    ppermute x2, waiting for transfers between devices, shifted(): return lax.ppermute(x, 'blocks', [(b, (b + db) % nb) for b in range(nb)])  8.36 us
    pallas_call x1, Pallas kernels, advect(): pl.pallas_call(advect_kernel, out_shape=jax.ShapeDtypeStruct(updated.shap...  4.15 us
    slice x2, local copies, waits for them, and re-layouts, body(): own_high = jnp.concatenate([field[:, :, 0], velocity[:, :, 0]], axis=0)  3.1 us
  transfers between devices with their start and end apart: 7, of which 4 were waited for; matrix products, arithmetic and copies ran while one was open for 2% of the time, Pallas kernels for 0%

profile of v12, /device:TPU:1, one launch (start us, length us, event | category | flops | bytes accessed | tf_op | source)
XLA Modules:
  0.0 81.6 jit_solution(8092040338935142932)
XLA Ops:
  0.0 1.6 %fusion = (f32[3,16,1,512]{3,2,1,0:T(1,128)S(1)}, f32[3,16,1,512]{3,2,1,0:T(1,128)S(1)}) fusion(f32[3,16,16,512]{3,2,1,0:T(8,128)} %f_hbm.1), kind=kLoop, calls=%fused_computation.15 | loop fusion | bytes 393216 | tf_op jit(solution)/shard_map/slice | solution.py:235
  1.6 1.6 %fusion.1 = (f32[3,16,1,512]{3,2,1,0:T(1,128)S(1)}, f32[3,16,1,512]{3,2,1,0:T(1,128)S(1)}) fusion(f32[3,16,16,512]{3,2,1,0:T(8,128)} %v_hbm.1), kind=kLoop, calls=%fused_computation.16 | loop fusion | bytes 393216 | tf_op jit(solution)/shard_map/slice | solution.py:235
  3.2 4.8 %collective-permute-start.3 = (f32[6,16,512]{2,1,0:T(8,128)S(1)}, f32[6,16,512]{2,1,0:T(8,128)S(1)}, u32[]{:S(2)}, u32[]{:S(2)}) collective-permute-start(f32[6,16,512]{2,1,0:T(8,128)S(1)} %pad_maximum_fusion.3), channel_id=1, source_target_pairs={{0,1},{1,2},{2,3},{3,0},{4,5},{5,6},{6,7},{7,4},{8,9},{9,10},{10,1... | collective-permute-start | bytes 589832 | tf_op jit(solution)/shard_map/ppermute | solution.py:18
  8.0 1.1 %slice_bitcast_fusion = (f32[3,16,512]{2,1,0:T(8,128)S(1)}, f32[3,16,512]{2,1,0:T(8,128)S(1)}, f32[3,16,512]{2,1,0:T(8,128)S(1)}, f32[3,16,512]{2,1,0:T(8,128)S(1)}) fusion(f32[3,16,16,512]{3,2,1,0:T(8,128)} %v_hbm.1, f32[3,16,16,512]{3,2,1,0:T(8,128)} %f_hbm.1), kind=kLoop, calls=%fused_computation.10 | loop fusion | bytes 786432 | tf_op jit(solution)/shard_map/squeeze | solution.py:233
  9.1 10.6 %collective-permute-start = (f32[6,16,512]{2,1,0:T(8,128)S(1)}, f32[6,16,512]{2,1,0:T(8,128)S(1)}, u32[]{:S(2)}, u32[]{:S(2)}) collective-permute-start(f32[6,16,512]{2,1,0:T(8,128)S(1)} %pad_maximum_fusion), channel_id=1, source_target_pairs={{0,4},{4,8},{8,12},{12,16},{16,20},{20,24},{24,28},{28,32},{32,36}... | collective-permute-start | bytes 589832 | tf_op jit(solution)/shard_map/ppermute | solution.py:16
  19.7 1.9 %collective-permute-start.1 = (f32[6,16,512]{2,1,0:T(8,128)S(1)}, f32[6,16,512]{2,1,0:T(8,128)S(1)}, u32[]{:S(2)}, u32[]{:S(2)}) collective-permute-start(f32[6,16,512]{2,1,0:T(8,128)S(1)} %pad_maximum_fusion.1), channel_id=1, source_target_pairs={{0,508},{4,0},{8,4},{12,8},{16,12},{20,16},{24,20},{28,24},{32,28}... | collective-permute-start | bytes 589832 | tf_op jit(solution)/shard_map/ppermute | solution.py:16
  21.7 4.0 %collective-permute-start.5 = (f32[6,16,512]{2,1,0:T(8,128)S(1)}, f32[6,16,512]{2,1,0:T(8,128)S(1)}, u32[]{:S(2)}, u32[]{:S(2)}) collective-permute-start(f32[6,16,512]{2,1,0:T(8,128)S(1)} %pad_maximum_fusion.5), channel_id=1, source_target_pairs={{0,3},{1,0},{2,1},{3,2},{4,7},{5,4},{6,5},{7,6},{8,11},{9,8},{10,9... | collective-permute-start | bytes 589832 | tf_op jit(solution)/shard_map/ppermute | solution.py:18
  25.7 0.0 collective-permute-done.xm_ref
  25.7 0.0 copy-start.1
  25.7 8.4 %collective-permute-done.1.xp_ref = f32[6,16,512]{2,1,0:T(8,128)S(1)} collective-permute-done((f32[6,16,512]{2,1,0:T(8,128)S(1)}, f32[6,16,512]{2,1,0:T(8,128)S(1)}, u32[]{:S(2)}, u32[]{:S(2)}) %collective-permute-start.1) | collective-permute-done | bytes 196640 | tf_op jit(solution)/shard_map/ppermute | solution.py:16
  34.1 0.0 copy-start.2
  34.1 3.9 %collective-permute-start.4 = (f32[6,9,512]{2,1,0:T(8,128)S(1)}, f32[6,9,512]{2,1,0:T(8,128)S(1)}, u32[]{:S(2)}, u32[]{:S(2)}) collective-permute-start(f32[6,9,512]{2,1,0:T(8,128)S(1)} %pad_maximum_fusion.4), channel_id=1, source_target_pairs={{0,3},{1,0},{2,1},{3,2},{4,7},{5,4},{6,5},{7,6},{8,11},{9,8},{10,9... | collective-permute-start | bytes 331784 | tf_op jit(solution)/shard_map/ppermute | solution.py:18
  38.1 1.9 %collective-permute-start.2 = (f32[6,9,512]{2,1,0:T(8,128)S(1)}, f32[6,9,512]{2,1,0:T(8,128)S(1)}, u32[]{:S(2)}, u32[]{:S(2)}) collective-permute-start(f32[6,9,512]{2,1,0:T(8,128)S(1)} %pad_maximum_fusion.2), channel_id=1, source_target_pairs={{0,1},{1,2},{2,3},{3,0},{4,5},{5,6},{6,7},{7,4},{8,9},{9,10},{10,1... | collective-permute-start | bytes 331784 | tf_op jit(solution)/shard_map/ppermute | solution.py:18
  40.0 0.6 add_convert_fusion.flag_ref
  40.6 0.0 collective-permute-done.3.lown_ref
  40.6 0.0 copy-start.3
  40.6 0.0 collective-permute-done.5.hown_ref
  40.6 0.0 copy-start.4
  40.6 1.4 %collective-permute-done.4.hend_ref = f32[6,9,512]{2,1,0:T(8,128)S(1)} collective-permute-done((f32[6,9,512]{2,1,0:T(8,128)S(1)}, f32[6,9,512]{2,1,0:T(8,128)S(1)}, u32[]{:S(2)}, u32[]{:S(2)}) %collective-permute-start.4) | collective-permute-done | bytes 110624 | tf_op jit(solution)/shard_map/ppermute | solution.py:18
  42.0 4.5 %collective-permute-done.2.lend_ref = f32[6,9,512]{2,1,0:T(8,128)S(1)} collective-permute-done((f32[6,9,512]{2,1,0:T(8,128)S(1)}, f32[6,9,512]{2,1,0:T(8,128)S(1)}, u32[]{:S(2)}, u32[]{:S(2)}) %collective-permute-start.2) | collective-permute-done | bytes 110624 | tf_op jit(solution)/shard_map/ppermute | solution.py:18
  46.6 0.0 copy-done.1
  46.6 0.0 copy-done.2
  46.6 0.0 copy-done.3
  46.6 0.0 copy-done.4
  46.6 0.0 copy-done.5
  46.6 0.0 copy-start.6
  46.6 0.7 copy-done.6
  47.3 8.8 %shard_map.64 = (f32[3,16,16,512]{3,2,1,0:T(8,128)}, f32[336,512]{1,0:T(8,128)}) custom-call(s32[2]{0:T(128)} %eshift_ref.1, f32[2]{0:T(128)} %efrac_ref.1, s32[2]{0:T(128)} %add_convert_fusion.flag_ref, f32[3,16,16,512]{3,2,1,0:T(8,128)} %f_hbm.1, f32[3,16,16,512]{3,2,1,0:T(8,128)} %v_hbm.1, f32[6,16,512]{2,1,0:T(8,128)} %copy-done.1, ...), custom_call_target="tpu_custom_call" | custom-call | flops 15728640 | bytes 4718592 | tf_op jit(solution)/shard_map/pallas_call | solution.py:164
  56.1 2.1 %collective-permute-start.6 = (f32[336,512]{1,0:T(8,128)}, f32[336,512]{1,0:T(8,128)S(1)}, u32[]{:S(2)}, u32[]{:S(2)}) collective-permute-start(f32[336,512]{1,0:T(8,128)} %get-tuple-element.8), channel_id=1, source_target_pairs={{0,1},{1,2},{2,3},{3,0},{4,5},{5,6},{6,7},{7,4},{8,9},{9,10},{10,1... | collective-permute-start | bytes 2064392 | tf_op jit(solution)/shard_map/ppermute | solution.py:18
  58.2 18.4 %collective-permute-done.6.rec_ref = f32[336,512]{1,0:T(8,128)S(1)} collective-permute-done((f32[336,512]{1,0:T(8,128)}, f32[336,512]{1,0:T(8,128)S(1)}, u32[]{:S(2)}, u32[]{:S(2)}) %collective-permute-start.6) | collective-permute-done | bytes 688160 | tf_op jit(solution)/shard_map/ppermute | solution.py:18
  76.6 0.8 %copy-done = f32[336,512]{1,0:T(8,128)} copy-done((f32[336,512]{1,0:T(8,128)}, f32[336,512]{1,0:T(8,128)S(1)}, u32[]{:S(2)}) %copy-start) | copy-done | bytes 688152
  77.4 4.2 %shard_map.65 = f32[3,16,16,512]{3,2,1,0:T(8,128)} custom-call(s32[16]{0:T(128)} %shift_ref.1, f32[16]{0:T(128)} %frac_ref.1, f32[3,16,16,512]{3,2,1,0:T(8,128)} %get-tuple-element.7.u_ref, f32[336,512]{1,0:T(8,128)} %copy-done), custom_call_target="tpu_custom_call" | custom-call | flops 1179648 | bytes 3833856 | tf_op jit(solution)/shard_map/pallas_call | solution.py:214
  (14 shorter events, 0.2 us)
Async XLA Ops:
  3.2 37.5 %collective-permute-start.3 = (f32[6,16,512]{2,1,0:T(8,128)S(1)}, f32[6,16,512]{2,1,0:T(8,128)S(1)}, u32[]{:S(2)}, u32[]{:S(2)}) collective-permute-start(f32[6,16,512]{2,1,0:T(8,128)S(1)} %pad_maximum_fusion.3), channel_id=1, source_target_pairs={{0,1},{1,2},{2,3},{3,0},{4,5},{5,6},{6,7},{7,4},{8,9},{9,10},{10,1... | collective-permute-start | bytes 589832 | tf_op jit(solution)/shard_map/ppermute | solution.py:18
  9.1 16.6 %collective-permute-start = (f32[6,16,512]{2,1,0:T(8,128)S(1)}, f32[6,16,512]{2,1,0:T(8,128)S(1)}, u32[]{:S(2)}, u32[]{:S(2)}) collective-permute-start(f32[6,16,512]{2,1,0:T(8,128)S(1)} %pad_maximum_fusion), channel_id=1, source_target_pairs={{0,4},{4,8},{8,12},{12,16},{16,20},{20,24},{24,28},{28,32},{32,36}... | collective-permute-start | bytes 589832 | tf_op jit(solution)/shard_map/ppermute | solution.py:16
  19.7 14.4 %collective-permute-start.1 = (f32[6,16,512]{2,1,0:T(8,128)S(1)}, f32[6,16,512]{2,1,0:T(8,128)S(1)}, u32[]{:S(2)}, u32[]{:S(2)}) collective-permute-start(f32[6,16,512]{2,1,0:T(8,128)S(1)} %pad_maximum_fusion.1), channel_id=1, source_target_pairs={{0,508},{4,0},{8,4},{12,8},{16,12},{20,16},{24,20},{28,24},{32,28}... | collective-permute-start | bytes 589832 | tf_op jit(solution)/shard_map/ppermute | solution.py:16
  21.7 19.0 %collective-permute-start.5 = (f32[6,16,512]{2,1,0:T(8,128)S(1)}, f32[6,16,512]{2,1,0:T(8,128)S(1)}, u32[]{:S(2)}, u32[]{:S(2)}) collective-permute-start(f32[6,16,512]{2,1,0:T(8,128)S(1)} %pad_maximum_fusion.5), channel_id=1, source_target_pairs={{0,3},{1,0},{2,1},{3,2},{4,7},{5,4},{6,5},{7,6},{8,11},{9,8},{10,9... | collective-permute-start | bytes 589832 | tf_op jit(solution)/shard_map/ppermute | solution.py:18
  25.7 20.9 %copy-start.1 = (f32[6,16,512]{2,1,0:T(8,128)}, f32[6,16,512]{2,1,0:T(8,128)S(1)}, u32[]{:S(2)}) copy-start(f32[6,16,512]{2,1,0:T(8,128)S(1)} %collective-permute-done.xm_ref) | copy-start | bytes 589828
  34.1 12.5 %copy-start.2 = (f32[6,16,512]{2,1,0:T(8,128)}, f32[6,16,512]{2,1,0:T(8,128)S(1)}, u32[]{:S(2)}) copy-start(f32[6,16,512]{2,1,0:T(8,128)S(1)} %collective-permute-done.1.xp_ref) | copy-start | bytes 589828
  34.1 7.9 %collective-permute-start.4 = (f32[6,9,512]{2,1,0:T(8,128)S(1)}, f32[6,9,512]{2,1,0:T(8,128)S(1)}, u32[]{:S(2)}, u32[]{:S(2)}) collective-permute-start(f32[6,9,512]{2,1,0:T(8,128)S(1)} %pad_maximum_fusion.4), channel_id=1, source_target_pairs={{0,3},{1,0},{2,1},{3,2},{4,7},{5,4},{6,5},{7,6},{8,11},{9,8},{10,9... | collective-permute-start | bytes 331784 | tf_op jit(solution)/shard_map/ppermute | solution.py:18
  38.1 8.5 %collective-permute-start.2 = (f32[6,9,512]{2,1,0:T(8,128)S(1)}, f32[6,9,512]{2,1,0:T(8,128)S(1)}, u32[]{:S(2)}, u32[]{:S(2)}) collective-permute-start(f32[6,9,512]{2,1,0:T(8,128)S(1)} %pad_maximum_fusion.2), channel_id=1, source_target_pairs={{0,1},{1,2},{2,3},{3,0},{4,5},{5,6},{6,7},{7,4},{8,9},{9,10},{10,1... | collective-permute-start | bytes 331784 | tf_op jit(solution)/shard_map/ppermute | solution.py:18
  40.6 5.9 %copy-start.3 = (f32[6,16,512]{2,1,0:T(8,128)}, f32[6,16,512]{2,1,0:T(8,128)S(1)}, u32[]{:S(2)}) copy-start(f32[6,16,512]{2,1,0:T(8,128)S(1)} %collective-permute-done.3.lown_ref) | copy-start | bytes 589828
  40.6 5.9 %copy-start.4 = (f32[6,16,512]{2,1,0:T(8,128)}, f32[6,16,512]{2,1,0:T(8,128)S(1)}, u32[]{:S(2)}) copy-start(f32[6,16,512]{2,1,0:T(8,128)S(1)} %collective-permute-done.5.hown_ref) | copy-start | bytes 589828
  42.0 4.6 %copy-start.5 = (f32[6,9,512]{2,1,0:T(8,128)}, f32[6,9,512]{2,1,0:T(8,128)S(1)}, u32[]{:S(2)}) copy-start(f32[6,9,512]{2,1,0:T(8,128)S(1)} %collective-permute-done.4.hend_ref) | copy-start | bytes 331780
  46.6 0.7 copy-start.6
  56.1 20.5 %collective-permute-start.6 = (f32[336,512]{1,0:T(8,128)}, f32[336,512]{1,0:T(8,128)S(1)}, u32[]{:S(2)}, u32[]{:S(2)}) collective-permute-start(f32[336,512]{1,0:T(8,128)} %get-tuple-element.8), channel_id=1, source_target_pairs={{0,1},{1,2},{2,3},{3,0},{4,5},{5,6},{6,7},{7,4},{8,9},{9,10},{10,1... | collective-permute-start | bytes 2064392 | tf_op jit(solution)/shard_map/ppermute | solution.py:18
  76.6 0.8 %copy-start = (f32[336,512]{1,0:T(8,128)}, f32[336,512]{1,0:T(8,128)S(1)}, u32[]{:S(2)}) copy-start(f32[336,512]{1,0:T(8,128)S(1)} %collective-permute-done.6.rec_ref) | copy-start | bytes 2064388

commit v13 on v6

--- a/solution.py
+++ b/solution.py
@@ -182,14 +182,19 @@
     )(eshift, efrac, flags, field, velocity, xm, xp, *low_in, *high_in)
 
 
-def advect_kernel(shift_ref, frac_ref, u_ref, rec_ref, o_ref, ext):
-    rows, ny = u_ref.shape[1], u_ref.shape[2]
+def advect_kernel(shift_ref, frac_ref, u_hbm, rec_hbm, o_ref, ext, rec_ref, sem):
+    rows, ny = u_hbm.shape[1], u_hbm.shape[2]
     lead = 8
     keep = KMAX + 1
+    body_copy = pltpu.make_async_copy(u_hbm, ext.at[:, :, pl.ds(lead, ny), :], sem.at[0])
+    rec_copy = pltpu.make_async_copy(rec_hbm, rec_ref, sem.at[1])
+    body_copy.start()
+    rec_copy.start()
+    rec_copy.wait()
     for c in range(3):
         for x in range(rows):
             ext[c, x, pl.ds(lead - keep, keep), :] = rec_ref[pl.ds((c * rows + x) * keep, keep), :]
-    ext[:, :, pl.ds(lead, ny), :] = u_ref[...]
+    body_copy.wait()
 
     def strip(x, carry):
         s = shift_ref[x]
@@ -209,12 +214,17 @@
     _, rows, ny, nz = updated.shape
     vmem = pl.BlockSpec(memory_space=pltpu.VMEM)
     smem = pl.BlockSpec(memory_space=pltpu.SMEM)
+    hbm = pl.BlockSpec(memory_space=pl.ANY)
     return pl.pallas_call(
         advect_kernel,
         out_shape=jax.ShapeDtypeStruct(updated.shape, updated.dtype),
-        in_specs=[smem, smem, vmem, vmem],
+        in_specs=[smem, smem, hbm, hbm],
         out_specs=vmem,
-        scratch_shapes=[pltpu.VMEM((3, rows, ny + 8, nz), jnp.float32)],
+        scratch_shapes=[
+            pltpu.VMEM((3, rows, ny + 8, nz), jnp.float32),
+            pltpu.VMEM(received.shape, jnp.float32),
+            pltpu.SemaphoreType.DMA((2,)),
+        ],
         cost_estimate=pl.CostEstimate(
             flops=3 * 3 * rows * ny * nz, transcendentals=0,
             bytes_accessed=4 * 3 * rows * (2 * ny + KMAX + 1) * nz,

time: 81.7 us -> 82.3 us (level)
  no operation moved by 1% of the time
where the time goes in v13:
time: 82.3 us; the launch traced here: 81.8 us
  waiting for transfers between devices  32.7 us (40%)
  starting transfers between devices  29.2 us (35%)
  Pallas kernels  13.2 us (16%)
  local copies, waits for them, and re-layouts  5.77 us (7%)
    ppermute x5, waiting for transfers between devices, shifted(): return lax.ppermute(x, 'phi', [(q, (q + dp) % nq) for q in range(nq)])  24.3 us
    ppermute x5, starting transfers between devices, shifted(): return lax.ppermute(x, 'phi', [(q, (q + dp) % nq) for q in range(nq)])  16.7 us
    ppermute x2, starting transfers between devices, shifted(): return lax.ppermute(x, 'blocks', [(b, (b + db) % nb) for b in range(nb)])  12.5 us
    pallas_call x1, Pallas kernels, ct_update(): pl.pallas_call(ct_kernel, out_shape=(jax.ShapeDtypeStruct((3, rows, ny, n...  8.48 us
    ppermute x2, waiting for transfers between devices, shifted(): return lax.ppermute(x, 'blocks', [(b, (b + db) % nb) for b in range(nb)])  8.36 us
    pallas_call x1, Pallas kernels, advect(): pl.pallas_call(advect_kernel, out_shape=jax.ShapeDtypeStruct(updated.shap...  4.73 us
    slice x2, local copies, waits for them, and re-layouts, body(): own_high = jnp.concatenate([field[:, :, 0], velocity[:, :, 0]], axis=0)  3.1 us
  transfers between devices with their start and end apart: 7, of which 4 were waited for; matrix products, arithmetic and copies ran while one was open for 2% of the time, Pallas kernels for 0%

profile of v13, /device:TPU:1, one launch (start us, length us, event | category | flops | bytes accessed | tf_op | source)
XLA Modules:
  0.0 81.8 jit_solution(6328625609906690112)
XLA Ops:
  0.0 1.6 %fusion = (f32[3,16,1,512]{3,2,1,0:T(1,128)S(1)}, f32[3,16,1,512]{3,2,1,0:T(1,128)S(1)}) fusion(f32[3,16,16,512]{3,2,1,0:T(8,128)} %f_hbm.1), kind=kLoop, calls=%fused_computation.15 | loop fusion | bytes 393216 | tf_op jit(solution)/shard_map/slice | solution.py:243
  1.6 1.6 %fusion.1 = (f32[3,16,1,512]{3,2,1,0:T(1,128)S(1)}, f32[3,16,1,512]{3,2,1,0:T(1,128)S(1)}) fusion(f32[3,16,16,512]{3,2,1,0:T(8,128)} %v_hbm.1), kind=kLoop, calls=%fused_computation.16 | loop fusion | bytes 393216 | tf_op jit(solution)/shard_map/slice | solution.py:243
  3.2 4.8 %collective-permute-start.3 = (f32[6,16,512]{2,1,0:T(8,128)S(1)}, f32[6,16,512]{2,1,0:T(8,128)S(1)}, u32[]{:S(2)}, u32[]{:S(2)}) collective-permute-start(f32[6,16,512]{2,1,0:T(8,128)S(1)} %pad_maximum_fusion.3), channel_id=1, source_target_pairs={{0,1},{1,2},{2,3},{3,0},{4,5},{5,6},{6,7},{7,4},{8,9},{9,10},{10,1... | collective-permute-start | bytes 589832 | tf_op jit(solution)/shard_map/ppermute | solution.py:18
  8.0 1.1 %slice_bitcast_fusion = (f32[3,16,512]{2,1,0:T(8,128)S(1)}, f32[3,16,512]{2,1,0:T(8,128)S(1)}, f32[3,16,512]{2,1,0:T(8,128)S(1)}, f32[3,16,512]{2,1,0:T(8,128)S(1)}) fusion(f32[3,16,16,512]{3,2,1,0:T(8,128)} %v_hbm.1, f32[3,16,16,512]{3,2,1,0:T(8,128)} %f_hbm.1), kind=kLoop, calls=%fused_computation.10 | loop fusion | bytes 786432 | tf_op jit(solution)/shard_map/squeeze | solution.py:241
  9.1 10.6 %collective-permute-start = (f32[6,16,512]{2,1,0:T(8,128)S(1)}, f32[6,16,512]{2,1,0:T(8,128)S(1)}, u32[]{:S(2)}, u32[]{:S(2)}) collective-permute-start(f32[6,16,512]{2,1,0:T(8,128)S(1)} %pad_maximum_fusion), channel_id=1, source_target_pairs={{0,4},{4,8},{8,12},{12,16},{16,20},{20,24},{24,28},{28,32},{32,36}... | collective-permute-start | bytes 589832 | tf_op jit(solution)/shard_map/ppermute | solution.py:16
  19.7 1.9 %collective-permute-start.1 = (f32[6,16,512]{2,1,0:T(8,128)S(1)}, f32[6,16,512]{2,1,0:T(8,128)S(1)}, u32[]{:S(2)}, u32[]{:S(2)}) collective-permute-start(f32[6,16,512]{2,1,0:T(8,128)S(1)} %pad_maximum_fusion.1), channel_id=1, source_target_pairs={{0,508},{4,0},{8,4},{12,8},{16,12},{20,16},{24,20},{28,24},{32,28}... | collective-permute-start | bytes 589832 | tf_op jit(solution)/shard_map/ppermute | solution.py:16
  21.7 4.0 %collective-permute-start.5 = (f32[6,16,512]{2,1,0:T(8,128)S(1)}, f32[6,16,512]{2,1,0:T(8,128)S(1)}, u32[]{:S(2)}, u32[]{:S(2)}) collective-permute-start(f32[6,16,512]{2,1,0:T(8,128)S(1)} %pad_maximum_fusion.5), channel_id=1, source_target_pairs={{0,3},{1,0},{2,1},{3,2},{4,7},{5,4},{6,5},{7,6},{8,11},{9,8},{10,9... | collective-permute-start | bytes 589832 | tf_op jit(solution)/shard_map/ppermute | solution.py:18
  25.7 0.0 collective-permute-done.xm_ref
  25.7 0.0 copy-start.1
  25.7 8.4 %collective-permute-done.1.xp_ref = f32[6,16,512]{2,1,0:T(8,128)S(1)} collective-permute-done((f32[6,16,512]{2,1,0:T(8,128)S(1)}, f32[6,16,512]{2,1,0:T(8,128)S(1)}, u32[]{:S(2)}, u32[]{:S(2)}) %collective-permute-start.1) | collective-permute-done | bytes 196640 | tf_op jit(solution)/shard_map/ppermute | solution.py:16
  34.1 0.0 copy-start.2
  34.1 3.9 %collective-permute-start.4 = (f32[6,9,512]{2,1,0:T(8,128)S(1)}, f32[6,9,512]{2,1,0:T(8,128)S(1)}, u32[]{:S(2)}, u32[]{:S(2)}) collective-permute-start(f32[6,9,512]{2,1,0:T(8,128)S(1)} %pad_maximum_fusion.4), channel_id=1, source_target_pairs={{0,3},{1,0},{2,1},{3,2},{4,7},{5,4},{6,5},{7,6},{8,11},{9,8},{10,9... | collective-permute-start | bytes 331784 | tf_op jit(solution)/shard_map/ppermute | solution.py:18
  38.1 1.9 %collective-permute-start.2 = (f32[6,9,512]{2,1,0:T(8,128)S(1)}, f32[6,9,512]{2,1,0:T(8,128)S(1)}, u32[]{:S(2)}, u32[]{:S(2)}) collective-permute-start(f32[6,9,512]{2,1,0:T(8,128)S(1)} %pad_maximum_fusion.2), channel_id=1, source_target_pairs={{0,1},{1,2},{2,3},{3,0},{4,5},{5,6},{6,7},{7,4},{8,9},{9,10},{10,1... | collective-permute-start | bytes 331784 | tf_op jit(solution)/shard_map/ppermute | solution.py:18
  40.0 0.6 add_convert_fusion.flag_ref
  40.6 0.0 collective-permute-done.3.lown_ref
  40.6 0.0 copy-start.3
  40.6 0.0 collective-permute-done.5.hown_ref
  40.6 0.0 copy-start.4
  40.6 1.4 %collective-permute-done.4.hend_ref = f32[6,9,512]{2,1,0:T(8,128)S(1)} collective-permute-done((f32[6,9,512]{2,1,0:T(8,128)S(1)}, f32[6,9,512]{2,1,0:T(8,128)S(1)}, u32[]{:S(2)}, u32[]{:S(2)}) %collective-permute-start.4) | collective-permute-done | bytes 110624 | tf_op jit(solution)/shard_map/ppermute | solution.py:18
  42.0 4.5 %collective-permute-done.2.lend_ref = f32[6,9,512]{2,1,0:T(8,128)S(1)} collective-permute-done((f32[6,9,512]{2,1,0:T(8,128)S(1)}, f32[6,9,512]{2,1,0:T(8,128)S(1)}, u32[]{:S(2)}, u32[]{:S(2)}) %collective-permute-start.2) | collective-permute-done | bytes 110624 | tf_op jit(solution)/shard_map/ppermute | solution.py:18
  46.6 0.0 copy-done.1
  46.6 0.0 copy-done.2
  46.6 0.0 copy-done.3
  46.6 0.0 copy-done.4
  46.6 0.0 copy-done.5
  46.6 0.0 copy-start.6
  46.6 0.7 copy-done.6
  47.3 8.5 %shard_map.64 = (f32[3,16,16,512]{3,2,1,0:T(8,128)}, f32[336,512]{1,0:T(8,128)}) custom-call(s32[2]{0:T(128)} %eshift_ref.1, f32[2]{0:T(128)} %efrac_ref.1, s32[2]{0:T(128)} %add_convert_fusion.flag_ref, f32[3,16,16,512]{3,2,1,0:T(8,128)} %f_hbm.1, f32[3,16,16,512]{3,2,1,0:T(8,128)} %v_hbm.1, f32[6,16,512]{2,1,0:T(8,128)} %copy-done.1, ...), custom_call_target="tpu_custom_call" | custom-call | flops 15728640 | bytes 4718592 | tf_op jit(solution)/shard_map/pallas_call | solution.py:162
  55.8 2.1 %collective-permute-start.6 = (f32[336,512]{1,0:T(8,128)}, f32[336,512]{1,0:T(8,128)S(1)}, u32[]{:S(2)}, u32[]{:S(2)}) collective-permute-start(f32[336,512]{1,0:T(8,128)} %get-tuple-element.8), channel_id=1, source_target_pairs={{0,1},{1,2},{2,3},{3,0},{4,5},{5,6},{6,7},{7,4},{8,9},{9,10},{10,1... | collective-permute-start | bytes 2064392 | tf_op jit(solution)/shard_map/ppermute | solution.py:18
  57.9 18.4 %collective-permute-done.6.rec_hbm = f32[336,512]{1,0:T(8,128)S(1)} collective-permute-done((f32[336,512]{1,0:T(8,128)}, f32[336,512]{1,0:T(8,128)S(1)}, u32[]{:S(2)}, u32[]{:S(2)}) %collective-permute-start.6) | collective-permute-done | bytes 688160 | tf_op jit(solution)/shard_map/ppermute | solution.py:18
  76.3 0.8 %copy-done = f32[336,512]{1,0:T(8,128)} copy-done((f32[336,512]{1,0:T(8,128)}, f32[336,512]{1,0:T(8,128)S(1)}, u32[]{:S(2)}) %copy-start) | copy-done | bytes 688152
  77.1 4.7 %shard_map.65 = f32[3,16,16,512]{3,2,1,0:T(8,128)} custom-call(s32[16]{0:T(128)} %shift_ref.1, f32[16]{0:T(128)} %frac_ref.1, f32[3,16,16,512]{3,2,1,0:T(8,128)} %get-tuple-element.7.u_hbm, f32[336,512]{1,0:T(8,128)} %copy-done), custom_call_target="tpu_custom_call" | custom-call | flops 1179648 | bytes 3833856 | tf_op jit(solution)/shard_map/pallas_call | solution.py:218
  (14 shorter events, 0.2 us)
Async XLA Ops:
  3.2 37.5 %collective-permute-start.3 = (f32[6,16,512]{2,1,0:T(8,128)S(1)}, f32[6,16,512]{2,1,0:T(8,128)S(1)}, u32[]{:S(2)}, u32[]{:S(2)}) collective-permute-start(f32[6,16,512]{2,1,0:T(8,128)S(1)} %pad_maximum_fusion.3), channel_id=1, source_target_pairs={{0,1},{1,2},{2,3},{3,0},{4,5},{5,6},{6,7},{7,4},{8,9},{9,10},{10,1... | collective-permute-start | bytes 589832 | tf_op jit(solution)/shard_map/ppermute | solution.py:18
  9.1 16.6 %collective-permute-start = (f32[6,16,512]{2,1,0:T(8,128)S(1)}, f32[6,16,512]{2,1,0:T(8,128)S(1)}, u32[]{:S(2)}, u32[]{:S(2)}) collective-permute-start(f32[6,16,512]{2,1,0:T(8,128)S(1)} %pad_maximum_fusion), channel_id=1, source_target_pairs={{0,4},{4,8},{8,12},{12,16},{16,20},{20,24},{24,28},{28,32},{32,36}... | collective-permute-start | bytes 589832 | tf_op jit(solution)/shard_map/ppermute | solution.py:16
  19.7 14.4 %collective-permute-start.1 = (f32[6,16,512]{2,1,0:T(8,128)S(1)}, f32[6,16,512]{2,1,0:T(8,128)S(1)}, u32[]{:S(2)}, u32[]{:S(2)}) collective-permute-start(f32[6,16,512]{2,1,0:T(8,128)S(1)} %pad_maximum_fusion.1), channel_id=1, source_target_pairs={{0,508},{4,0},{8,4},{12,8},{16,12},{20,16},{24,20},{28,24},{32,28}... | collective-permute-start | bytes 589832 | tf_op jit(solution)/shard_map/ppermute | solution.py:16
  21.7 19.0 %collective-permute-start.5 = (f32[6,16,512]{2,1,0:T(8,128)S(1)}, f32[6,16,512]{2,1,0:T(8,128)S(1)}, u32[]{:S(2)}, u32[]{:S(2)}) collective-permute-start(f32[6,16,512]{2,1,0:T(8,128)S(1)} %pad_maximum_fusion.5), channel_id=1, source_target_pairs={{0,3},{1,0},{2,1},{3,2},{4,7},{5,4},{6,5},{7,6},{8,11},{9,8},{10,9... | collective-permute-start | bytes 589832 | tf_op jit(solution)/shard_map/ppermute | solution.py:18
  25.7 20.9 %copy-start.1 = (f32[6,16,512]{2,1,0:T(8,128)}, f32[6,16,512]{2,1,0:T(8,128)S(1)}, u32[]{:S(2)}) copy-start(f32[6,16,512]{2,1,0:T(8,128)S(1)} %collective-permute-done.xm_ref) | copy-start | bytes 589828
  34.1 12.5 %copy-start.2 = (f32[6,16,512]{2,1,0:T(8,128)}, f32[6,16,512]{2,1,0:T(8,128)S(1)}, u32[]{:S(2)}) copy-start(f32[6,16,512]{2,1,0:T(8,128)S(1)} %collective-permute-done.1.xp_ref) | copy-start | bytes 589828
  34.1 7.9 %collective-permute-start.4 = (f32[6,9,512]{2,1,0:T(8,128)S(1)}, f32[6,9,512]{2,1,0:T(8,128)S(1)}, u32[]{:S(2)}, u32[]{:S(2)}) collective-permute-start(f32[6,9,512]{2,1,0:T(8,128)S(1)} %pad_maximum_fusion.4), channel_id=1, source_target_pairs={{0,3},{1,0},{2,1},{3,2},{4,7},{5,4},{6,5},{7,6},{8,11},{9,8},{10,9... | collective-permute-start | bytes 331784 | tf_op jit(solution)/shard_map/ppermute | solution.py:18
  38.1 8.5 %collective-permute-start.2 = (f32[6,9,512]{2,1,0:T(8,128)S(1)}, f32[6,9,512]{2,1,0:T(8,128)S(1)}, u32[]{:S(2)}, u32[]{:S(2)}) collective-permute-start(f32[6,9,512]{2,1,0:T(8,128)S(1)} %pad_maximum_fusion.2), channel_id=1, source_target_pairs={{0,1},{1,2},{2,3},{3,0},{4,5},{5,6},{6,7},{7,4},{8,9},{9,10},{10,1... | collective-permute-start | bytes 331784 | tf_op jit(solution)/shard_map/ppermute | solution.py:18
  40.6 5.9 %copy-start.3 = (f32[6,16,512]{2,1,0:T(8,128)}, f32[6,16,512]{2,1,0:T(8,128)S(1)}, u32[]{:S(2)}) copy-start(f32[6,16,512]{2,1,0:T(8,128)S(1)} %collective-permute-done.3.lown_ref) | copy-start | bytes 589828
  40.6 5.9 %copy-start.4 = (f32[6,16,512]{2,1,0:T(8,128)}, f32[6,16,512]{2,1,0:T(8,128)S(1)}, u32[]{:S(2)}) copy-start(f32[6,16,512]{2,1,0:T(8,128)S(1)} %collective-permute-done.5.hown_ref) | copy-start | bytes 589828
  42.0 4.6 %copy-start.5 = (f32[6,9,512]{2,1,0:T(8,128)}, f32[6,9,512]{2,1,0:T(8,128)S(1)}, u32[]{:S(2)}) copy-start(f32[6,9,512]{2,1,0:T(8,128)S(1)} %collective-permute-done.4.hend_ref) | copy-start | bytes 331780
  46.6 0.7 copy-start.6
  55.8 20.5 %collective-permute-start.6 = (f32[336,512]{1,0:T(8,128)}, f32[336,512]{1,0:T(8,128)S(1)}, u32[]{:S(2)}, u32[]{:S(2)}) collective-permute-start(f32[336,512]{1,0:T(8,128)} %get-tuple-element.8), channel_id=1, source_target_pairs={{0,1},{1,2},{2,3},{3,0},{4,5},{5,6},{6,7},{7,4},{8,9},{9,10},{10,1... | collective-permute-start | bytes 2064392 | tf_op jit(solution)/shard_map/ppermute | solution.py:18
  76.2 0.8 %copy-start = (f32[336,512]{1,0:T(8,128)}, f32[336,512]{1,0:T(8,128)S(1)}, u32[]{:S(2)}) copy-start(f32[336,512]{1,0:T(8,128)S(1)} %collective-permute-done.6.rec_hbm) | copy-start | bytes 2064388

commit v14 on v6

--- a/solution.py
+++ b/solution.py
@@ -145,12 +145,11 @@
         )
         for c in range(3):
             u_ref[c, r] = new[c]
+            top_ref[pl.ds((c * rows + r) * keep, keep), :] = new[c][ny - keep :]
         return carry
 
-    lax.fori_loop(0, rows, update_row, 0)
-    for c in range(3):
-        for r in range(rows):
-            top_ref[pl.ds((c * rows + r) * keep, keep), :] = u_ref[c, r, pl.ds(ny - keep, keep), :]
+    for r in range(rows):
+        update_row(r, 0)
 
 
 def ct_update(eshift, efrac, flags, field, velocity, xm, xp, low_in, high_in):

time: 81.7 us -> 80.8 us (0.989)
    pallas_call x1, Pallas kernels: 8.48 us -> 7.58 us  [ct_update(): pl.pallas_call(ct_kernel, out_shape=(jax.ShapeDtypeStruct((3, rows, ny, n...]
where the time goes in v14:
time: 80.8 us; the launch traced here: 80.4 us
  waiting for transfers between devices  32.7 us (40%)
  starting transfers between devices  29.2 us (36%)
  Pallas kernels  11.8 us (15%)
  local copies, waits for them, and re-layouts  5.77 us (7%)
    ppermute x5, waiting for transfers between devices, shifted(): return lax.ppermute(x, 'phi', [(q, (q + dp) % nq) for q in range(nq)])  24.3 us
    ppermute x5, starting transfers between devices, shifted(): return lax.ppermute(x, 'phi', [(q, (q + dp) % nq) for q in range(nq)])  16.7 us
    ppermute x2, starting transfers between devices, shifted(): return lax.ppermute(x, 'blocks', [(b, (b + db) % nb) for b in range(nb)])  12.5 us
    ppermute x2, waiting for transfers between devices, shifted(): return lax.ppermute(x, 'blocks', [(b, (b + db) % nb) for b in range(nb)])  8.36 us
    pallas_call x1, Pallas kernels, ct_update(): pl.pallas_call(ct_kernel, out_shape=(jax.ShapeDtypeStruct((3, rows, ny, n...  7.58 us
    pallas_call x1, Pallas kernels, advect(): pl.pallas_call(advect_kernel, out_shape=jax.ShapeDtypeStruct(updated.shap...  4.17 us
    slice x2, local copies, waits for them, and re-layouts, body(): own_high = jnp.concatenate([field[:, :, 0], velocity[:, :, 0]], axis=0)  3.1 us
  transfers between devices with their start and end apart: 7, of which 4 were waited for; matrix products, arithmetic and copies ran while one was open for 2% of the time, Pallas kernels for 0%

profile of v14, /device:TPU:1, one launch (start us, length us, event | category | flops | bytes accessed | tf_op | source)
XLA Modules:
  0.0 80.4 jit_solution(16271881708984133857)
XLA Ops:
  0.0 1.6 %fusion = (f32[3,16,1,512]{3,2,1,0:T(1,128)S(1)}, f32[3,16,1,512]{3,2,1,0:T(1,128)S(1)}) fusion(f32[3,16,16,512]{3,2,1,0:T(8,128)} %f_hbm.1), kind=kLoop, calls=%fused_computation.15 | loop fusion | bytes 393216 | tf_op jit(solution)/shard_map/slice | solution.py:232
  1.6 1.6 %fusion.1 = (f32[3,16,1,512]{3,2,1,0:T(1,128)S(1)}, f32[3,16,1,512]{3,2,1,0:T(1,128)S(1)}) fusion(f32[3,16,16,512]{3,2,1,0:T(8,128)} %v_hbm.1), kind=kLoop, calls=%fused_computation.16 | loop fusion | bytes 393216 | tf_op jit(solution)/shard_map/slice | solution.py:232
  3.2 4.8 %collective-permute-start.3 = (f32[6,16,512]{2,1,0:T(8,128)S(1)}, f32[6,16,512]{2,1,0:T(8,128)S(1)}, u32[]{:S(2)}, u32[]{:S(2)}) collective-permute-start(f32[6,16,512]{2,1,0:T(8,128)S(1)} %pad_maximum_fusion.3), channel_id=1, source_target_pairs={{0,1},{1,2},{2,3},{3,0},{4,5},{5,6},{6,7},{7,4},{8,9},{9,10},{10,1... | collective-permute-start | bytes 589832 | tf_op jit(solution)/shard_map/ppermute | solution.py:18
  8.0 1.1 %slice_bitcast_fusion = (f32[3,16,512]{2,1,0:T(8,128)S(1)}, f32[3,16,512]{2,1,0:T(8,128)S(1)}, f32[3,16,512]{2,1,0:T(8,128)S(1)}, f32[3,16,512]{2,1,0:T(8,128)S(1)}) fusion(f32[3,16,16,512]{3,2,1,0:T(8,128)} %v_hbm.1, f32[3,16,16,512]{3,2,1,0:T(8,128)} %f_hbm.1), kind=kLoop, calls=%fused_computation.10 | loop fusion | bytes 786432 | tf_op jit(solution)/shard_map/squeeze | solution.py:230
  9.1 10.6 %collective-permute-start = (f32[6,16,512]{2,1,0:T(8,128)S(1)}, f32[6,16,512]{2,1,0:T(8,128)S(1)}, u32[]{:S(2)}, u32[]{:S(2)}) collective-permute-start(f32[6,16,512]{2,1,0:T(8,128)S(1)} %pad_maximum_fusion), channel_id=1, source_target_pairs={{0,4},{4,8},{8,12},{12,16},{16,20},{20,24},{24,28},{28,32},{32,36}... | collective-permute-start | bytes 589832 | tf_op jit(solution)/shard_map/ppermute | solution.py:16
  19.7 1.9 %collective-permute-start.1 = (f32[6,16,512]{2,1,0:T(8,128)S(1)}, f32[6,16,512]{2,1,0:T(8,128)S(1)}, u32[]{:S(2)}, u32[]{:S(2)}) collective-permute-start(f32[6,16,512]{2,1,0:T(8,128)S(1)} %pad_maximum_fusion.1), channel_id=1, source_target_pairs={{0,508},{4,0},{8,4},{12,8},{16,12},{20,16},{24,20},{28,24},{32,28}... | collective-permute-start | bytes 589832 | tf_op jit(solution)/shard_map/ppermute | solution.py:16
  21.7 4.0 %collective-permute-start.5 = (f32[6,16,512]{2,1,0:T(8,128)S(1)}, f32[6,16,512]{2,1,0:T(8,128)S(1)}, u32[]{:S(2)}, u32[]{:S(2)}) collective-permute-start(f32[6,16,512]{2,1,0:T(8,128)S(1)} %pad_maximum_fusion.5), channel_id=1, source_target_pairs={{0,3},{1,0},{2,1},{3,2},{4,7},{5,4},{6,5},{7,6},{8,11},{9,8},{10,9... | collective-permute-start | bytes 589832 | tf_op jit(solution)/shard_map/ppermute | solution.py:18
  25.7 0.0 collective-permute-done.xm_ref
  25.7 0.0 copy-start.1
  25.7 8.4 %collective-permute-done.1.xp_ref = f32[6,16,512]{2,1,0:T(8,128)S(1)} collective-permute-done((f32[6,16,512]{2,1,0:T(8,128)S(1)}, f32[6,16,512]{2,1,0:T(8,128)S(1)}, u32[]{:S(2)}, u32[]{:S(2)}) %collective-permute-start.1) | collective-permute-done | bytes 196640 | tf_op jit(solution)/shard_map/ppermute | solution.py:16
  34.1 0.0 copy-start.2
  34.1 3.9 %collective-permute-start.4 = (f32[6,9,512]{2,1,0:T(8,128)S(1)}, f32[6,9,512]{2,1,0:T(8,128)S(1)}, u32[]{:S(2)}, u32[]{:S(2)}) collective-permute-start(f32[6,9,512]{2,1,0:T(8,128)S(1)} %pad_maximum_fusion.4), channel_id=1, source_target_pairs={{0,3},{1,0},{2,1},{3,2},{4,7},{5,4},{6,5},{7,6},{8,11},{9,8},{10,9... | collective-permute-start | bytes 331784 | tf_op jit(solution)/shard_map/ppermute | solution.py:18
  38.1 1.9 %collective-permute-start.2 = (f32[6,9,512]{2,1,0:T(8,128)S(1)}, f32[6,9,512]{2,1,0:T(8,128)S(1)}, u32[]{:S(2)}, u32[]{:S(2)}) collective-permute-start(f32[6,9,512]{2,1,0:T(8,128)S(1)} %pad_maximum_fusion.2), channel_id=1, source_target_pairs={{0,1},{1,2},{2,3},{3,0},{4,5},{5,6},{6,7},{7,4},{8,9},{9,10},{10,1... | collective-permute-start | bytes 331784 | tf_op jit(solution)/shard_map/ppermute | solution.py:18
  40.0 0.6 add_convert_fusion.flag_ref
  40.6 0.0 collective-permute-done.3.lown_ref
  40.6 0.0 copy-start.3
  40.6 0.0 collective-permute-done.5.hown_ref
  40.6 0.0 copy-start.4
  40.6 1.4 %collective-permute-done.4.hend_ref = f32[6,9,512]{2,1,0:T(8,128)S(1)} collective-permute-done((f32[6,9,512]{2,1,0:T(8,128)S(1)}, f32[6,9,512]{2,1,0:T(8,128)S(1)}, u32[]{:S(2)}, u32[]{:S(2)}) %collective-permute-start.4) | collective-permute-done | bytes 110624 | tf_op jit(solution)/shard_map/ppermute | solution.py:18
  42.0 4.5 %collective-permute-done.2.lend_ref = f32[6,9,512]{2,1,0:T(8,128)S(1)} collective-permute-done((f32[6,9,512]{2,1,0:T(8,128)S(1)}, f32[6,9,512]{2,1,0:T(8,128)S(1)}, u32[]{:S(2)}, u32[]{:S(2)}) %collective-permute-start.2) | collective-permute-done | bytes 110624 | tf_op jit(solution)/shard_map/ppermute | solution.py:18
  46.6 0.0 copy-done.1
  46.6 0.0 copy-done.2
  46.6 0.0 copy-done.3
  46.6 0.0 copy-done.4
  46.6 0.0 copy-done.5
  46.6 0.0 copy-start.6
  46.6 0.7 copy-done.6
  47.3 7.6 %shard_map.64 = (f32[3,16,16,512]{3,2,1,0:T(8,128)}, f32[336,512]{1,0:T(8,128)}) custom-call(s32[2]{0:T(128)} %eshift_ref.1, f32[2]{0:T(128)} %efrac_ref.1, s32[2]{0:T(128)} %add_convert_fusion.flag_ref, f32[3,16,16,512]{3,2,1,0:T(8,128)} %f_hbm.1, f32[3,16,16,512]{3,2,1,0:T(8,128)} %v_hbm.1, f32[6,16,512]{2,1,0:T(8,128)} %copy-done.1, ...), custom_call_target="tpu_custom_call" | custom-call | flops 15728640 | bytes 4718592 | tf_op jit(solution)/shard_map/pallas_call | solution.py:161
  54.9 2.1 %collective-permute-start.6 = (f32[336,512]{1,0:T(8,128)}, f32[336,512]{1,0:T(8,128)S(1)}, u32[]{:S(2)}, u32[]{:S(2)}) collective-permute-start(f32[336,512]{1,0:T(8,128)} %get-tuple-element.8), channel_id=1, source_target_pairs={{0,1},{1,2},{2,3},{3,0},{4,5},{5,6},{6,7},{7,4},{8,9},{9,10},{10,1... | collective-permute-start | bytes 2064392 | tf_op jit(solution)/shard_map/ppermute | solution.py:18
  57.0 18.4 %collective-permute-done.6.rec_ref = f32[336,512]{1,0:T(8,128)S(1)} collective-permute-done((f32[336,512]{1,0:T(8,128)}, f32[336,512]{1,0:T(8,128)S(1)}, u32[]{:S(2)}, u32[]{:S(2)}) %collective-permute-start.6) | collective-permute-done | bytes 688160 | tf_op jit(solution)/shard_map/ppermute | solution.py:18
  75.4 0.8 %copy-done = f32[336,512]{1,0:T(8,128)} copy-done((f32[336,512]{1,0:T(8,128)}, f32[336,512]{1,0:T(8,128)S(1)}, u32[]{:S(2)}) %copy-start) | copy-done | bytes 688152
  76.2 4.2 %shard_map.65 = f32[3,16,16,512]{3,2,1,0:T(8,128)} custom-call(s32[16]{0:T(128)} %shift_ref.1, f32[16]{0:T(128)} %frac_ref.1, f32[3,16,16,512]{3,2,1,0:T(8,128)} %get-tuple-element.7.u_ref, f32[336,512]{1,0:T(8,128)} %copy-done), custom_call_target="tpu_custom_call" | custom-call | flops 1179648 | bytes 3833856 | tf_op jit(solution)/shard_map/pallas_call | solution.py:211
  (14 shorter events, 0.2 us)
Async XLA Ops:
  3.2 37.5 %collective-permute-start.3 = (f32[6,16,512]{2,1,0:T(8,128)S(1)}, f32[6,16,512]{2,1,0:T(8,128)S(1)}, u32[]{:S(2)}, u32[]{:S(2)}) collective-permute-start(f32[6,16,512]{2,1,0:T(8,128)S(1)} %pad_maximum_fusion.3), channel_id=1, source_target_pairs={{0,1},{1,2},{2,3},{3,0},{4,5},{5,6},{6,7},{7,4},{8,9},{9,10},{10,1... | collective-permute-start | bytes 589832 | tf_op jit(solution)/shard_map/ppermute | solution.py:18
  9.1 16.6 %collective-permute-start = (f32[6,16,512]{2,1,0:T(8,128)S(1)}, f32[6,16,512]{2,1,0:T(8,128)S(1)}, u32[]{:S(2)}, u32[]{:S(2)}) collective-permute-start(f32[6,16,512]{2,1,0:T(8,128)S(1)} %pad_maximum_fusion), channel_id=1, source_target_pairs={{0,4},{4,8},{8,12},{12,16},{16,20},{20,24},{24,28},{28,32},{32,36}... | collective-permute-start | bytes 589832 | tf_op jit(solution)/shard_map/ppermute | solution.py:16
  19.7 14.4 %collective-permute-start.1 = (f32[6,16,512]{2,1,0:T(8,128)S(1)}, f32[6,16,512]{2,1,0:T(8,128)S(1)}, u32[]{:S(2)}, u32[]{:S(2)}) collective-permute-start(f32[6,16,512]{2,1,0:T(8,128)S(1)} %pad_maximum_fusion.1), channel_id=1, source_target_pairs={{0,508},{4,0},{8,4},{12,8},{16,12},{20,16},{24,20},{28,24},{32,28}... | collective-permute-start | bytes 589832 | tf_op jit(solution)/shard_map/ppermute | solution.py:16
  21.7 19.0 %collective-permute-start.5 = (f32[6,16,512]{2,1,0:T(8,128)S(1)}, f32[6,16,512]{2,1,0:T(8,128)S(1)}, u32[]{:S(2)}, u32[]{:S(2)}) collective-permute-start(f32[6,16,512]{2,1,0:T(8,128)S(1)} %pad_maximum_fusion.5), channel_id=1, source_target_pairs={{0,3},{1,0},{2,1},{3,2},{4,7},{5,4},{6,5},{7,6},{8,11},{9,8},{10,9... | collective-permute-start | bytes 589832 | tf_op jit(solution)/shard_map/ppermute | solution.py:18
  25.7 20.9 %copy-start.1 = (f32[6,16,512]{2,1,0:T(8,128)}, f32[6,16,512]{2,1,0:T(8,128)S(1)}, u32[]{:S(2)}) copy-start(f32[6,16,512]{2,1,0:T(8,128)S(1)} %collective-permute-done.xm_ref) | copy-start | bytes 589828
  34.1 12.5 %copy-start.2 = (f32[6,16,512]{2,1,0:T(8,128)}, f32[6,16,512]{2,1,0:T(8,128)S(1)}, u32[]{:S(2)}) copy-start(f32[6,16,512]{2,1,0:T(8,128)S(1)} %collective-permute-done.1.xp_ref) | copy-start | bytes 589828
  34.1 7.9 %collective-permute-start.4 = (f32[6,9,512]{2,1,0:T(8,128)S(1)}, f32[6,9,512]{2,1,0:T(8,128)S(1)}, u32[]{:S(2)}, u32[]{:S(2)}) collective-permute-start(f32[6,9,512]{2,1,0:T(8,128)S(1)} %pad_maximum_fusion.4), channel_id=1, source_target_pairs={{0,3},{1,0},{2,1},{3,2},{4,7},{5,4},{6,5},{7,6},{8,11},{9,8},{10,9... | collective-permute-start | bytes 331784 | tf_op jit(solution)/shard_map/ppermute | solution.py:18
  38.1 8.5 %collective-permute-start.2 = (f32[6,9,512]{2,1,0:T(8,128)S(1)}, f32[6,9,512]{2,1,0:T(8,128)S(1)}, u32[]{:S(2)}, u32[]{:S(2)}) collective-permute-start(f32[6,9,512]{2,1,0:T(8,128)S(1)} %pad_maximum_fusion.2), channel_id=1, source_target_pairs={{0,1},{1,2},{2,3},{3,0},{4,5},{5,6},{6,7},{7,4},{8,9},{9,10},{10,1... | collective-permute-start | bytes 331784 | tf_op jit(solution)/shard_map/ppermute | solution.py:18
  40.6 5.9 %copy-start.3 = (f32[6,16,512]{2,1,0:T(8,128)}, f32[6,16,512]{2,1,0:T(8,128)S(1)}, u32[]{:S(2)}) copy-start(f32[6,16,512]{2,1,0:T(8,128)S(1)} %collective-permute-done.3.lown_ref) | copy-start | bytes 589828
  40.6 5.9 %copy-start.4 = (f32[6,16,512]{2,1,0:T(8,128)}, f32[6,16,512]{2,1,0:T(8,128)S(1)}, u32[]{:S(2)}) copy-start(f32[6,16,512]{2,1,0:T(8,128)S(1)} %collective-permute-done.5.hown_ref) | copy-start | bytes 589828
  42.0 4.6 %copy-start.5 = (f32[6,9,512]{2,1,0:T(8,128)}, f32[6,9,512]{2,1,0:T(8,128)S(1)}, u32[]{:S(2)}) copy-start(f32[6,9,512]{2,1,0:T(8,128)S(1)} %collective-permute-done.4.hend_ref) | copy-start | bytes 331780
  46.6 0.7 copy-start.6
  54.9 20.5 %collective-permute-start.6 = (f32[336,512]{1,0:T(8,128)}, f32[336,512]{1,0:T(8,128)S(1)}, u32[]{:S(2)}, u32[]{:S(2)}) collective-permute-start(f32[336,512]{1,0:T(8,128)} %get-tuple-element.8), channel_id=1, source_target_pairs={{0,1},{1,2},{2,3},{3,0},{4,5},{5,6},{6,7},{7,4},{8,9},{9,10},{10,1... | collective-permute-start | bytes 2064392 | tf_op jit(solution)/shard_map/ppermute | solution.py:18
  75.4 0.8 %copy-start = (f32[336,512]{1,0:T(8,128)}, f32[336,512]{1,0:T(8,128)S(1)}, u32[]{:S(2)}) copy-start(f32[336,512]{1,0:T(8,128)S(1)} %collective-permute-done.6.rec_ref) | copy-start | bytes 2064388

commit v15 on v14

--- a/solution.py
+++ b/solution.py
@@ -122,7 +122,8 @@
         ex_s[a - 1, pl.ds(0, ny + 1), :] = xvz * xfy - xvy * xfz
         return carry
 
-    lax.fori_loop(1, rows + 2, emf_row, 0)
+    for a in range(1, rows + 2):
+        emf_row(a, 0)
 
     keep = KMAX + 1
 

time: 80.8 us -> 80.2 us (level)
  no operation moved by 1% of the time
where the time goes in v15:
time: 80.2 us; the launch traced here: 79.7 us
  waiting for transfers between devices  32.7 us (41%)
  starting transfers between devices  29.2 us (36%)
  Pallas kernels  11.1 us (14%)
  local copies, waits for them, and re-layouts  5.77 us (7%)
    ppermute x5, waiting for transfers between devices, shifted(): return lax.ppermute(x, 'phi', [(q, (q + dp) % nq) for q in range(nq)])  24.3 us
    ppermute x5, starting transfers between devices, shifted(): return lax.ppermute(x, 'phi', [(q, (q + dp) % nq) for q in range(nq)])  16.7 us
    ppermute x2, starting transfers between devices, shifted(): return lax.ppermute(x, 'blocks', [(b, (b + db) % nb) for b in range(nb)])  12.5 us
    ppermute x2, waiting for transfers between devices, shifted(): return lax.ppermute(x, 'blocks', [(b, (b + db) % nb) for b in range(nb)])  8.36 us
    pallas_call x1, Pallas kernels, ct_update(): pl.pallas_call(ct_kernel, out_shape=(jax.ShapeDtypeStruct((3, rows, ny, n...  6.97 us
    pallas_call x1, Pallas kernels, advect(): pl.pallas_call(advect_kernel, out_shape=jax.ShapeDtypeStruct(updated.shap...  4.15 us
    slice x2, local copies, waits for them, and re-layouts, body(): own_high = jnp.concatenate([field[:, :, 0], velocity[:, :, 0]], axis=0)  3.1 us
  transfers between devices with their start and end apart: 7, of which 4 were waited for; matrix products, arithmetic and copies ran while one was open for 2% of the time, Pallas kernels for 0%

profile of v15, /device:TPU:1, one launch (start us, length us, event | category | flops | bytes accessed | tf_op | source)
XLA Modules:
  0.0 79.7 jit_solution(1573050120547373129)
XLA Ops:
  0.0 1.6 %fusion = (f32[3,16,1,512]{3,2,1,0:T(1,128)S(1)}, f32[3,16,1,512]{3,2,1,0:T(1,128)S(1)}) fusion(f32[3,16,16,512]{3,2,1,0:T(8,128)} %f_hbm.1), kind=kLoop, calls=%fused_computation.15 | loop fusion | bytes 393216 | tf_op jit(solution)/shard_map/slice | solution.py:233
  1.6 1.6 %fusion.1 = (f32[3,16,1,512]{3,2,1,0:T(1,128)S(1)}, f32[3,16,1,512]{3,2,1,0:T(1,128)S(1)}) fusion(f32[3,16,16,512]{3,2,1,0:T(8,128)} %v_hbm.1), kind=kLoop, calls=%fused_computation.16 | loop fusion | bytes 393216 | tf_op jit(solution)/shard_map/slice | solution.py:233
  3.2 4.8 %collective-permute-start.3 = (f32[6,16,512]{2,1,0:T(8,128)S(1)}, f32[6,16,512]{2,1,0:T(8,128)S(1)}, u32[]{:S(2)}, u32[]{:S(2)}) collective-permute-start(f32[6,16,512]{2,1,0:T(8,128)S(1)} %pad_maximum_fusion.3), channel_id=1, source_target_pairs={{0,1},{1,2},{2,3},{3,0},{4,5},{5,6},{6,7},{7,4},{8,9},{9,10},{10,1... | collective-permute-start | bytes 589832 | tf_op jit(solution)/shard_map/ppermute | solution.py:18
  8.0 1.1 %slice_bitcast_fusion = (f32[3,16,512]{2,1,0:T(8,128)S(1)}, f32[3,16,512]{2,1,0:T(8,128)S(1)}, f32[3,16,512]{2,1,0:T(8,128)S(1)}, f32[3,16,512]{2,1,0:T(8,128)S(1)}) fusion(f32[3,16,16,512]{3,2,1,0:T(8,128)} %v_hbm.1, f32[3,16,16,512]{3,2,1,0:T(8,128)} %f_hbm.1), kind=kLoop, calls=%fused_computation.10 | loop fusion | bytes 786432 | tf_op jit(solution)/shard_map/squeeze | solution.py:231
  9.1 10.6 %collective-permute-start = (f32[6,16,512]{2,1,0:T(8,128)S(1)}, f32[6,16,512]{2,1,0:T(8,128)S(1)}, u32[]{:S(2)}, u32[]{:S(2)}) collective-permute-start(f32[6,16,512]{2,1,0:T(8,128)S(1)} %pad_maximum_fusion), channel_id=1, source_target_pairs={{0,4},{4,8},{8,12},{12,16},{16,20},{20,24},{24,28},{28,32},{32,36}... | collective-permute-start | bytes 589832 | tf_op jit(solution)/shard_map/ppermute | solution.py:16
  19.7 1.9 %collective-permute-start.1 = (f32[6,16,512]{2,1,0:T(8,128)S(1)}, f32[6,16,512]{2,1,0:T(8,128)S(1)}, u32[]{:S(2)}, u32[]{:S(2)}) collective-permute-start(f32[6,16,512]{2,1,0:T(8,128)S(1)} %pad_maximum_fusion.1), channel_id=1, source_target_pairs={{0,508},{4,0},{8,4},{12,8},{16,12},{20,16},{24,20},{28,24},{32,28}... | collective-permute-start | bytes 589832 | tf_op jit(solution)/shard_map/ppermute | solution.py:16
  21.7 4.0 %collective-permute-start.5 = (f32[6,16,512]{2,1,0:T(8,128)S(1)}, f32[6,16,512]{2,1,0:T(8,128)S(1)}, u32[]{:S(2)}, u32[]{:S(2)}) collective-permute-start(f32[6,16,512]{2,1,0:T(8,128)S(1)} %pad_maximum_fusion.5), channel_id=1, source_target_pairs={{0,3},{1,0},{2,1},{3,2},{4,7},{5,4},{6,5},{7,6},{8,11},{9,8},{10,9... | collective-permute-start | bytes 589832 | tf_op jit(solution)/shard_map/ppermute | solution.py:18
  25.7 0.0 collective-permute-done.xm_ref
  25.7 0.0 copy-start.1
  25.7 8.4 %collective-permute-done.1.xp_ref = f32[6,16,512]{2,1,0:T(8,128)S(1)} collective-permute-done((f32[6,16,512]{2,1,0:T(8,128)S(1)}, f32[6,16,512]{2,1,0:T(8,128)S(1)}, u32[]{:S(2)}, u32[]{:S(2)}) %collective-permute-start.1) | collective-permute-done | bytes 196640 | tf_op jit(solution)/shard_map/ppermute | solution.py:16
  34.1 0.0 copy-start.2
  34.1 3.9 %collective-permute-start.4 = (f32[6,9,512]{2,1,0:T(8,128)S(1)}, f32[6,9,512]{2,1,0:T(8,128)S(1)}, u32[]{:S(2)}, u32[]{:S(2)}) collective-permute-start(f32[6,9,512]{2,1,0:T(8,128)S(1)} %pad_maximum_fusion.4), channel_id=1, source_target_pairs={{0,3},{1,0},{2,1},{3,2},{4,7},{5,4},{6,5},{7,6},{8,11},{9,8},{10,9... | collective-permute-start | bytes 331784 | tf_op jit(solution)/shard_map/ppermute | solution.py:18
  38.1 1.9 %collective-permute-start.2 = (f32[6,9,512]{2,1,0:T(8,128)S(1)}, f32[6,9,512]{2,1,0:T(8,128)S(1)}, u32[]{:S(2)}, u32[]{:S(2)}) collective-permute-start(f32[6,9,512]{2,1,0:T(8,128)S(1)} %pad_maximum_fusion.2), channel_id=1, source_target_pairs={{0,1},{1,2},{2,3},{3,0},{4,5},{5,6},{6,7},{7,4},{8,9},{9,10},{10,1... | collective-permute-start | bytes 331784 | tf_op jit(solution)/shard_map/ppermute | solution.py:18
  40.0 0.6 add_convert_fusion.flag_ref
  40.6 0.0 collective-permute-done.3.lown_ref
  40.6 0.0 copy-start.3
  40.6 0.0 collective-permute-done.5.hown_ref
  40.6 0.0 copy-start.4
  40.6 1.4 %collective-permute-done.4.hend_ref = f32[6,9,512]{2,1,0:T(8,128)S(1)} collective-permute-done((f32[6,9,512]{2,1,0:T(8,128)S(1)}, f32[6,9,512]{2,1,0:T(8,128)S(1)}, u32[]{:S(2)}, u32[]{:S(2)}) %collective-permute-start.4) | collective-permute-done | bytes 110624 | tf_op jit(solution)/shard_map/ppermute | solution.py:18
  42.0 4.5 %collective-permute-done.2.lend_ref = f32[6,9,512]{2,1,0:T(8,128)S(1)} collective-permute-done((f32[6,9,512]{2,1,0:T(8,128)S(1)}, f32[6,9,512]{2,1,0:T(8,128)S(1)}, u32[]{:S(2)}, u32[]{:S(2)}) %collective-permute-start.2) | collective-permute-done | bytes 110624 | tf_op jit(solution)/shard_map/ppermute | solution.py:18
  46.6 0.0 copy-done.1
  46.6 0.0 copy-done.2
  46.6 0.0 copy-done.3
  46.6 0.0 copy-done.4
  46.6 0.0 copy-done.5
  46.6 0.0 copy-start.6
  46.6 0.7 copy-done.6
  47.3 7.0 %shard_map.64 = (f32[3,16,16,512]{3,2,1,0:T(8,128)}, f32[336,512]{1,0:T(8,128)}) custom-call(s32[2]{0:T(128)} %eshift_ref.1, f32[2]{0:T(128)} %efrac_ref.1, s32[2]{0:T(128)} %add_convert_fusion.flag_ref, f32[3,16,16,512]{3,2,1,0:T(8,128)} %f_hbm.1, f32[3,16,16,512]{3,2,1,0:T(8,128)} %v_hbm.1, f32[6,16,512]{2,1,0:T(8,128)} %copy-done.1, ...), custom_call_target="tpu_custom_call" | custom-call | flops 15728640 | bytes 4718592 | tf_op jit(solution)/shard_map/pallas_call | solution.py:162
  54.2 2.1 %collective-permute-start.6 = (f32[336,512]{1,0:T(8,128)}, f32[336,512]{1,0:T(8,128)S(1)}, u32[]{:S(2)}, u32[]{:S(2)}) collective-permute-start(f32[336,512]{1,0:T(8,128)} %get-tuple-element.8), channel_id=1, source_target_pairs={{0,1},{1,2},{2,3},{3,0},{4,5},{5,6},{6,7},{7,4},{8,9},{9,10},{10,1... | collective-permute-start | bytes 2064392 | tf_op jit(solution)/shard_map/ppermute | solution.py:18
  56.3 18.4 %collective-permute-done.6.rec_ref = f32[336,512]{1,0:T(8,128)S(1)} collective-permute-done((f32[336,512]{1,0:T(8,128)}, f32[336,512]{1,0:T(8,128)S(1)}, u32[]{:S(2)}, u32[]{:S(2)}) %collective-permute-start.6) | collective-permute-done | bytes 688160 | tf_op jit(solution)/shard_map/ppermute | solution.py:18
  74.7 0.8 %copy-done = f32[336,512]{1,0:T(8,128)} copy-done((f32[336,512]{1,0:T(8,128)}, f32[336,512]{1,0:T(8,128)S(1)}, u32[]{:S(2)}) %copy-start) | copy-done | bytes 688152
  75.6 4.2 %shard_map.65 = f32[3,16,16,512]{3,2,1,0:T(8,128)} custom-call(s32[16]{0:T(128)} %shift_ref.1, f32[16]{0:T(128)} %frac_ref.1, f32[3,16,16,512]{3,2,1,0:T(8,128)} %get-tuple-element.7.u_ref, f32[336,512]{1,0:T(8,128)} %copy-done), custom_call_target="tpu_custom_call" | custom-call | flops 1179648 | bytes 3833856 | tf_op jit(solution)/shard_map/pallas_call | solution.py:212
  (14 shorter events, 0.2 us)
Async XLA Ops:
  3.2 37.5 %collective-permute-start.3 = (f32[6,16,512]{2,1,0:T(8,128)S(1)}, f32[6,16,512]{2,1,0:T(8,128)S(1)}, u32[]{:S(2)}, u32[]{:S(2)}) collective-permute-start(f32[6,16,512]{2,1,0:T(8,128)S(1)} %pad_maximum_fusion.3), channel_id=1, source_target_pairs={{0,1},{1,2},{2,3},{3,0},{4,5},{5,6},{6,7},{7,4},{8,9},{9,10},{10,1... | collective-permute-start | bytes 589832 | tf_op jit(solution)/shard_map/ppermute | solution.py:18
  9.1 16.6 %collective-permute-start = (f32[6,16,512]{2,1,0:T(8,128)S(1)}, f32[6,16,512]{2,1,0:T(8,128)S(1)}, u32[]{:S(2)}, u32[]{:S(2)}) collective-permute-start(f32[6,16,512]{2,1,0:T(8,128)S(1)} %pad_maximum_fusion), channel_id=1, source_target_pairs={{0,4},{4,8},{8,12},{12,16},{16,20},{20,24},{24,28},{28,32},{32,36}... | collective-permute-start | bytes 589832 | tf_op jit(solution)/shard_map/ppermute | solution.py:16
  19.7 14.4 %collective-permute-start.1 = (f32[6,16,512]{2,1,0:T(8,128)S(1)}, f32[6,16,512]{2,1,0:T(8,128)S(1)}, u32[]{:S(2)}, u32[]{:S(2)}) collective-permute-start(f32[6,16,512]{2,1,0:T(8,128)S(1)} %pad_maximum_fusion.1), channel_id=1, source_target_pairs={{0,508},{4,0},{8,4},{12,8},{16,12},{20,16},{24,20},{28,24},{32,28}... | collective-permute-start | bytes 589832 | tf_op jit(solution)/shard_map/ppermute | solution.py:16
  21.7 19.0 %collective-permute-start.5 = (f32[6,16,512]{2,1,0:T(8,128)S(1)}, f32[6,16,512]{2,1,0:T(8,128)S(1)}, u32[]{:S(2)}, u32[]{:S(2)}) collective-permute-start(f32[6,16,512]{2,1,0:T(8,128)S(1)} %pad_maximum_fusion.5), channel_id=1, source_target_pairs={{0,3},{1,0},{2,1},{3,2},{4,7},{5,4},{6,5},{7,6},{8,11},{9,8},{10,9... | collective-permute-start | bytes 589832 | tf_op jit(solution)/shard_map/ppermute | solution.py:18
  25.7 20.9 %copy-start.1 = (f32[6,16,512]{2,1,0:T(8,128)}, f32[6,16,512]{2,1,0:T(8,128)S(1)}, u32[]{:S(2)}) copy-start(f32[6,16,512]{2,1,0:T(8,128)S(1)} %collective-permute-done.xm_ref) | copy-start | bytes 589828
  34.1 12.5 %copy-start.2 = (f32[6,16,512]{2,1,0:T(8,128)}, f32[6,16,512]{2,1,0:T(8,128)S(1)}, u32[]{:S(2)}) copy-start(f32[6,16,512]{2,1,0:T(8,128)S(1)} %collective-permute-done.1.xp_ref) | copy-start | bytes 589828
  34.1 7.9 %collective-permute-start.4 = (f32[6,9,512]{2,1,0:T(8,128)S(1)}, f32[6,9,512]{2,1,0:T(8,128)S(1)}, u32[]{:S(2)}, u32[]{:S(2)}) collective-permute-start(f32[6,9,512]{2,1,0:T(8,128)S(1)} %pad_maximum_fusion.4), channel_id=1, source_target_pairs={{0,3},{1,0},{2,1},{3,2},{4,7},{5,4},{6,5},{7,6},{8,11},{9,8},{10,9... | collective-permute-start | bytes 331784 | tf_op jit(solution)/shard_map/ppermute | solution.py:18
  38.1 8.5 %collective-permute-start.2 = (f32[6,9,512]{2,1,0:T(8,128)S(1)}, f32[6,9,512]{2,1,0:T(8,128)S(1)}, u32[]{:S(2)}, u32[]{:S(2)}) collective-permute-start(f32[6,9,512]{2,1,0:T(8,128)S(1)} %pad_maximum_fusion.2), channel_id=1, source_target_pairs={{0,1},{1,2},{2,3},{3,0},{4,5},{5,6},{6,7},{7,4},{8,9},{9,10},{10,1... | collective-permute-start | bytes 331784 | tf_op jit(solution)/shard_map/ppermute | solution.py:18
  40.6 5.9 %copy-start.3 = (f32[6,16,512]{2,1,0:T(8,128)}, f32[6,16,512]{2,1,0:T(8,128)S(1)}, u32[]{:S(2)}) copy-start(f32[6,16,512]{2,1,0:T(8,128)S(1)} %collective-permute-done.3.lown_ref) | copy-start | bytes 589828
  40.6 5.9 %copy-start.4 = (f32[6,16,512]{2,1,0:T(8,128)}, f32[6,16,512]{2,1,0:T(8,128)S(1)}, u32[]{:S(2)}) copy-start(f32[6,16,512]{2,1,0:T(8,128)S(1)} %collective-permute-done.5.hown_ref) | copy-start | bytes 589828
  42.0 4.6 %copy-start.5 = (f32[6,9,512]{2,1,0:T(8,128)}, f32[6,9,512]{2,1,0:T(8,128)S(1)}, u32[]{:S(2)}) copy-start(f32[6,9,512]{2,1,0:T(8,128)S(1)} %collective-permute-done.4.hend_ref) | copy-start | bytes 331780
  46.6 0.7 copy-start.6
  54.2 20.5 %collective-permute-start.6 = (f32[336,512]{1,0:T(8,128)}, f32[336,512]{1,0:T(8,128)S(1)}, u32[]{:S(2)}, u32[]{:S(2)}) collective-permute-start(f32[336,512]{1,0:T(8,128)} %get-tuple-element.8), channel_id=1, source_target_pairs={{0,1},{1,2},{2,3},{3,0},{4,5},{5,6},{6,7},{7,4},{8,9},{9,10},{10,1... | collective-permute-start | bytes 2064392 | tf_op jit(solution)/shard_map/ppermute | solution.py:18
  74.7 0.8 %copy-start = (f32[336,512]{1,0:T(8,128)}, f32[336,512]{1,0:T(8,128)S(1)}, u32[]{:S(2)}) copy-start(f32[336,512]{1,0:T(8,128)S(1)} %collective-permute-done.6.rec_ref) | copy-start | bytes 2064388

commit v16 on v15

--- a/solution.py
+++ b/solution.py
@@ -202,7 +202,8 @@
                 o_ref[:, x] = (1.0 - w) * near + w * far
         return carry
 
-    lax.fori_loop(0, rows, strip, 0)
+    for x in range(rows):
+        strip(x, 0)
 
 
 def advect(updated, received, strip_shift, strip_frac):

time: 80.2 us -> 80.1 us (level)
  no operation moved by 1% of the time
where the time goes in v16:
time: 80.1 us; the launch traced here: 79.6 us
  waiting for transfers between devices  32.7 us (41%)
  starting transfers between devices  29.2 us (36%)
  Pallas kernels  11 us (14%)
  local copies, waits for them, and re-layouts  5.77 us (7%)
    ppermute x5, waiting for transfers between devices, shifted(): return lax.ppermute(x, 'phi', [(q, (q + dp) % nq) for q in range(nq)])  24.3 us
    ppermute x5, starting transfers between devices, shifted(): return lax.ppermute(x, 'phi', [(q, (q + dp) % nq) for q in range(nq)])  16.7 us
    ppermute x2, starting transfers between devices, shifted(): return lax.ppermute(x, 'blocks', [(b, (b + db) % nb) for b in range(nb)])  12.5 us
    ppermute x2, waiting for transfers between devices, shifted(): return lax.ppermute(x, 'blocks', [(b, (b + db) % nb) for b in range(nb)])  8.36 us
    pallas_call x1, Pallas kernels, ct_update(): pl.pallas_call(ct_kernel, out_shape=(jax.ShapeDtypeStruct((3, rows, ny, n...  6.97 us
    pallas_call x1, Pallas kernels, advect(): pl.pallas_call(advect_kernel, out_shape=jax.ShapeDtypeStruct(updated.shap...  4.03 us
    slice x2, local copies, waits for them, and re-layouts, body(): own_high = jnp.concatenate([field[:, :, 0], velocity[:, :, 0]], axis=0)  3.1 us
  transfers between devices with their start and end apart: 7, of which 4 were waited for; matrix products, arithmetic and copies ran while one was open for 2% of the time, Pallas kernels for 0%

profile of v16, /device:TPU:1, one launch (start us, length us, event | category | flops | bytes accessed | tf_op | source)
XLA Modules:
  0.0 79.6 jit_solution(16493513087447061165)
XLA Ops:
  0.0 1.6 %fusion = (f32[3,16,1,512]{3,2,1,0:T(1,128)S(1)}, f32[3,16,1,512]{3,2,1,0:T(1,128)S(1)}) fusion(f32[3,16,16,512]{3,2,1,0:T(8,128)} %f_hbm.1), kind=kLoop, calls=%fused_computation.15 | loop fusion | bytes 393216 | tf_op jit(solution)/shard_map/slice | solution.py:234
  1.6 1.6 %fusion.1 = (f32[3,16,1,512]{3,2,1,0:T(1,128)S(1)}, f32[3,16,1,512]{3,2,1,0:T(1,128)S(1)}) fusion(f32[3,16,16,512]{3,2,1,0:T(8,128)} %v_hbm.1), kind=kLoop, calls=%fused_computation.16 | loop fusion | bytes 393216 | tf_op jit(solution)/shard_map/slice | solution.py:234
  3.2 4.8 %collective-permute-start.3 = (f32[6,16,512]{2,1,0:T(8,128)S(1)}, f32[6,16,512]{2,1,0:T(8,128)S(1)}, u32[]{:S(2)}, u32[]{:S(2)}) collective-permute-start(f32[6,16,512]{2,1,0:T(8,128)S(1)} %pad_maximum_fusion.3), channel_id=1, source_target_pairs={{0,1},{1,2},{2,3},{3,0},{4,5},{5,6},{6,7},{7,4},{8,9},{9,10},{10,1... | collective-permute-start | bytes 589832 | tf_op jit(solution)/shard_map/ppermute | solution.py:18
  8.0 1.1 %slice_bitcast_fusion = (f32[3,16,512]{2,1,0:T(8,128)S(1)}, f32[3,16,512]{2,1,0:T(8,128)S(1)}, f32[3,16,512]{2,1,0:T(8,128)S(1)}, f32[3,16,512]{2,1,0:T(8,128)S(1)}) fusion(f32[3,16,16,512]{3,2,1,0:T(8,128)} %v_hbm.1, f32[3,16,16,512]{3,2,1,0:T(8,128)} %f_hbm.1), kind=kLoop, calls=%fused_computation.10 | loop fusion | bytes 786432 | tf_op jit(solution)/shard_map/squeeze | solution.py:232
  9.1 10.6 %collective-permute-start = (f32[6,16,512]{2,1,0:T(8,128)S(1)}, f32[6,16,512]{2,1,0:T(8,128)S(1)}, u32[]{:S(2)}, u32[]{:S(2)}) collective-permute-start(f32[6,16,512]{2,1,0:T(8,128)S(1)} %pad_maximum_fusion), channel_id=1, source_target_pairs={{0,4},{4,8},{8,12},{12,16},{16,20},{20,24},{24,28},{28,32},{32,36}... | collective-permute-start | bytes 589832 | tf_op jit(solution)/shard_map/ppermute | solution.py:16
  19.7 1.9 %collective-permute-start.1 = (f32[6,16,512]{2,1,0:T(8,128)S(1)}, f32[6,16,512]{2,1,0:T(8,128)S(1)}, u32[]{:S(2)}, u32[]{:S(2)}) collective-permute-start(f32[6,16,512]{2,1,0:T(8,128)S(1)} %pad_maximum_fusion.1), channel_id=1, source_target_pairs={{0,508},{4,0},{8,4},{12,8},{16,12},{20,16},{24,20},{28,24},{32,28}... | collective-permute-start | bytes 589832 | tf_op jit(solution)/shard_map/ppermute | solution.py:16
  21.7 4.0 %collective-permute-start.5 = (f32[6,16,512]{2,1,0:T(8,128)S(1)}, f32[6,16,512]{2,1,0:T(8,128)S(1)}, u32[]{:S(2)}, u32[]{:S(2)}) collective-permute-start(f32[6,16,512]{2,1,0:T(8,128)S(1)} %pad_maximum_fusion.5), channel_id=1, source_target_pairs={{0,3},{1,0},{2,1},{3,2},{4,7},{5,4},{6,5},{7,6},{8,11},{9,8},{10,9... | collective-permute-start | bytes 589832 | tf_op jit(solution)/shard_map/ppermute | solution.py:18
  25.7 0.0 collective-permute-done.xm_ref
  25.7 0.0 copy-start.1
  25.7 8.4 %collective-permute-done.1.xp_ref = f32[6,16,512]{2,1,0:T(8,128)S(1)} collective-permute-done((f32[6,16,512]{2,1,0:T(8,128)S(1)}, f32[6,16,512]{2,1,0:T(8,128)S(1)}, u32[]{:S(2)}, u32[]{:S(2)}) %collective-permute-start.1) | collective-permute-done | bytes 196640 | tf_op jit(solution)/shard_map/ppermute | solution.py:16
  34.1 0.0 copy-start.2
  34.1 3.9 %collective-permute-start.4 = (f32[6,9,512]{2,1,0:T(8,128)S(1)}, f32[6,9,512]{2,1,0:T(8,128)S(1)}, u32[]{:S(2)}, u32[]{:S(2)}) collective-permute-start(f32[6,9,512]{2,1,0:T(8,128)S(1)} %pad_maximum_fusion.4), channel_id=1, source_target_pairs={{0,3},{1,0},{2,1},{3,2},{4,7},{5,4},{6,5},{7,6},{8,11},{9,8},{10,9... | collective-permute-start | bytes 331784 | tf_op jit(solution)/shard_map/ppermute | solution.py:18
  38.1 1.9 %collective-permute-start.2 = (f32[6,9,512]{2,1,0:T(8,128)S(1)}, f32[6,9,512]{2,1,0:T(8,128)S(1)}, u32[]{:S(2)}, u32[]{:S(2)}) collective-permute-start(f32[6,9,512]{2,1,0:T(8,128)S(1)} %pad_maximum_fusion.2), channel_id=1, source_target_pairs={{0,1},{1,2},{2,3},{3,0},{4,5},{5,6},{6,7},{7,4},{8,9},{9,10},{10,1... | collective-permute-start | bytes 331784 | tf_op jit(solution)/shard_map/ppermute | solution.py:18
  40.0 0.6 add_convert_fusion.flag_ref
  40.6 0.0 collective-permute-done.3.lown_ref
  40.6 0.0 copy-start.3
  40.6 0.0 collective-permute-done.5.hown_ref
  40.6 0.0 copy-start.4
  40.6 1.4 %collective-permute-done.4.hend_ref = f32[6,9,512]{2,1,0:T(8,128)S(1)} collective-permute-done((f32[6,9,512]{2,1,0:T(8,128)S(1)}, f32[6,9,512]{2,1,0:T(8,128)S(1)}, u32[]{:S(2)}, u32[]{:S(2)}) %collective-permute-start.4) | collective-permute-done | bytes 110624 | tf_op jit(solution)/shard_map/ppermute | solution.py:18
  42.0 4.5 %collective-permute-done.2.lend_ref = f32[6,9,512]{2,1,0:T(8,128)S(1)} collective-permute-done((f32[6,9,512]{2,1,0:T(8,128)S(1)}, f32[6,9,512]{2,1,0:T(8,128)S(1)}, u32[]{:S(2)}, u32[]{:S(2)}) %collective-permute-start.2) | collective-permute-done | bytes 110624 | tf_op jit(solution)/shard_map/ppermute | solution.py:18
  46.6 0.0 copy-done.1
  46.6 0.0 copy-done.2
  46.6 0.0 copy-done.3
  46.6 0.0 copy-done.4
  46.6 0.0 copy-done.5
  46.6 0.0 copy-start.6
  46.6 0.7 copy-done.6
  47.3 7.0 %shard_map.64 = (f32[3,16,16,512]{3,2,1,0:T(8,128)}, f32[336,512]{1,0:T(8,128)}) custom-call(s32[2]{0:T(128)} %eshift_ref.1, f32[2]{0:T(128)} %efrac_ref.1, s32[2]{0:T(128)} %add_convert_fusion.flag_ref, f32[3,16,16,512]{3,2,1,0:T(8,128)} %f_hbm.1, f32[3,16,16,512]{3,2,1,0:T(8,128)} %v_hbm.1, f32[6,16,512]{2,1,0:T(8,128)} %copy-done.1, ...), custom_call_target="tpu_custom_call" | custom-call | flops 15728640 | bytes 4718592 | tf_op jit(solution)/shard_map/pallas_call | solution.py:162
  54.2 2.1 %collective-permute-start.6 = (f32[336,512]{1,0:T(8,128)}, f32[336,512]{1,0:T(8,128)S(1)}, u32[]{:S(2)}, u32[]{:S(2)}) collective-permute-start(f32[336,512]{1,0:T(8,128)} %get-tuple-element.8), channel_id=1, source_target_pairs={{0,1},{1,2},{2,3},{3,0},{4,5},{5,6},{6,7},{7,4},{8,9},{9,10},{10,1... | collective-permute-start | bytes 2064392 | tf_op jit(solution)/shard_map/ppermute | solution.py:18
  56.3 18.4 %collective-permute-done.6.rec_ref = f32[336,512]{1,0:T(8,128)S(1)} collective-permute-done((f32[336,512]{1,0:T(8,128)}, f32[336,512]{1,0:T(8,128)S(1)}, u32[]{:S(2)}, u32[]{:S(2)}) %collective-permute-start.6) | collective-permute-done | bytes 688160 | tf_op jit(solution)/shard_map/ppermute | solution.py:18
  74.7 0.8 %copy-done = f32[336,512]{1,0:T(8,128)} copy-done((f32[336,512]{1,0:T(8,128)}, f32[336,512]{1,0:T(8,128)S(1)}, u32[]{:S(2)}) %copy-start) | copy-done | bytes 688152
  75.6 4.0 %shard_map.65 = f32[3,16,16,512]{3,2,1,0:T(8,128)} custom-call(s32[16]{0:T(128)} %shift_ref.1, f32[16]{0:T(128)} %frac_ref.1, f32[3,16,16,512]{3,2,1,0:T(8,128)} %get-tuple-element.7.u_ref, f32[336,512]{1,0:T(8,128)} %copy-done), custom_call_target="tpu_custom_call" | custom-call | flops 1179648 | bytes 3833856 | tf_op jit(solution)/shard_map/pallas_call | solution.py:213
  (14 shorter events, 0.2 us)
Async XLA Ops:
  3.2 37.5 %collective-permute-start.3 = (f32[6,16,512]{2,1,0:T(8,128)S(1)}, f32[6,16,512]{2,1,0:T(8,128)S(1)}, u32[]{:S(2)}, u32[]{:S(2)}) collective-permute-start(f32[6,16,512]{2,1,0:T(8,128)S(1)} %pad_maximum_fusion.3), channel_id=1, source_target_pairs={{0,1},{1,2},{2,3},{3,0},{4,5},{5,6},{6,7},{7,4},{8,9},{9,10},{10,1... | collective-permute-start | bytes 589832 | tf_op jit(solution)/shard_map/ppermute | solution.py:18
  9.1 16.6 %collective-permute-start = (f32[6,16,512]{2,1,0:T(8,128)S(1)}, f32[6,16,512]{2,1,0:T(8,128)S(1)}, u32[]{:S(2)}, u32[]{:S(2)}) collective-permute-start(f32[6,16,512]{2,1,0:T(8,128)S(1)} %pad_maximum_fusion), channel_id=1, source_target_pairs={{0,4},{4,8},{8,12},{12,16},{16,20},{20,24},{24,28},{28,32},{32,36}... | collective-permute-start | bytes 589832 | tf_op jit(solution)/shard_map/ppermute | solution.py:16
  19.7 14.4 %collective-permute-start.1 = (f32[6,16,512]{2,1,0:T(8,128)S(1)}, f32[6,16,512]{2,1,0:T(8,128)S(1)}, u32[]{:S(2)}, u32[]{:S(2)}) collective-permute-start(f32[6,16,512]{2,1,0:T(8,128)S(1)} %pad_maximum_fusion.1), channel_id=1, source_target_pairs={{0,508},{4,0},{8,4},{12,8},{16,12},{20,16},{24,20},{28,24},{32,28}... | collective-permute-start | bytes 589832 | tf_op jit(solution)/shard_map/ppermute | solution.py:16
  21.7 19.0 %collective-permute-start.5 = (f32[6,16,512]{2,1,0:T(8,128)S(1)}, f32[6,16,512]{2,1,0:T(8,128)S(1)}, u32[]{:S(2)}, u32[]{:S(2)}) collective-permute-start(f32[6,16,512]{2,1,0:T(8,128)S(1)} %pad_maximum_fusion.5), channel_id=1, source_target_pairs={{0,3},{1,0},{2,1},{3,2},{4,7},{5,4},{6,5},{7,6},{8,11},{9,8},{10,9... | collective-permute-start | bytes 589832 | tf_op jit(solution)/shard_map/ppermute | solution.py:18
  25.7 20.9 %copy-start.1 = (f32[6,16,512]{2,1,0:T(8,128)}, f32[6,16,512]{2,1,0:T(8,128)S(1)}, u32[]{:S(2)}) copy-start(f32[6,16,512]{2,1,0:T(8,128)S(1)} %collective-permute-done.xm_ref) | copy-start | bytes 589828
  34.1 12.5 %copy-start.2 = (f32[6,16,512]{2,1,0:T(8,128)}, f32[6,16,512]{2,1,0:T(8,128)S(1)}, u32[]{:S(2)}) copy-start(f32[6,16,512]{2,1,0:T(8,128)S(1)} %collective-permute-done.1.xp_ref) | copy-start | bytes 589828
  34.1 7.9 %collective-permute-start.4 = (f32[6,9,512]{2,1,0:T(8,128)S(1)}, f32[6,9,512]{2,1,0:T(8,128)S(1)}, u32[]{:S(2)}, u32[]{:S(2)}) collective-permute-start(f32[6,9,512]{2,1,0:T(8,128)S(1)} %pad_maximum_fusion.4), channel_id=1, source_target_pairs={{0,3},{1,0},{2,1},{3,2},{4,7},{5,4},{6,5},{7,6},{8,11},{9,8},{10,9... | collective-permute-start | bytes 331784 | tf_op jit(solution)/shard_map/ppermute | solution.py:18
  38.1 8.5 %collective-permute-start.2 = (f32[6,9,512]{2,1,0:T(8,128)S(1)}, f32[6,9,512]{2,1,0:T(8,128)S(1)}, u32[]{:S(2)}, u32[]{:S(2)}) collective-permute-start(f32[6,9,512]{2,1,0:T(8,128)S(1)} %pad_maximum_fusion.2), channel_id=1, source_target_pairs={{0,1},{1,2},{2,3},{3,0},{4,5},{5,6},{6,7},{7,4},{8,9},{9,10},{10,1... | collective-permute-start | bytes 331784 | tf_op jit(solution)/shard_map/ppermute | solution.py:18
  40.6 5.9 %copy-start.3 = (f32[6,16,512]{2,1,0:T(8,128)}, f32[6,16,512]{2,1,0:T(8,128)S(1)}, u32[]{:S(2)}) copy-start(f32[6,16,512]{2,1,0:T(8,128)S(1)} %collective-permute-done.3.lown_ref) | copy-start | bytes 589828
  40.6 5.9 %copy-start.4 = (f32[6,16,512]{2,1,0:T(8,128)}, f32[6,16,512]{2,1,0:T(8,128)S(1)}, u32[]{:S(2)}) copy-start(f32[6,16,512]{2,1,0:T(8,128)S(1)} %collective-permute-done.5.hown_ref) | copy-start | bytes 589828
  42.0 4.6 %copy-start.5 = (f32[6,9,512]{2,1,0:T(8,128)}, f32[6,9,512]{2,1,0:T(8,128)S(1)}, u32[]{:S(2)}) copy-start(f32[6,9,512]{2,1,0:T(8,128)S(1)} %collective-permute-done.4.hend_ref) | copy-start | bytes 331780
  46.6 0.7 copy-start.6
  54.2 20.5 %collective-permute-start.6 = (f32[336,512]{1,0:T(8,128)}, f32[336,512]{1,0:T(8,128)S(1)}, u32[]{:S(2)}, u32[]{:S(2)}) collective-permute-start(f32[336,512]{1,0:T(8,128)} %get-tuple-element.8), channel_id=1, source_target_pairs={{0,1},{1,2},{2,3},{3,0},{4,5},{5,6},{6,7},{7,4},{8,9},{9,10},{10,1... | collective-permute-start | bytes 2064392 | tf_op jit(solution)/shard_map/ppermute | solution.py:18
  74.7 0.8 %copy-start = (f32[336,512]{1,0:T(8,128)}, f32[336,512]{1,0:T(8,128)S(1)}, u32[]{:S(2)}) copy-start(f32[336,512]{1,0:T(8,128)S(1)} %collective-permute-done.6.rec_ref) | copy-start | bytes 2064388
